TPU v7x, 128 devices: a whole 4x4x4 slice. The times are simulated.
128 devices in a mesh: lat: 8 (over y, core), lon: 16 (over x, z).
Axes of the slice: x: 4, y: 4, z: 4, core: 2. Of those that a mesh axis runs over, the one named last changes fastest.
Arguments:
- grid_latent: bfloat16 [262144, 512], P(('lat', 'lon')), may hold values from -6 to 6
- mesh_latent: bfloat16 [10240, 512], P(('lat', 'lon')), may hold values from -6 to 6
- encoder_slots: int32 [2, 262144], P(None, ('lat', 'lon')), may hold values from 0 to 719, as said below
- decoder_slots: int32 [3, 262144], P(None, ('lat', 'lon')), may hold values from 0 to 719, as said below
- peer_rows: int32 [128, 128, 4], P(('lat', 'lon')), may hold values from 0 to 79, as said below
- edge_source: int32 [81920], P(('lat', 'lon')), may hold values from 0 to 511
- edge_target: int32 [81920], P(('lat', 'lon')), may hold values from 0 to 79
- encoder_sender: bfloat16 [512, 512], replicated, may hold values from -0.25 to 0.25
- encoder_receiver: bfloat16 [512, 512], replicated, may hold values from -0.25 to 0.25
- encoder_output: bfloat16 [512, 512], replicated, may hold values from -0.25 to 0.25
- encoder_merge: bfloat16 [512, 512], replicated, may hold values from -0.25 to 0.25
- encoder_self: bfloat16 [512, 512], replicated, may hold values from -0.25 to 0.25
- process_sender: bfloat16 [2, 512, 512], replicated, may hold values from -0.25 to 0.25
- process_receiver: bfloat16 [2, 512, 512], replicated, may hold values from -0.25 to 0.25
- process_output: bfloat16 [2, 512, 512], replicated, may hold values from -0.25 to 0.25
- process_merge: bfloat16 [2, 512, 512], replicated, may hold values from -0.25 to 0.25
- process_self: bfloat16 [2, 512, 512], replicated, may hold values from -0.25 to 0.25
- decoder_sender: bfloat16 [512, 512], replicated, may hold values from -0.25 to 0.25
- decoder_receiver: bfloat16 [512, 512], replicated, may hold values from -0.25 to 0.25
- decoder_output: bfloat16 [512, 512], replicated, may hold values from -0.25 to 0.25
Outputs:
- grid_update: bfloat16 [262144, 512], P(('lat', 'lon'))
Inputs may be any that keep to these rules, and one draw needn't show every extreme that they name: `encoder_slots`: every slot names a mesh node of the grid node's own tile or of one of its up to eight neighbouring tiles that exists in the window. `decoder_slots`: every slot names a mesh node of the grid node's own tile or of one of its up to eight neighbouring tiles that exists in the window. `peer_rows`: for each pair of tiles the 4 entries are distinct rows.
All inputs are finite; a program needn't handle non-finite values.
Results may differ from a plain program's by a relative error of at most 0.0085.
Values may be sent and summed in bfloat16 or wider, within the bound.
No kernel may reach another device: no remote copies, remote signals or barrier semaphores. Data moves between devices by JAX's collectives and lax.ppermute only.
A program may use at most 128 MiB of HBM per device.

v0:
```python
import jax
import jax.numpy as jnp
from jax import lax
from jax.sharding import PartitionSpec as P

CAP = 4
LAYERS = 2
DEC_FAN = 3


def padded_2(shard, sides, width):
    for axis, dim in sides:
        count, length = (lax.axis_size(axis), shard.shape[dim])
        up = [(i, (i + 1) % count) for i in range(count - 1)]
        down = [(j, i) for i, j in up]
        last = lax.slice_in_dim(shard, length - width, length, axis=dim)
        initial = lax.slice_in_dim(shard, 0, width, axis=dim)
        before = lax.ppermute(last, axis, up)
        after = lax.ppermute(initial, axis, down)
        shard = jnp.concatenate([before, shard, after], axis=dim)
    return shard


def layer_norm(values):
    centre = values - jnp.mean(values, axis=-1, keepdims=True)
    spread = jnp.mean(centre * centre, axis=-1, keepdims=True)
    return centre * lax.rsqrt(spread + 1e-05)


def product(left, right):
    return jnp.dot(left, right, preferred_element_type=jnp.float32)


def neighbours(mesh_rows):
    padded = padded_2(mesh_rows[None, None], (("lat", 0), ("lon", 1)), 1)
    return padded.reshape(9 * mesh_rows.shape[0], mesh_rows.shape[1])


def local(
    grid_latent,
    mesh_latent,
    encoder_slots,
    decoder_slots,
    peer_rows,
    edge_source,
    edge_target,
    encoder_sender,
    encoder_receiver,
    encoder_output,
    encoder_merge,
    encoder_self,
    process_sender,
    process_receiver,
    process_output,
    process_merge,
    process_self,
    decoder_sender,
    decoder_receiver,
    decoder_output,
):
    width = grid_latent.shape[1]
    owned = mesh_latent.shape[0]
    sender = product(grid_latent, encoder_sender)
    near_rows = product(neighbours(mesh_latent), encoder_receiver)
    hidden = jax.nn.silu(sender[None] + near_rows[encoder_slots]).astype(jnp.bfloat16)
    message = product(hidden.reshape(-1, width), encoder_output)
    partial_value = jax.ops.segment_sum(
        message, encoder_slots.reshape(-1), num_segments=9 * owned
    ).astype(jnp.bfloat16)
    padded = padded_2(partial_value.reshape(3, 3, owned, width), (("lat", 0), ("lon", 1)), 1)
    encoder_sum = jnp.sum(padded[0::2, 0::2].astype(jnp.float32), axis=(0, 1))
    update = product(encoder_sum.astype(jnp.bfloat16), encoder_merge) + product(
        mesh_latent, encoder_self
    )
    mesh_state = (mesh_latent.astype(jnp.float32) + layer_norm(jax.nn.silu(update))).astype(
        jnp.bfloat16
    )
    wanted = peer_rows[0]
    tiles = wanted.shape[0]
    asked = lax.all_to_all(wanted, ("lat", "lon"), split_axis=0, concat_axis=0, tiled=True)
    for depth in range(LAYERS):
        sent = lax.optimization_barrier(
            product(mesh_state, process_sender[depth]).astype(jnp.bfloat16)
        )
        outgoing = sent[asked]
        incoming = lax.all_to_all(outgoing, ("lat", "lon"), split_axis=0, concat_axis=0, tiled=True)
        fetched = incoming.reshape(tiles * CAP, width)[edge_source]
        received = product(mesh_state, process_receiver[depth])
        hidden = jax.nn.silu(fetched.astype(jnp.float32) + received[edge_target]).astype(
            jnp.bfloat16
        )
        message = product(hidden, process_output[depth])
        process_sum = jax.ops.segment_sum(message, edge_target, num_segments=owned)
        update = product(process_sum.astype(jnp.bfloat16), process_merge[depth]) + product(
            mesh_state, process_self[depth]
        )
        mesh_state = (mesh_state.astype(jnp.float32) + layer_norm(jax.nn.silu(update))).astype(
            jnp.bfloat16
        )
    decoded_near = product(neighbours(mesh_state), decoder_sender)
    receiver = product(grid_latent, decoder_receiver)
    hidden = jax.nn.silu(decoded_near[decoder_slots] + receiver[None]).astype(jnp.bfloat16)
    message = product(hidden.reshape(-1, width), decoder_output).reshape(DEC_FAN, -1, width)
    decoder_sum = jnp.sum(message, axis=0)
    return (grid_latent.astype(jnp.float32) + layer_norm(decoder_sum)).astype(jnp.bfloat16)


def solution(mesh):
    return jax.shard_map(
        local,
        mesh=mesh,
        in_specs=(
            P(("lat", "lon"), None),
            P(("lat", "lon"), None),
            P(None, ("lat", "lon")),
            P(None, ("lat", "lon")),
            P(("lat", "lon"), None, None),
            P(("lat", "lon")),
            P(("lat", "lon")),
            P(),
            P(),
            P(),
            P(),
            P(),
            P(),
            P(),
            P(),
            P(),
            P(),
            P(),
            P(),
            P(),
        ),
        out_specs=P(("lat", "lon"), None),
        check_vma=False,
    )
```

profile of v0, /device:TPU:3, one launch (start us, length us, event | category | flops | bytes accessed | tf_op | source)
XLA Modules:
  0.0 259.2 jit_solution(9718943759382392445)
XLA Ops:
  0.0 3.9 %collective-permute-start = (bf16[1,1,80,512]{3,2,1,0:T(8,128)(2,1)}, bf16[1,1,80,512]{3,2,1,0:T(8,128)(2,1)S(1)}, u32[]{:S(2)}, u32[]{:S(2)}) collective-permute-start(bf16[1,1,80,512]{3,2,1,0:T(8,128)(2,1)} %bitcast.101), channel_id=1, source_target_pairs={{0,16},{16,32},{32,48},{48,64},{64,80},{80,96},{96,112},{1,17},{17... | collective-permute-start | bytes 245768 | tf_op jit(solution)/shard_map/ppermute | solution.py:18
  5.8 4.9 %fusion.54 = f32[2048,512]{1,0:T(8,128)} fusion(bf16[2048,512]{1,0:T(8,128)(2,1)} %param.20, bf16[512,512]{1,0:T(8,128)(2,1)} %param.27), kind=kOutput, calls=%fused_computation.110 | convolution fusion | flops 1073741824 | bytes 6815744 | tf_op jit(solution)/shard_map/dot_general | solution.py:31
  10.8 3.7 %collective-permute-start.2 = (bf16[3,1,80,512]{3,2,1,0:T(8,128)(2,1)S(1)}, bf16[3,1,80,512]{3,2,1,0:T(8,128)(2,1)S(1)}, u32[]{:S(2)}, u32[]{:S(2)}) collective-permute-start(bf16[3,1,80,512]{3,2,1,0:T(8,128)(2,1)S(1)} %pad_maximum_fusion.6), channel_id=1, source_target_pairs={{0,1},{1,2},{2,3},{3,4},{4,5},{5,6},{6,7},{7,8},{8,9},{9,10},{10,1... | collective-permute-start | bytes 737288 | tf_op jit(solution)/shard_map/ppermute | solution.py:18
  14.5 4.0 %collective-permute-start.3 = (bf16[3,1,80,512]{3,2,1,0:T(8,128)(2,1)S(1)}, bf16[3,1,80,512]{3,2,1,0:T(8,128)(2,1)S(1)}, u32[]{:S(2)}, u32[]{:S(2)}) collective-permute-start(bf16[3,1,80,512]{3,2,1,0:T(8,128)(2,1)S(1)} %pad_maximum_fusion.6), channel_id=1, source_target_pairs={{1,0},{2,1},{3,2},{4,3},{5,4},{6,5},{7,6},{8,7},{9,8},{10,9},{11,1... | collective-permute-start | bytes 737288 | tf_op jit(solution)/shard_map/ppermute | solution.py:19
  23.5 16.8 %gather_fusion = f32[4096,512]{1,0:T(8,128)} fusion(f32[720,512]{1,0:T(8,128)S(1)} %fusion.55, s32[4096]{0:T(1024)S(1)} %broadcast_clamp_fusion.1), kind=kCustom, calls=%fused_computation | custom fusion | bytes 16793600 | tf_op jit(solution)/shard_map/gather | solution.py:65
  40.3 6.1 %broadcast_add_fusion = f32[2,2048,512]{2,1,0:T(8,128)S(1)} fusion(f32[2,2048,512]{2,1,0:T(8,128)} %bitcast.95, f32[2048,512]{1,0:T(8,128)} %fusion.54), kind=kLoop, calls=%fused_computation.21 | loop fusion | flops 2097152 | bytes 20971520 | tf_op jit(solution)/shard_map/add | solution.py:65
  49.2 5.6 %fusion.56 = f32[4096,512]{1,0:T(8,128)} fusion(bf16[4096,512]{1,0:T(8,128)(2,1)S(1)} %fusion.3, bf16[512,512]{1,0:T(8,128)(2,1)S(1)} %copy-done), kind=kOutput, calls=%fused_computation.112 | convolution fusion | flops 2147483648 | bytes 13107200 | tf_op jit(solution)/shard_map/dot_general | solution.py:31
  54.8 25.6 %scatter_custom_fusion = f32[720,512]{1,0:T(8,128)S(1)} fusion(s32[4096]{0:T(1024)S(1)} %bitcast.110, f32[4096,512]{1,0:T(8,128)} %fusion.56, f32[]{:T(128)} %constant.16.clone.1), kind=kCustom, calls=%fused_computation.33 | custom fusion | flops 2097152 | bytes 1475072 | tf_op jit(solution)/shard_map/scatter-add | solution.py:67
  80.5 5.2 %collective-permute-start.4 = (bf16[1,3,80,512]{3,2,1,0:T(8,128)(2,1)S(1)}, bf16[1,3,80,512]{3,2,1,0:T(8,128)(2,1)S(1)}, u32[]{:S(2)}, u32[]{:S(2)}) collective-permute-start(bf16[1,3,80,512]{3,2,1,0:T(8,128)(2,1)S(1)} %bitcast.107), channel_id=1, source_target_pairs={{0,16},{16,32},{32,48},{48,64},{64,80},{80,96},{96,112},{1,17},{17... | collective-permute-start | bytes 737288 | tf_op jit(solution)/shard_map/ppermute | solution.py:18
  88.4 10.7 %all-to-all-start = ((s32[128,1,4]{2,1,0:T(1,128)}), s32[128,1,4]{2,1,0:T(1,128)S(1)}, u32[]{:S(2)}, u32[]{:S(2)}) async-start(s32[128,1,4]{2,1,0:T(1,128)} %bitcast.8), calls=%async_computation | async-start | bytes 131072 | tf_op jit(solution)/shard_map/all_to_all | solution.py:80
  99.5 3.2 %collective-permute-start.6 = (bf16[5,1,80,512]{3,2,1,0:T(8,128)(2,1)S(1)}, bf16[5,1,80,512]{3,2,1,0:T(8,128)(2,1)S(1)}, u32[]{:S(2)}, u32[]{:S(2)}) collective-permute-start(bf16[5,1,80,512]{3,2,1,0:T(8,128)(2,1)S(1)} %get-tuple-element.7), channel_id=1, source_target_pairs={{0,1},{1,2},{2,3},{3,4},{4,5},{5,6},{6,7},{7,8},{8,9},{9,10},{10,1... | collective-permute-start | bytes 1228808 | tf_op jit(solution)/shard_map/ppermute | solution.py:18
  102.7 4.3 %collective-permute-start.7 = (bf16[5,1,80,512]{3,2,1,0:T(8,128)(2,1)S(1)}, bf16[5,1,80,512]{3,2,1,0:T(8,128)(2,1)S(1)}, u32[]{:S(2)}, u32[]{:S(2)}) collective-permute-start(bf16[5,1,80,512]{3,2,1,0:T(8,128)(2,1)S(1)} %get-tuple-element.8), channel_id=1, source_target_pairs={{1,0},{2,1},{3,2},{4,3},{5,4},{6,5},{7,6},{8,7},{9,8},{10,9},{11,1... | collective-permute-start | bytes 1228808 | tf_op jit(solution)/shard_map/ppermute | solution.py:19
  107.7 6.6 %collective-permute-done.6 = bf16[5,1,80,512]{3,2,1,0:T(8,128)(2,1)S(1)} collective-permute-done((bf16[5,1,80,512]{3,2,1,0:T(8,128)(2,1)S(1)}, bf16[5,1,80,512]{3,2,1,0:T(8,128)(2,1)S(1)}, u32[]{:S(2)}, u32[]{:S(2)}) %collective-permute-start.6) | collective-permute-done | bytes 409632 | tf_op jit(solution)/shard_map/ppermute | solution.py:18
  119.7 11.7 %all-to-all-start.1 = ((bf16[128,4,512]{2,1,0:T(4,128)(2,1)}), bf16[128,4,512]{2,1,0:T(4,128)(2,1)S(1)}, u32[]{:S(2)}, u32[]{:S(2)}) async-start(bf16[128,4,512]{2,1,0:T(4,128)(2,1)} %reshape.121), calls=%async_computation.1 | async-start | bytes 1048576 | tf_op jit(solution)/shard_map/all_to_all | solution.py:86
  133.8 9.7 %all-to-all-done.1 = bf16[128,4,512]{2,1,0:T(4,128)(2,1)S(1)} async-done(((bf16[128,4,512]{2,1,0:T(4,128)(2,1)}), bf16[128,4,512]{2,1,0:T(4,128)(2,1)S(1)}, u32[]{:S(2)}, u32[]{:S(2)}) %all-to-all-start.1) | async-done | bytes 524320 | tf_op jit(solution)/shard_map/all_to_all | solution.py:86
  149.1 7.4 %scatter_custom_fusion.1 = f32[80,512]{1,0:T(8,128)S(1)} fusion(s32[640]{0:T(1024)S(1)} %copy-done.14, f32[640,512]{1,0:T(8,128)} %fusion.7, f32[]{:T(128)} %constant.16.clone.1), kind=kCustom, calls=%fused_computation.83 | custom fusion | flops 327680 | bytes 164352 | tf_op jit(solution)/shard_map/scatter-add | solution.py:93
  162.6 5.9 %all-to-all-start.2 = ((bf16[128,4,512]{2,1,0:T(4,128)(2,1)}), bf16[128,4,512]{2,1,0:T(4,128)(2,1)S(1)}, u32[]{:S(2)}, u32[]{:S(2)}) async-start(bf16[128,4,512]{2,1,0:T(4,128)(2,1)} %reshape.145), calls=%async_computation.2 | async-start | bytes 1048576 | tf_op jit(solution)/shard_map/all_to_all | solution.py:86
  171.0 9.9 %all-to-all-done.2 = bf16[128,4,512]{2,1,0:T(4,128)(2,1)S(1)} async-done(((bf16[128,4,512]{2,1,0:T(4,128)(2,1)}), bf16[128,4,512]{2,1,0:T(4,128)(2,1)S(1)}, u32[]{:S(2)}, u32[]{:S(2)}) %all-to-all-start.2) | async-done | bytes 524320 | tf_op jit(solution)/shard_map/all_to_all | solution.py:86
  186.4 7.4 %scatter_custom_fusion.2 = f32[80,512]{1,0:T(8,128)S(1)} fusion(s32[640]{0:T(1024)S(1)} %copy-done.14, f32[640,512]{1,0:T(8,128)} %fusion.8, f32[]{:T(128)} %constant.16.clone.1), kind=kCustom, calls=%fused_computation.81 | custom fusion | flops 327680 | bytes 164352 | tf_op jit(solution)/shard_map/scatter-add | solution.py:93
  196.9 3.6 %collective-permute-start.8 = (bf16[1,1,80,512]{3,2,1,0:T(8,128)(2,1)S(1)}, bf16[1,1,80,512]{3,2,1,0:T(8,128)(2,1)S(1)}, u32[]{:S(2)}, u32[]{:S(2)}) collective-permute-start(bf16[1,1,80,512]{3,2,1,0:T(8,128)(2,1)S(1)} %fusion.38), channel_id=1, source_target_pairs={{0,16},{16,32},{32,48},{48,64},{64,80},{80,96},{96,112},{1,17},{17... | collective-permute-start | bytes 245768 | tf_op jit(solution)/shard_map/ppermute | solution.py:18
  202.4 3.8 %collective-permute-done.9 = bf16[1,1,80,512]{3,2,1,0:T(8,128)(2,1)S(1)} collective-permute-done((bf16[1,1,80,512]{3,2,1,0:T(8,128)(2,1)S(1)}, bf16[1,1,80,512]{3,2,1,0:T(8,128)(2,1)S(1)}, u32[]{:S(2)}, u32[]{:S(2)}) %collective-permute-start.9) | collective-permute-done | bytes 81952 | tf_op jit(solution)/shard_map/ppermute | solution.py:19
  209.4 5.2 %collective-permute-start.11 = (bf16[3,1,80,512]{3,2,1,0:T(8,128)(2,1)}, bf16[3,1,80,512]{3,2,1,0:T(8,128)(2,1)S(1)}, u32[]{:S(2)}, u32[]{:S(2)}) collective-permute-start(bf16[3,1,80,512]{3,2,1,0:T(8,128)(2,1)} %pad_maximum_fusion.7), channel_id=1, source_target_pairs={{1,0},{2,1},{3,2},{4,3},{5,4},{6,5},{7,6},{8,7},{9,8},{10,9},{11,1... | collective-permute-start | bytes 737288 | tf_op jit(solution)/shard_map/ppermute | solution.py:19
  220.9 24.6 %gather_fusion.7 = f32[6144,512]{1,0:T(8,128)} fusion(f32[720,512]{1,0:T(8,128)S(1)} %fusion.58, s32[6144]{0:T(1024)S(1)} %broadcast_clamp_fusion), kind=kCustom, calls=%fused_computation.7 | custom fusion | bytes 25190400 | tf_op jit(solution)/shard_map/gather | solution.py:102
  245.5 8.7 %fusion.49 = (f32[2048]{0:T(1024)S(1)}, f32[2048,512]{0,1:T(8,128)S(1)}) fusion(bf16[512,512]{1,0:T(8,128)(2,1)S(1)} %copy-done.19, f32[3,2048,512]{2,1,0:T(8,128)} %bitcast.96, f32[2048,512]{1,0:T(8,128)} %fusion.59), kind=kOutput, calls=%fused_computation.105 | convolution fusion | flops 3245340672 | bytes 21504000 | tf_op jit(solution)/shard_map/dot_general | solution.py:31
  (123 shorter events, 60.0 us)
Async XLA Ops:
  0.0 49.2 %copy-start = (bf16[512,512]{1,0:T(8,128)(2,1)S(1)}, bf16[512,512]{1,0:T(8,128)(2,1)}, u32[]{:S(2)}) copy-start(bf16[512,512]{1,0:T(8,128)(2,1)} %param.29) | copy-start | bytes 1572868
  0.0 18.5 %copy-start.11 = (s32[2,2048]{1,0:T(2,128)S(1)}, s32[2,2048]{1,0:T(2,128)}, u32[]{:S(2)}) copy-start(s32[2,2048]{1,0:T(2,128)} %param.22) | copy-start | bytes 49156
  0.0 10.7 %collective-permute-start = (bf16[1,1,80,512]{3,2,1,0:T(8,128)(2,1)}, bf16[1,1,80,512]{3,2,1,0:T(8,128)(2,1)S(1)}, u32[]{:S(2)}, u32[]{:S(2)}) collective-permute-start(bf16[1,1,80,512]{3,2,1,0:T(8,128)(2,1)} %bitcast.101), channel_id=1, source_target_pairs={{0,16},{16,32},{32,48},{48,64},{64,80},{80,96},{96,112},{1,17},{17... | collective-permute-start | bytes 245768 | tf_op jit(solution)/shard_map/ppermute | solution.py:18
  3.9 6.8 %collective-permute-start.1 = (bf16[1,1,80,512]{3,2,1,0:T(8,128)(2,1)}, bf16[1,1,80,512]{3,2,1,0:T(8,128)(2,1)S(1)}, u32[]{:S(2)}, u32[]{:S(2)}) collective-permute-start(bf16[1,1,80,512]{3,2,1,0:T(8,128)(2,1)} %bitcast.102), channel_id=1, source_target_pairs={{16,0},{32,16},{48,32},{64,48},{80,64},{96,80},{112,96},{17,1},{33... | collective-permute-start | bytes 245768 | tf_op jit(solution)/shard_map/ppermute | solution.py:19
  10.8 10.3 %collective-permute-start.2 = (bf16[3,1,80,512]{3,2,1,0:T(8,128)(2,1)S(1)}, bf16[3,1,80,512]{3,2,1,0:T(8,128)(2,1)S(1)}, u32[]{:S(2)}, u32[]{:S(2)}) collective-permute-start(bf16[3,1,80,512]{3,2,1,0:T(8,128)(2,1)S(1)} %pad_maximum_fusion.6), channel_id=1, source_target_pairs={{0,1},{1,2},{2,3},{3,4},{4,5},{5,6},{6,7},{7,8},{8,9},{9,10},{10,1... | collective-permute-start | bytes 737288 | tf_op jit(solution)/shard_map/ppermute | solution.py:18
  14.5 8.4 %collective-permute-start.3 = (bf16[3,1,80,512]{3,2,1,0:T(8,128)(2,1)S(1)}, bf16[3,1,80,512]{3,2,1,0:T(8,128)(2,1)S(1)}, u32[]{:S(2)}, u32[]{:S(2)}) collective-permute-start(bf16[3,1,80,512]{3,2,1,0:T(8,128)(2,1)S(1)} %pad_maximum_fusion.6), channel_id=1, source_target_pairs={{1,0},{2,1},{3,2},{4,3},{5,4},{6,5},{7,6},{8,7},{9,8},{10,9},{11,1... | collective-permute-start | bytes 737288 | tf_op jit(solution)/shard_map/ppermute | solution.py:19
  54.8 32.9 %copy-start.15 = (s32[1,128,4]{1,2,0:T(4,128)S(1)}, s32[1,128,4]{1,2,0:T(4,128)}, u32[]{:S(2)}) copy-start(s32[1,128,4]{1,2,0:T(4,128)} %param.24) | copy-start | bytes 6148
  54.8 44.3 %copy-start.8 = (bf16[512,512]{1,0:T(8,128)(2,1)S(1)}, bf16[512,512]{1,0:T(8,128)(2,1)}, u32[]{:S(2)}) copy-start(bf16[512,512]{1,0:T(8,128)(2,1)} %param.31) | copy-start | bytes 1572868
  80.5 26.6 %copy-start.13 = (s32[640]{0:T(1024)S(1)}, s32[640]{0:T(1024)}, u32[]{:S(2)}) copy-start(s32[640]{0:T(1024)} %param.25) | copy-start | bytes 7684
  80.5 18.8 %collective-permute-start.4 = (bf16[1,3,80,512]{3,2,1,0:T(8,128)(2,1)S(1)}, bf16[1,3,80,512]{3,2,1,0:T(8,128)(2,1)S(1)}, u32[]{:S(2)}, u32[]{:S(2)}) collective-permute-start(bf16[1,3,80,512]{3,2,1,0:T(8,128)(2,1)S(1)} %bitcast.107), channel_id=1, source_target_pairs={{0,16},{16,32},{32,48},{48,64},{64,80},{80,96},{96,112},{1,17},{17... | collective-permute-start | bytes 737288 | tf_op jit(solution)/shard_map/ppermute | solution.py:18
  85.7 13.6 %collective-permute-start.5 = (bf16[1,3,80,512]{3,2,1,0:T(8,128)(2,1)S(1)}, bf16[1,3,80,512]{3,2,1,0:T(8,128)(2,1)S(1)}, u32[]{:S(2)}, u32[]{:S(2)}) collective-permute-start(bf16[1,3,80,512]{3,2,1,0:T(8,128)(2,1)S(1)} %bitcast.106), channel_id=1, source_target_pairs={{16,0},{32,16},{48,32},{64,48},{80,64},{96,80},{112,96},{17,1},{33... | collective-permute-start | bytes 737288 | tf_op jit(solution)/shard_map/ppermute | solution.py:19
  88.4 19.1 %all-to-all-start = ((s32[128,1,4]{2,1,0:T(1,128)}), s32[128,1,4]{2,1,0:T(1,128)S(1)}, u32[]{:S(2)}, u32[]{:S(2)}) async-start(s32[128,1,4]{2,1,0:T(1,128)} %bitcast.8), calls=%async_computation | async-start | bytes 131072 | tf_op jit(solution)/shard_map/all_to_all | solution.py:80
  99.5 14.8 %collective-permute-start.6 = (bf16[5,1,80,512]{3,2,1,0:T(8,128)(2,1)S(1)}, bf16[5,1,80,512]{3,2,1,0:T(8,128)(2,1)S(1)}, u32[]{:S(2)}, u32[]{:S(2)}) collective-permute-start(bf16[5,1,80,512]{3,2,1,0:T(8,128)(2,1)S(1)} %get-tuple-element.7), channel_id=1, source_target_pairs={{0,1},{1,2},{2,3},{3,4},{4,5},{5,6},{6,7},{7,8},{8,9},{9,10},{10,1... | collective-permute-start | bytes 1228808 | tf_op jit(solution)/shard_map/ppermute | solution.py:18
  102.7 12.3 %collective-permute-start.7 = (bf16[5,1,80,512]{3,2,1,0:T(8,128)(2,1)S(1)}, bf16[5,1,80,512]{3,2,1,0:T(8,128)(2,1)S(1)}, u32[]{:S(2)}, u32[]{:S(2)}) collective-permute-start(bf16[5,1,80,512]{3,2,1,0:T(8,128)(2,1)S(1)} %get-tuple-element.8), channel_id=1, source_target_pairs={{1,0},{2,1},{3,2},{4,3},{5,4},{6,5},{7,6},{8,7},{9,8},{10,9},{11,1... | collective-permute-start | bytes 1228808 | tf_op jit(solution)/shard_map/ppermute | solution.py:19
  119.7 23.9 %all-to-all-start.1 = ((bf16[128,4,512]{2,1,0:T(4,128)(2,1)}), bf16[128,4,512]{2,1,0:T(4,128)(2,1)S(1)}, u32[]{:S(2)}, u32[]{:S(2)}) async-start(bf16[128,4,512]{2,1,0:T(4,128)(2,1)} %reshape.121), calls=%async_computation.1 | async-start | bytes 1048576 | tf_op jit(solution)/shard_map/all_to_all | solution.py:86
  162.6 18.2 %all-to-all-start.2 = ((bf16[128,4,512]{2,1,0:T(4,128)(2,1)}), bf16[128,4,512]{2,1,0:T(4,128)(2,1)S(1)}, u32[]{:S(2)}, u32[]{:S(2)}) async-start(bf16[128,4,512]{2,1,0:T(4,128)(2,1)} %reshape.145), calls=%async_computation.2 | async-start | bytes 1048576 | tf_op jit(solution)/shard_map/all_to_all | solution.py:86
  186.4 16.0 %copy-start.12 = (s32[3,2048]{1,0:T(4,128)S(1)}, s32[3,2048]{1,0:T(4,128)}, u32[]{:S(2)}) copy-start(s32[3,2048]{1,0:T(4,128)} %param.23) | copy-start | bytes 73732
  186.4 28.2 %copy-start.2 = (bf16[2048,512]{1,0:T(8,128)(2,1)S(1)}, bf16[2048,512]{1,0:T(8,128)(2,1)}, u32[]{:S(2)}) copy-start(bf16[2048,512]{1,0:T(8,128)(2,1)} %param.20) | copy-start | bytes 6291460
  186.4 28.2 %copy-start.7 = (bf16[512,512]{1,0:T(8,128)(2,1)S(1)}, bf16[512,512]{1,0:T(8,128)(2,1)}, u32[]{:S(2)}) copy-start(bf16[512,512]{1,0:T(8,128)(2,1)} %param.38) | copy-start | bytes 1572868
  196.9 5.6 %collective-permute-start.8 = (bf16[1,1,80,512]{3,2,1,0:T(8,128)(2,1)S(1)}, bf16[1,1,80,512]{3,2,1,0:T(8,128)(2,1)S(1)}, u32[]{:S(2)}, u32[]{:S(2)}) collective-permute-start(bf16[1,1,80,512]{3,2,1,0:T(8,128)(2,1)S(1)} %fusion.38), channel_id=1, source_target_pairs={{0,16},{16,32},{32,48},{48,64},{64,80},{80,96},{96,112},{1,17},{17... | collective-permute-start | bytes 245768 | tf_op jit(solution)/shard_map/ppermute | solution.py:18
  200.4 5.8 %collective-permute-start.9 = (bf16[1,1,80,512]{3,2,1,0:T(8,128)(2,1)S(1)}, bf16[1,1,80,512]{3,2,1,0:T(8,128)(2,1)S(1)}, u32[]{:S(2)}, u32[]{:S(2)}) collective-permute-start(bf16[1,1,80,512]{3,2,1,0:T(8,128)(2,1)S(1)} %fusion.38), channel_id=1, source_target_pairs={{16,0},{32,16},{48,32},{64,48},{80,64},{96,80},{112,96},{17,1},{33... | collective-permute-start | bytes 245768 | tf_op jit(solution)/shard_map/ppermute | solution.py:19
  206.9 13.3 %collective-permute-start.10 = (bf16[3,1,80,512]{3,2,1,0:T(8,128)(2,1)}, bf16[3,1,80,512]{3,2,1,0:T(8,128)(2,1)S(1)}, u32[]{:S(2)}, u32[]{:S(2)}) collective-permute-start(bf16[3,1,80,512]{3,2,1,0:T(8,128)(2,1)} %pad_maximum_fusion.7), channel_id=1, source_target_pairs={{0,1},{1,2},{2,3},{3,4},{4,5},{5,6},{6,7},{7,8},{8,9},{9,10},{10,1... | collective-permute-start | bytes 737288 | tf_op jit(solution)/shard_map/ppermute | solution.py:18
  209.4 10.8 %collective-permute-start.11 = (bf16[3,1,80,512]{3,2,1,0:T(8,128)(2,1)}, bf16[3,1,80,512]{3,2,1,0:T(8,128)(2,1)S(1)}, u32[]{:S(2)}, u32[]{:S(2)}) collective-permute-start(bf16[3,1,80,512]{3,2,1,0:T(8,128)(2,1)} %pad_maximum_fusion.7), channel_id=1, source_target_pairs={{1,0},{2,1},{3,2},{4,3},{5,4},{6,5},{7,6},{8,7},{9,8},{10,9},{11,1... | collective-permute-start | bytes 737288 | tf_op jit(solution)/shard_map/ppermute | solution.py:19
  220.9 24.7 %copy-start.19 = (bf16[512,512]{1,0:T(8,128)(2,1)S(1)}, bf16[512,512]{1,0:T(8,128)(2,1)}, u32[]{:S(2)}) copy-start(bf16[512,512]{1,0:T(8,128)(2,1)} %param.39) | copy-start | bytes 1572868
  (11 other events, 82.0 us)
where the time goes:
time: 260 us; the launch traced here: 259 us
  starting transfers between devices  69.6 us (27%)
  local copies, waits for them, and re-layouts  64.7 us (25%)
  other arithmetic  53.3 us (20%)
  waiting for transfers between devices  35.5 us (14%)
  matrix products  35.3 us (14%)
    dot_general x18, matrix products, product(): return jnp.dot(left, right, preferred_element_type=jnp.float32)  35.3 us
    scatter-add x1, other arithmetic, local(): jax.ops.segment_sum(message, encoder_slots.reshape(-1), num_segments=9 *...  25.6 us
    gather x1, local copies, waits for them, and re-layouts, local(): decoded_near[decoder_slots] + receiver[None]  24.6 us
    ppermute x6, starting transfers between devices, padded_2(): before = lax.ppermute(last, axis, up)  22.1 us
    all_to_all x2, waiting for transfers between devices, local(): lax.all_to_all(outgoing, ('lat', 'lon'), split_axis=0, concat_axis=0, til...  19.6 us
    ppermute x6, starting transfers between devices, padded_2(): after = lax.ppermute(initial, axis, down)  19.3 us
    all_to_all x2, starting transfers between devices, local(): lax.all_to_all(outgoing, ('lat', 'lon'), split_axis=0, concat_axis=0, til...  17.6 us
    gather x1, local copies, waits for them, and re-layouts, local(): near_rows[encoder_slots]  16.8 us
  transfers between devices with their start and end apart: 15, of which 8 were waited for; matrix products, arithmetic and copies ran while one was open for 6% of the time, Pallas kernels for 0%

commit v1 on v0

v1 whole, which is shorter than its diff:
```python
import functools

import jax
import jax.numpy as jnp
from jax import lax
from jax.experimental import pallas as pl
from jax.experimental.pallas import tpu as pltpu
from jax.sharding import PartitionSpec as P

CAP = 4
LAYERS = 2
ENC_FAN = 2
DEC_FAN = 3
SIDE = 3
ENC_ROWS = 512
DEC_ROWS = 512
PRE_ROWS = 512


def up128(n):
    return -(-n // 128) * 128


def dot(left, right):
    return jnp.dot(left, right, preferred_element_type=jnp.float32)


def silu(v):
    half = 0.5 * v
    return half + half * jnp.tanh(half)


def norm(v):
    centre = v - jnp.mean(v, axis=-1, keepdims=True)
    spread = jnp.mean(centre * centre, axis=-1, keepdims=True)
    return centre * lax.rsqrt(spread + 1e-05)


def hot_rows(column, width):
    lanes = lax.broadcasted_iota(jnp.int32, (column.shape[0], width), 1)
    return jnp.where(lanes == column, 1.0, 0.0).astype(jnp.bfloat16)


def hot_columns(row, height):
    subs = lax.broadcasted_iota(jnp.int32, (height, row.shape[1]), 0)
    return jnp.where(subs == row, 1.0, 0.0).astype(jnp.bfloat16)


def bf(v):
    return v.astype(jnp.bfloat16)


def pre_kernel(grid_ref, ws_ref, dr_ref, s_ref, r_ref):
    g = grid_ref[...]
    s_ref[...] = bf(dot(g, ws_ref[...]))
    r_ref[...] = bf(dot(g, dr_ref[...]))


def pre(grid_latent, ws, dr):
    n, d = grid_latent.shape
    tile = pl.BlockSpec((PRE_ROWS, d), lambda i: (i, 0))
    whole = pl.BlockSpec((d, d), lambda i: (0, 0))
    return pl.pallas_call(
        pre_kernel,
        grid=(n // PRE_ROWS,),
        in_specs=[tile, whole, whole],
        out_specs=[tile, tile],
        out_shape=[jax.ShapeDtypeStruct((n, d), jnp.bfloat16)] * 2,
        name="pre",
    )(grid_latent, ws, dr)


def enc_kernel(s_ref, row_ref, col_ref, n0, n1, n2, wr_ref, out_ref, near, acc, hid):
    step = pl.program_id(0)
    rows = s_ref.shape[0]
    third = n0.shape[0]
    height = near.shape[0]

    @pl.when(step == 0)
    def _():
        w = wr_ref[...]
        for k, ref in enumerate((n0, n1, n2)):
            near[k * third : (k + 1) * third] = bf(dot(ref[...], w))
        near[SIDE * third :] = jnp.zeros((height - SIDE * third, near.shape[1]), jnp.bfloat16)
        acc[...] = jnp.zeros_like(acc)

    s = s_ref[...].astype(jnp.float32)
    for f in range(ENC_FAN):
        v = dot(hot_rows(col_ref[:, f : f + 1], height), near[...]) + s
        hid[f * rows : (f + 1) * rows] = bf(silu(v))
    chosen = jnp.concatenate(
        [hot_columns(row_ref[f : f + 1, :], height) for f in range(ENC_FAN)], axis=1
    )
    acc[...] += dot(chosen, hid[...])

    @pl.when(step == pl.num_programs(0) - 1)
    def _():
        out_ref[...] = bf(acc[: out_ref.shape[0]])


def encode(s, slot_rows, slot_cols, near, wr):
    n, d = s.shape
    third = near[0].shape[0]
    height = up128(SIDE * third)
    whole = pl.BlockSpec((third, d), lambda i: (0, 0))
    return pl.pallas_call(
        enc_kernel,
        grid=(n // ENC_ROWS,),
        in_specs=[
            pl.BlockSpec((ENC_ROWS, d), lambda i: (i, 0)),
            pl.BlockSpec((ENC_FAN, ENC_ROWS), lambda i: (0, i)),
            pl.BlockSpec((ENC_ROWS, ENC_FAN), lambda i: (i, 0)),
            whole,
            whole,
            whole,
            pl.BlockSpec((d, d), lambda i: (0, 0)),
        ],
        out_specs=pl.BlockSpec((SIDE * third, d), lambda i: (0, 0)),
        out_shape=jax.ShapeDtypeStruct((SIDE * third, d), jnp.bfloat16),
        scratch_shapes=[
            pltpu.VMEM((height, d), jnp.bfloat16),
            pltpu.VMEM((height, d), jnp.float32),
            pltpu.VMEM((ENC_FAN * ENC_ROWS, d), jnp.bfloat16),
        ],
        name="encode",
    )(s, slot_rows, slot_cols, *near, wr)


def merge_kernel(
    own_ref, a_ref, b_ref, mesh_ref, asked_ref, wo, wm, wself, ws, state_ref, out_ref
):
    mesh = mesh_ref[...]
    total = own_ref[...] + a_ref[...].astype(jnp.float32) + b_ref[...].astype(jnp.float32)
    summed = bf(dot(bf(total), wo[...]))
    update = dot(summed, wm[...]) + dot(mesh, wself[...])
    state = bf(mesh.astype(jnp.float32) + norm(silu(update)))
    state_ref[...] = state
    sent = bf(dot(state, ws[...]))
    out_ref[...] = bf(dot(hot_rows(asked_ref[...], state.shape[0]), sent))


def merge(own, a, b, mesh, asked, wo, wm, wself, ws):
    rows, d = mesh.shape
    return pl.pallas_call(
        merge_kernel,
        out_shape=[
            jax.ShapeDtypeStruct((rows, d), jnp.bfloat16),
            jax.ShapeDtypeStruct((asked.shape[0], d), jnp.bfloat16),
        ],
        name="merge",
    )(own, a, b, mesh, asked, wo, wm, wself, ws)


def layer_kernel(
    last, in_ref, state_ref, src_ref, tgt_ref, tgt_row_ref, asked_ref, wr, wo, wm, wself, wn, *outs
):
    state = state_ref[...]
    owned = state.shape[0]
    received = bf(dot(state, wr[...]))
    v = dot(hot_rows(src_ref[...], in_ref.shape[0]), in_ref[...])
    v += dot(hot_rows(tgt_ref[...], owned), received)
    hidden = bf(silu(v))
    gathered = dot(hot_columns(tgt_row_ref[...], owned), hidden)
    summed = bf(dot(bf(gathered), wo[...]))
    update = dot(summed, wm[...]) + dot(state, wself[...])
    new = bf(state.astype(jnp.float32) + norm(silu(update)))
    sent = bf(dot(new, wn[...]))
    if last:
        outs[0][...] = sent
    else:
        outs[0][...] = new
        outs[1][...] = bf(dot(hot_rows(asked_ref[...], owned), sent))


def layer(last, incoming, state, src, tgt, tgt_row, asked, wr, wo, wm, wself, wn):
    rows, d = state.shape
    out = [jax.ShapeDtypeStruct((rows, d), jnp.bfloat16)]
    if not last:
        out.append(jax.ShapeDtypeStruct((asked.shape[0], d), jnp.bfloat16))
    return pl.pallas_call(
        functools.partial(layer_kernel, last),
        out_shape=out,
        name="layer_last" if last else "layer_first",
    )(incoming, state, src, tgt, tgt_row, asked, wr, wo, wm, wself, wn)


def dec_kernel(r_ref, grid_ref, col_ref, n0, n1, n2, wo, out_ref, near):
    third = n0.shape[0]
    height = near.shape[0]

    @pl.when(pl.program_id(0) == 0)
    def _():
        for k, ref in enumerate((n0, n1, n2)):
            near[k * third : (k + 1) * third] = ref[...]
        near[SIDE * third :] = jnp.zeros((height - SIDE * third, near.shape[1]), jnp.bfloat16)

    r = r_ref[...].astype(jnp.float32)
    total = None
    for f in range(DEC_FAN):
        v = dot(hot_rows(col_ref[:, f : f + 1], height), near[...]) + r
        h = bf(silu(v)).astype(jnp.float32)
        total = h if total is None else total + h
    high = bf(total)
    low = bf(total - high.astype(jnp.float32))
    w = wo[...]
    update = dot(high, w) + dot(low, w)
    out_ref[...] = bf(grid_ref[...].astype(jnp.float32) + norm(update))


def decode(r, grid_latent, slot_cols, near, wo):
    n, d = r.shape
    third = near[0].shape[0]
    height = up128(SIDE * third)
    whole = pl.BlockSpec((third, d), lambda i: (0, 0))
    tile = pl.BlockSpec((DEC_ROWS, d), lambda i: (i, 0))
    return pl.pallas_call(
        dec_kernel,
        grid=(n // DEC_ROWS,),
        in_specs=[
            tile,
            tile,
            pl.BlockSpec((DEC_ROWS, DEC_FAN), lambda i: (i, 0)),
            whole,
            whole,
            whole,
            pl.BlockSpec((d, d), lambda i: (0, 0)),
        ],
        out_specs=tile,
        out_shape=jax.ShapeDtypeStruct((n, d), jnp.bfloat16),
        scratch_shapes=[pltpu.VMEM((height, d), jnp.bfloat16)],
        name="decode",
    )(r, grid_latent, slot_cols, *near, wo)


def swaps(axis):
    count = lax.axis_size(axis)
    first = [(i, i ^ 1) for i in range(count)]
    second = []
    for i in range(1, count - 1, 2):
        second += [(i, i + 1), (i + 1, i)]
    return first, second


def swap_both(axis, to_first, to_second):
    first, second = swaps(axis)
    b = lax.ppermute(to_second, axis, second)
    a = lax.ppermute(to_first, axis, first)
    return a, b


def neighbours(rows):
    a, b = swap_both("lon", rows, rows)
    line = jnp.concatenate([rows, a, b], axis=0)
    c, d = swap_both("lat", line, line)
    return line, c, d


def to_owners(partial_sums):
    a, b = swap_both("lat", partial_sums[1], partial_sums[2])
    line = (
        partial_sums[0].astype(jnp.float32) + a.astype(jnp.float32) + b.astype(jnp.float32)
    )
    c, d = swap_both("lon", bf(line[1]), bf(line[2]))
    return line[0], c, d


def place(offset, axis):
    odd = lax.axis_index(axis) % 2
    return jnp.where(odd == 1, (4 - offset) % 3, (offset + 2) % 3)


def exchange_slots(slots, owned):
    block, row = slots // owned, slots % owned
    return (place(block // 3, "lat") * 3 + place(block % 3, "lon")) * owned + row


def local(
    grid_latent,
    mesh_latent,
    encoder_slots,
    decoder_slots,
    peer_rows,
    edge_source,
    edge_target,
    encoder_sender,
    encoder_receiver,
    encoder_output,
    encoder_merge,
    encoder_self,
    process_sender,
    process_receiver,
    process_output,
    process_merge,
    process_self,
    decoder_sender,
    decoder_receiver,
    decoder_output,
):
    owned, width = mesh_latent.shape
    wanted = peer_rows[0]
    tiles = wanted.shape[0]
    near = neighbours(mesh_latent)
    asked = lax.all_to_all(wanted, ("lat", "lon"), split_axis=0, concat_axis=0, tiled=True)
    asked = asked.reshape(tiles * CAP, 1)
    s, r = pre(grid_latent, encoder_sender, decoder_receiver)
    enc = exchange_slots(encoder_slots, owned)
    dec = exchange_slots(decoder_slots, owned)
    partial_sums = encode(s, enc, enc.T, near, encoder_receiver)
    own, a, b = to_owners(partial_sums.reshape(SIDE, SIDE, owned, width))
    state, outgoing = merge(
        own,
        a,
        b,
        mesh_latent,
        asked,
        encoder_output,
        encoder_merge,
        encoder_self,
        process_sender[0],
    )
    src = edge_source[:, None]
    tgt = edge_target[:, None]
    tgt_row = edge_target[None, :]
    for depth in range(LAYERS):
        last = depth == LAYERS - 1
        incoming = lax.all_to_all(
            outgoing.reshape(tiles, CAP, width),
            ("lat", "lon"),
            split_axis=0,
            concat_axis=0,
            tiled=True,
        ).reshape(tiles * CAP, width)
        result = layer(
            last,
            incoming,
            state,
            src,
            tgt,
            tgt_row,
            asked,
            process_receiver[depth],
            process_output[depth],
            process_merge[depth],
            process_self[depth],
            decoder_sender if last else process_sender[depth + 1],
        )
        if not last:
            state, outgoing = result
    return decode(r, grid_latent, dec.T, neighbours(result[0]), decoder_output)


def solution(mesh):
    return jax.shard_map(
        local,
        mesh=mesh,
        in_specs=(
            P(("lat", "lon"), None),
            P(("lat", "lon"), None),
            P(None, ("lat", "lon")),
            P(None, ("lat", "lon")),
            P(("lat", "lon"), None, None),
            P(("lat", "lon")),
            P(("lat", "lon")),
            P(),
            P(),
            P(),
            P(),
            P(),
            P(),
            P(),
            P(),
            P(),
            P(),
            P(),
            P(),
            P(),
        ),
        out_specs=P(("lat", "lon"), None),
        check_vma=False,
    )
```

time: 260 us -> 158 us (0.61)
  Pallas kernels: 0 us -> 44.5 us
  local copies, waits for them, and re-layouts: 64.7 us -> 22.9 us
  other arithmetic: 53.3 us -> 11.9 us
  matrix products: 35.3 us -> 0 us
  starting transfers between devices: 69.6 us -> 45.4 us
  waiting for transfers between devices: 35.5 us -> 13.9 us
  blocking collectives: 0 us -> 17.8 us
    gather x10 -> x0, local copies, waits for them, and re-layouts: 57.1 us -> none  [the longest x1 24.6 us: local(): decoded_near[decoder_slots] + receiver[None]]
    pallas_call x0 -> x6, Pallas kernels: none -> 44.5 us  [the longest x1 13.5 us: decode(): pl.pallas_call(dec_kernel, grid=(n // DEC_ROWS,), in_specs=[tile, tile, p...]
    scatter-add x3 -> x0, other arithmetic: 40.4 us -> none  [the longest x1 25.6 us: local(): jax.ops.segment_sum(message, encoder_slots.reshape(-1), num_segments=9 *...]
    dot_general x18 -> x0, matrix products: 35.3 us -> none  [product(): return jnp.dot(left, right, preferred_element_type=jnp.float32)]
    all_to_all x0 -> x1, blocking collectives: none -> 17.8 us  [local(): lax.all_to_all(outgoing.reshape(tiles, CAP, width), ('lat', 'lon'), split...]
    ppermute x12, starting transfers between devices: 41.3 us -> 27.9 us  [the longest x6 20.7 us: swap_both(): b = lax.ppermute(to_second, axis, second)]
    all_to_all x2 -> x1, waiting for transfers between devices: 19.6 us -> 8.5 us  [local(): lax.all_to_all(outgoing.reshape(tiles, CAP, width), ('lat', 'lon'), split...]
    ppermute x12, waiting for transfers between devices: 15.4 us -> 5.41 us  [the longest x6 5.4 us: swap_both(): b = lax.ppermute(to_second, axis, second)]
  transfers between devices with their start and end apart: 15 -> 14, of which waited for: 8 -> 4; matrix products, arithmetic and copies ran while one was open for 6% -> 18% of each run, Pallas kernels for 0% -> 11%
where the time goes in v1:
time: 158 us; the launch traced here: 157 us
  starting transfers between devices  45.4 us (29%)
  Pallas kernels  44.5 us (28%)
  local copies, waits for them, and re-layouts  22.9 us (14%)
  blocking collectives  17.8 us (11%)
  waiting for transfers between devices  13.9 us (9%)
  other arithmetic  11.9 us (8%)
    ppermute x6, starting transfers between devices, swap_both(): b = lax.ppermute(to_second, axis, second)  20.7 us
    all_to_all x1, blocking collectives, local(): lax.all_to_all(outgoing.reshape(tiles, CAP, width), ('lat', 'lon'), split...  17.8 us
    pallas_call x1, Pallas kernels, decode(): pl.pallas_call(dec_kernel, grid=(n // DEC_ROWS,), in_specs=[tile, tile, p...  13.5 us
    pallas_call x1, Pallas kernels, encode(): pl.pallas_call(enc_kernel, grid=(n // ENC_ROWS,), in_specs=[pl.BlockSpec(...  12 us
    pallas_call x2, Pallas kernels, layer(): pl.pallas_call(functools.partial(layer_kernel, last), out_shape=out, name...  9.66 us
    all_to_all x1, starting transfers between devices, local(): lax.all_to_all(outgoing.reshape(tiles, CAP, width), ('lat', 'lon'), split...  8.74 us
    all_to_all x1, starting transfers between devices, local(): lax.all_to_all(wanted, ('lat', 'lon'), split_axis=0, concat_axis=0, tiled...  8.71 us
    all_to_all x1, waiting for transfers between devices, local(): lax.all_to_all(outgoing.reshape(tiles, CAP, width), ('lat', 'lon'), split...  8.5 us
  transfers between devices with their start and end apart: 14, of which 4 were waited for; matrix products, arithmetic and copies ran while one was open for 18% of the time, Pallas kernels for 11%

profile of v1, /device:TPU:3, one launch (start us, length us, event | category | flops | bytes accessed | tf_op | source)
XLA Modules:
  0.0 156.8 jit_solution(6178594383248132027)
XLA Ops:
  0.0 1.6 %collective-permute-start = (bf16[80,512]{1,0:T(8,128)(2,1)}, bf16[80,512]{1,0:T(8,128)(2,1)S(1)}, u32[]{:S(2)}, u32[]{:S(2)}) collective-permute-start(bf16[80,512]{1,0:T(8,128)(2,1)} %mesh_ref.1), channel_id=1, source_target_pairs={{0,1},{1,0},{2,3},{3,2},{4,5},{5,4},{6,7},{7,6},{8,9},{9,8},{10,11... | collective-permute-start | bytes 245768 | tf_op jit(solution)/shard_map/ppermute | solution.py:247
  1.6 4.1 %collective-permute-start.1 = (bf16[80,512]{1,0:T(8,128)(2,1)}, bf16[80,512]{1,0:T(8,128)(2,1)S(1)}, u32[]{:S(2)}, u32[]{:S(2)}) collective-permute-start(bf16[80,512]{1,0:T(8,128)(2,1)} %mesh_ref.1), channel_id=1, source_target_pairs={{1,2},{2,1},{3,4},{4,3},{5,6},{6,5},{7,8},{8,7},{9,10},{10,9},{11,... | collective-permute-start | bytes 245768 | tf_op jit(solution)/shard_map/ppermute | solution.py:246
  7.2 8.7 %all-to-all-start = ((s32[128,1,4]{2,1,0:T(1,128)}), s32[128,1,4]{2,1,0:T(1,128)S(1)}, u32[]{:S(2)}, u32[]{:S(2)}) async-start(s32[128,1,4]{2,1,0:T(1,128)} %bitcast.8), calls=%async_computation | async-start | bytes 131072 | tf_op jit(solution)/shard_map/all_to_all | solution.py:303
  20.0 3.1 %collective-permute-start.3 = (bf16[240,512]{1,0:T(8,128)(2,1)S(1)}, bf16[240,512]{1,0:T(8,128)(2,1)}, u32[]{:S(2)}, u32[]{:S(2)}) collective-permute-start(bf16[240,512]{1,0:T(8,128)(2,1)S(1)} %constant_dynamic-update-slice_fusion.n0), channel_id=1, source_target_pairs={{16,32},{32,16},{48,64},{64,48},{80,96},{96,80},{17,33},{33,17},{4... | collective-permute-start | bytes 737288 | tf_op jit(solution)/shard_map/ppermute | solution.py:246
  23.1 5.3 %fusion.11 = s32[2,2048]{0,1:T(8,128)S(1)} fusion(s32[2,2048]{0,1:T(8,128)S(1)} %copy.87, s32[2,2048]{0,1:T(8,128)} %copy.88, s32[2,2048]{0,1:T(8,128)S(1)} %copy.83, pred[]{:T(512)S(6)} %eq.28, pred[]{:T(512)S(6)} %eq.27), kind=kLoop, calls=%fused_computation.25 | loop fusion | flops 229376 | bytes 65538 | tf_op jit(solution)/shard_map/add | solution.py:274
  29.3 5.6 %pre.1 = (bf16[2048,512]{1,0:T(8,128)(2,1)}, bf16[2048,512]{1,0:T(8,128)(2,1)}) custom-call(bf16[2048,512]{1,0:T(8,128)(2,1)} %grid_ref.3, bf16[512,512]{1,0:T(8,128)(2,1)} %ws_ref.1, bf16[512,512]{1,0:T(8,128)(2,1)} %dr_ref.1), custom_call_target="tpu_custom_call" | custom-call | tf_op jit(solution)/shard_map/pre/pallas_call | solution.py:63
  35.0 12.0 %encode.1 = bf16[720,512]{1,0:T(8,128)(2,1)} custom-call(bf16[2048,512]{1,0:T(8,128)(2,1)} %get-tuple-element.12.s_ref, s32[2,2048]{1,0:T(2,128)} %copy.89.row_ref, s32[2048,2]{1,0:T(8,128)} %bitcast.34, bf16[240,512]{1,0:T(8,128)(2,1)} %copy-done.7, bf16[240,512]{1,0:T(8,128)(2,1)} %collective-permute-done.2.n1, ...), custom_call_target="tpu_custom_call" | custom-call | tf_op jit(solution)/shard_map/encode/pallas_call | solution.py:106
  48.4 3.5 %collective-permute-start.5 = (bf16[3,80,512]{2,1,0:T(8,128)(2,1)S(1)}, bf16[3,80,512]{2,1,0:T(8,128)(2,1)S(1)}, u32[]{:S(2)}, u32[]{:S(2)}) collective-permute-start(bf16[3,80,512]{2,1,0:T(8,128)(2,1)S(1)} %bitcast.36), channel_id=1, source_target_pairs={{16,32},{32,16},{48,64},{64,48},{80,96},{96,80},{17,33},{33,17},{4... | collective-permute-start | bytes 737288 | tf_op jit(solution)/shard_map/ppermute | solution.py:246
  57.5 1.5 collective-permute-start.6
  59.1 4.0 %collective-permute-start.7 = (bf16[80,512]{1,0:T(8,128)(2,1)S(1)}, bf16[80,512]{1,0:T(8,128)(2,1)S(1)}, u32[]{:S(2)}, u32[]{:S(2)}) collective-permute-start(bf16[80,512]{1,0:T(8,128)(2,1)S(1)} %get-tuple-element.36), channel_id=1, source_target_pairs={{1,2},{2,1},{3,4},{4,3},{5,6},{6,5},{7,8},{8,7},{9,10},{10,9},{11,... | collective-permute-start | bytes 245768 | tf_op jit(solution)/shard_map/ppermute | solution.py:246
  63.7 2.6 %collective-permute-done.7.b_ref = bf16[80,512]{1,0:T(8,128)(2,1)S(1)} collective-permute-done((bf16[80,512]{1,0:T(8,128)(2,1)S(1)}, bf16[80,512]{1,0:T(8,128)(2,1)S(1)}, u32[]{:S(2)}, u32[]{:S(2)}) %collective-permute-start.7) | collective-permute-done | bytes 81952 | tf_op jit(solution)/shard_map/ppermute | solution.py:246
  67.0 3.7 %merge.1 = (bf16[80,512]{1,0:T(8,128)(2,1)}, bf16[512,512]{1,0:T(8,128)(2,1)}) custom-call(f32[80,512]{1,0:T(8,128)} %slice_bitcast_fusion.10.own_ref, bf16[80,512]{1,0:T(8,128)(2,1)} %copy-done.13, bf16[80,512]{1,0:T(8,128)(2,1)} %copy-done.14, bf16[80,512]{1,0:T(8,128)(2,1)} %mesh_ref.1, s32[512,1]{1,0:T(8,128)} %reshape.36.asked_ref, ...), custom_call_target="tpu_custom_call" | custom-call | tf_op jit(solution)/shard_map/merge/pallas_call | solution.py:144
  70.7 2.0 %reshape.31 = bf16[128,4,512]{2,1,0:T(4,128)(2,1)} reshape(bf16[512,512]{1,0:T(8,128)(2,1)} %get-tuple-element.13) | data formatting | bytes 1048576 | tf_op jit(solution)/shard_map/reshape | solution.py:327
  72.7 8.7 %all-to-all-start.1 = ((bf16[128,4,512]{2,1,0:T(4,128)(2,1)}), bf16[128,4,512]{2,1,0:T(4,128)(2,1)S(1)}, u32[]{:S(2)}, u32[]{:S(2)}) async-start(bf16[128,4,512]{2,1,0:T(4,128)(2,1)} %reshape.31), calls=%async_computation.1 | async-start | bytes 1048576 | tf_op jit(solution)/shard_map/all_to_all | solution.py:326
  85.1 8.5 %all-to-all-done.1 = bf16[128,4,512]{2,1,0:T(4,128)(2,1)S(1)} async-done(((bf16[128,4,512]{2,1,0:T(4,128)(2,1)}), bf16[128,4,512]{2,1,0:T(4,128)(2,1)S(1)}, u32[]{:S(2)}, u32[]{:S(2)}) %all-to-all-start.1) | async-done | bytes 524320 | tf_op jit(solution)/shard_map/all_to_all | solution.py:326
  94.5 5.0 %layer_first.1 = (bf16[80,512]{1,0:T(8,128)(2,1)}, bf16[512,512]{1,0:T(8,128)(2,1)}) custom-call(bf16[512,512]{1,0:T(8,128)(2,1)} %reshape.32.in_ref, bf16[80,512]{1,0:T(8,128)(2,1)} %get-tuple-element.14.state_ref, s32[640,1]{1,0:T(8,128)} %broadcast_in_dim.12.src_ref, s32[640,1]{1,0:T(8,128)} %broadcast_in_dim.13.tgt_ref, ...), custom_call_target="tpu_custom_call" | custom-call | tf_op jit(solution)/shard_map/layer_first/pallas_call | solution.py:180
  100.8 17.8 %all_to_all.19 = bf16[128,4,512]{2,1,0:T(4,128)(2,1)S(1)} all-to-all(bf16[128,4,512]{2,1,0:T(4,128)(2,1)S(1)} %reshape.33), channel_id=1, replica_groups=mesh['lat'=8,'lon'=16] {'lat','lon'}, dimensions={0} | all-to-all | bytes 1048576 | tf_op jit(solution)/shard_map/all_to_all | solution.py:326
  119.5 4.6 %layer_last.1 = bf16[80,512]{1,0:T(8,128)(2,1)} custom-call(bf16[512,512]{1,0:T(8,128)(2,1)} %reshape.34.in_ref, bf16[80,512]{1,0:T(8,128)(2,1)} %get-tuple-element.16.state_ref, s32[640,1]{1,0:T(8,128)} %broadcast_in_dim.12.src_ref, s32[640,1]{1,0:T(8,128)} %broadcast_in_dim.13.tgt_ref, s32[1,640]{1,0:T(1,128)} %broadcast_in_dim.11.tgt_row_ref, ...), custom_call_target="tpu_custom_call" | custom-call | tf_op jit(solution)/shard_map/layer_last/pallas_call | solution.py:180
  124.7 3.9 %collective-permute-start.9 = (bf16[80,512]{1,0:T(8,128)(2,1)}, bf16[80,512]{1,0:T(8,128)(2,1)S(1)}, u32[]{:S(2)}, u32[]{:S(2)}) collective-permute-start(bf16[80,512]{1,0:T(8,128)(2,1)} %layer_last.1), channel_id=1, source_target_pairs={{1,2},{2,1},{3,4},{4,3},{5,6},{6,5},{7,8},{8,7},{9,10},{10,9},{11,... | collective-permute-start | bytes 245768 | tf_op jit(solution)/shard_map/ppermute | solution.py:246
  129.8 2.4 %collective-permute-done.9 = bf16[80,512]{1,0:T(8,128)(2,1)S(1)} collective-permute-done((bf16[80,512]{1,0:T(8,128)(2,1)}, bf16[80,512]{1,0:T(8,128)(2,1)S(1)}, u32[]{:S(2)}, u32[]{:S(2)}) %collective-permute-start.9) | collective-permute-done | bytes 81952 | tf_op jit(solution)/shard_map/ppermute | solution.py:246
  132.2 2.9 %collective-permute-start.10 = (bf16[240,512]{1,0:T(8,128)(2,1)S(1)}, bf16[240,512]{1,0:T(8,128)(2,1)S(1)}, u32[]{:S(2)}, u32[]{:S(2)}) collective-permute-start(bf16[240,512]{1,0:T(8,128)(2,1)S(1)} %pad_maximum_fusion.n0), channel_id=1, source_target_pairs={{0,16},{16,0},{32,48},{48,32},{64,80},{80,64},{96,112},{112,96},{1... | collective-permute-start | bytes 737288 | tf_op jit(solution)/shard_map/ppermute | solution.py:247
  135.1 2.2 %collective-permute-start.11 = (bf16[240,512]{1,0:T(8,128)(2,1)S(1)}, bf16[240,512]{1,0:T(8,128)(2,1)S(1)}, u32[]{:S(2)}, u32[]{:S(2)}) collective-permute-start(bf16[240,512]{1,0:T(8,128)(2,1)S(1)} %pad_maximum_fusion.n0), channel_id=1, source_target_pairs={{16,32},{32,16},{48,64},{64,48},{80,96},{96,80},{17,33},{33,17},{4... | collective-permute-start | bytes 737288 | tf_op jit(solution)/shard_map/ppermute | solution.py:246
  137.3 5.0 %fusion.5.col_ref = s32[2048,3]{1,0:T(8,128)} fusion(s32[3,2048]{0,1:T(8,128)S(1)} %copy.81, s32[3,2048]{0,1:T(8,128)S(1)} %copy.82, s32[3,2048]{0,1:T(8,128)S(1)} %copy.77, pred[]{:T(512)S(6)} %eq.28, pred[]{:T(512)S(6)} %eq.27), kind=kLoop, calls=%fused_computation.19 | loop fusion | flops 344064 | bytes 98306 | tf_op jit(solution)/shard_map/transpose | solution.py:349
  143.4 13.5 %decode.1 = bf16[2048,512]{1,0:T(8,128)(2,1)} custom-call(bf16[2048,512]{1,0:T(8,128)(2,1)} %get-tuple-element.11.r_ref, bf16[2048,512]{1,0:T(8,128)(2,1)} %grid_ref.3, s32[2048,3]{1,0:T(8,128)} %fusion.5.col_ref, bf16[240,512]{1,0:T(8,128)(2,1)} %copy-done.6, bf16[240,512]{1,0:T(8,128)(2,1)} %copy-done.10, bf16[240,512]{1,0:T(8,128)(2,1)} %copy-done.11, ...), custom_call_target="tpu_custom_call" | custom-call | tf_op jit(solution)/shard_map/decode/pallas_call | solution.py:216
  (78 shorter events, 24.1 us)
Async XLA Ops:
  0.0 19.5 %copy-start.8 = (bf16[80,512]{1,0:T(8,128)(2,1)S(1)}, bf16[80,512]{1,0:T(8,128)(2,1)}, u32[]{:S(2)}) copy-start(bf16[80,512]{1,0:T(8,128)(2,1)} %mesh_ref.1) | copy-start | bytes 245764
  0.0 19.5 %collective-permute-start = (bf16[80,512]{1,0:T(8,128)(2,1)}, bf16[80,512]{1,0:T(8,128)(2,1)S(1)}, u32[]{:S(2)}, u32[]{:S(2)}) collective-permute-start(bf16[80,512]{1,0:T(8,128)(2,1)} %mesh_ref.1), channel_id=1, source_target_pairs={{0,1},{1,0},{2,3},{3,2},{4,5},{5,4},{6,7},{7,6},{8,9},{9,8},{10,11... | collective-permute-start | bytes 245768 | tf_op jit(solution)/shard_map/ppermute | solution.py:247
  1.6 17.9 %collective-permute-start.1 = (bf16[80,512]{1,0:T(8,128)(2,1)}, bf16[80,512]{1,0:T(8,128)(2,1)S(1)}, u32[]{:S(2)}, u32[]{:S(2)}) collective-permute-start(bf16[80,512]{1,0:T(8,128)(2,1)} %mesh_ref.1), channel_id=1, source_target_pairs={{1,2},{2,1},{3,4},{4,3},{5,6},{6,5},{7,8},{8,7},{9,10},{10,9},{11,... | collective-permute-start | bytes 245768 | tf_op jit(solution)/shard_map/ppermute | solution.py:246
  7.2 48.1 %all-to-all-start = ((s32[128,1,4]{2,1,0:T(1,128)}), s32[128,1,4]{2,1,0:T(1,128)S(1)}, u32[]{:S(2)}, u32[]{:S(2)}) async-start(s32[128,1,4]{2,1,0:T(1,128)} %bitcast.8), calls=%async_computation | async-start | bytes 131072 | tf_op jit(solution)/shard_map/all_to_all | solution.py:303
  19.5 8.9 %copy-start.7 = (bf16[240,512]{1,0:T(8,128)(2,1)}, bf16[240,512]{1,0:T(8,128)(2,1)S(1)}, u32[]{:S(2)}) copy-start(bf16[240,512]{1,0:T(8,128)(2,1)S(1)} %constant_dynamic-update-slice_fusion.n0) | copy-start | bytes 737284
  19.5 15.4 %collective-permute-start.2 = (bf16[240,512]{1,0:T(8,128)(2,1)S(1)}, bf16[240,512]{1,0:T(8,128)(2,1)}, u32[]{:S(2)}, u32[]{:S(2)}) collective-permute-start(bf16[240,512]{1,0:T(8,128)(2,1)S(1)} %constant_dynamic-update-slice_fusion.n0), channel_id=1, source_target_pairs={{0,16},{16,0},{32,48},{48,32},{64,80},{80,64},{96,112},{112,96},{1... | collective-permute-start | bytes 737288 | tf_op jit(solution)/shard_map/ppermute | solution.py:247
  20.0 14.9 %collective-permute-start.3 = (bf16[240,512]{1,0:T(8,128)(2,1)S(1)}, bf16[240,512]{1,0:T(8,128)(2,1)}, u32[]{:S(2)}, u32[]{:S(2)}) collective-permute-start(bf16[240,512]{1,0:T(8,128)(2,1)S(1)} %constant_dynamic-update-slice_fusion.n0), channel_id=1, source_target_pairs={{16,32},{32,16},{48,64},{64,48},{80,96},{96,80},{17,33},{33,17},{4... | collective-permute-start | bytes 737288 | tf_op jit(solution)/shard_map/ppermute | solution.py:246
  28.4 6.6 %copy-start = (s32[2,2048]{0,1:T(8,128)}, s32[2,2048]{0,1:T(8,128)S(1)}, u32[]{:S(2)}) copy-start(s32[2,2048]{0,1:T(8,128)S(1)} %fusion.11) | copy-start | bytes 49156
  35.0 16.9 %copy-start.1 = (bf16[2,512,512]{2,1,0:T(8,128)(2,1)S(1)}, bf16[2,512,512]{2,1,0:T(8,128)(2,1)}, u32[]{:S(2)}) copy-start(bf16[2,512,512]{2,1,0:T(8,128)(2,1)} %param.32) | copy-start | bytes 3145732
  47.0 7.4 %copy-start.16 = (s32[640]{0:T(1024)S(1)}, s32[640]{0:T(1024)}, u32[]{:S(2)}) copy-start(s32[640]{0:T(1024)} %param.25) | copy-start | bytes 7684
  48.3 9.1 %collective-permute-start.4 = (bf16[3,80,512]{2,1,0:T(8,128)(2,1)S(1)}, bf16[3,80,512]{2,1,0:T(8,128)(2,1)S(1)}, u32[]{:S(2)}, u32[]{:S(2)}) collective-permute-start(bf16[3,80,512]{2,1,0:T(8,128)(2,1)S(1)} %bitcast.37), channel_id=1, source_target_pairs={{0,16},{16,0},{32,48},{48,32},{64,80},{80,64},{96,112},{112,96},{1... | collective-permute-start | bytes 737288 | tf_op jit(solution)/shard_map/ppermute | solution.py:247
  48.4 9.0 %collective-permute-start.5 = (bf16[3,80,512]{2,1,0:T(8,128)(2,1)S(1)}, bf16[3,80,512]{2,1,0:T(8,128)(2,1)S(1)}, u32[]{:S(2)}, u32[]{:S(2)}) collective-permute-start(bf16[3,80,512]{2,1,0:T(8,128)(2,1)S(1)} %bitcast.36), channel_id=1, source_target_pairs={{16,32},{32,16},{48,64},{64,48},{80,96},{96,80},{17,33},{33,17},{4... | collective-permute-start | bytes 737288 | tf_op jit(solution)/shard_map/ppermute | solution.py:246
  57.5 6.2 %collective-permute-start.6 = (bf16[80,512]{1,0:T(8,128)(2,1)S(1)}, bf16[80,512]{1,0:T(8,128)(2,1)S(1)}, u32[]{:S(2)}, u32[]{:S(2)}) collective-permute-start(bf16[80,512]{1,0:T(8,128)(2,1)S(1)} %get-tuple-element.37), channel_id=1, source_target_pairs={{0,1},{1,0},{2,3},{3,2},{4,5},{5,4},{6,7},{7,6},{8,9},{9,8},{10,11... | collective-permute-start | bytes 245768 | tf_op jit(solution)/shard_map/ppermute | solution.py:247
  59.1 7.3 %collective-permute-start.7 = (bf16[80,512]{1,0:T(8,128)(2,1)S(1)}, bf16[80,512]{1,0:T(8,128)(2,1)S(1)}, u32[]{:S(2)}, u32[]{:S(2)}) collective-permute-start(bf16[80,512]{1,0:T(8,128)(2,1)S(1)} %get-tuple-element.36), channel_id=1, source_target_pairs={{1,2},{2,1},{3,4},{4,3},{5,6},{6,5},{7,8},{8,7},{9,10},{10,9},{11,... | collective-permute-start | bytes 245768 | tf_op jit(solution)/shard_map/ppermute | solution.py:246
  67.0 14.5 %copy-start.2 = (bf16[2,512,512]{2,1,0:T(8,128)(2,1)S(1)}, bf16[2,512,512]{2,1,0:T(8,128)(2,1)}, u32[]{:S(2)}) copy-start(bf16[2,512,512]{2,1,0:T(8,128)(2,1)} %param.36) | copy-start | bytes 3145732
  67.0 14.5 %copy-start.3 = (bf16[2,512,512]{2,1,0:T(8,128)(2,1)S(1)}, bf16[2,512,512]{2,1,0:T(8,128)(2,1)}, u32[]{:S(2)}) copy-start(bf16[2,512,512]{2,1,0:T(8,128)(2,1)} %param.35) | copy-start | bytes 3145732
  72.7 20.9 %all-to-all-start.1 = ((bf16[128,4,512]{2,1,0:T(4,128)(2,1)}), bf16[128,4,512]{2,1,0:T(4,128)(2,1)S(1)}, u32[]{:S(2)}, u32[]{:S(2)}) async-start(bf16[128,4,512]{2,1,0:T(4,128)(2,1)} %reshape.31), calls=%async_computation.1 | async-start | bytes 1048576 | tf_op jit(solution)/shard_map/all_to_all | solution.py:326
  119.5 9.2 %copy-start.12 = (s32[3,2048]{1,0:T(4,128)S(1)}, s32[3,2048]{1,0:T(4,128)}, u32[]{:S(2)}) copy-start(s32[3,2048]{1,0:T(4,128)} %param.23) | copy-start | bytes 73732
  124.1 8.1 %copy-start.9 = (bf16[80,512]{1,0:T(8,128)(2,1)S(1)}, bf16[80,512]{1,0:T(8,128)(2,1)}, u32[]{:S(2)}) copy-start(bf16[80,512]{1,0:T(8,128)(2,1)} %layer_last.1) | copy-start | bytes 245764
  124.1 5.7 %collective-permute-start.8 = (bf16[80,512]{1,0:T(8,128)(2,1)}, bf16[80,512]{1,0:T(8,128)(2,1)S(1)}, u32[]{:S(2)}, u32[]{:S(2)}) collective-permute-start(bf16[80,512]{1,0:T(8,128)(2,1)} %layer_last.1), channel_id=1, source_target_pairs={{0,1},{1,0},{2,3},{3,2},{4,5},{5,4},{6,7},{7,6},{8,9},{9,8},{10,11... | collective-permute-start | bytes 245768 | tf_op jit(solution)/shard_map/ppermute | solution.py:247
  124.7 7.5 %collective-permute-start.9 = (bf16[80,512]{1,0:T(8,128)(2,1)}, bf16[80,512]{1,0:T(8,128)(2,1)S(1)}, u32[]{:S(2)}, u32[]{:S(2)}) collective-permute-start(bf16[80,512]{1,0:T(8,128)(2,1)} %layer_last.1), channel_id=1, source_target_pairs={{1,2},{2,1},{3,4},{4,3},{5,6},{6,5},{7,8},{8,7},{9,10},{10,9},{11,... | collective-permute-start | bytes 245768 | tf_op jit(solution)/shard_map/ppermute | solution.py:246
  132.2 10.1 %copy-start.6 = (bf16[240,512]{1,0:T(8,128)(2,1)}, bf16[240,512]{1,0:T(8,128)(2,1)S(1)}, u32[]{:S(2)}) copy-start(bf16[240,512]{1,0:T(8,128)(2,1)S(1)} %pad_maximum_fusion.n0) | copy-start | bytes 737284
  132.2 10.1 %collective-permute-start.10 = (bf16[240,512]{1,0:T(8,128)(2,1)S(1)}, bf16[240,512]{1,0:T(8,128)(2,1)S(1)}, u32[]{:S(2)}, u32[]{:S(2)}) collective-permute-start(bf16[240,512]{1,0:T(8,128)(2,1)S(1)} %pad_maximum_fusion.n0), channel_id=1, source_target_pairs={{0,16},{16,0},{32,48},{48,32},{64,80},{80,64},{96,112},{112,96},{1... | collective-permute-start | bytes 737288 | tf_op jit(solution)/shard_map/ppermute | solution.py:247
  135.1 7.5 %collective-permute-start.11 = (bf16[240,512]{1,0:T(8,128)(2,1)S(1)}, bf16[240,512]{1,0:T(8,128)(2,1)S(1)}, u32[]{:S(2)}, u32[]{:S(2)}) collective-permute-start(bf16[240,512]{1,0:T(8,128)(2,1)S(1)} %pad_maximum_fusion.n0), channel_id=1, source_target_pairs={{16,32},{32,16},{48,64},{64,48},{80,96},{96,80},{17,33},{33,17},{4... | collective-permute-start | bytes 737288 | tf_op jit(solution)/shard_map/ppermute | solution.py:246
  (7 other events, 15.1 us)

commit v2 on v1

v2 whole, which is shorter than its diff:
```python
import functools

import jax
import jax.numpy as jnp
from jax import lax
from jax.experimental import pallas as pl
from jax.experimental.pallas import tpu as pltpu
from jax.sharding import PartitionSpec as P

CAP = 4
LAYERS = 2
ENC_FAN = 2
DEC_FAN = 3
SIDE = 3
ENC_ROWS = 1024
DEC_ROWS = 512
PRE_ROWS = 1024


def up128(n):
    return -(-n // 128) * 128


def dot(left, right):
    return jnp.dot(left, right, preferred_element_type=jnp.float32)


def silu(v):
    half = 0.5 * v
    return half + half * jnp.tanh(half)


def norm(v):
    centre = v - jnp.mean(v, axis=-1, keepdims=True)
    spread = jnp.mean(centre * centre, axis=-1, keepdims=True)
    return centre * lax.rsqrt(spread + 1e-05)


def hot_rows(row, width):
    n = row.shape[1]
    columns = jnp.broadcast_to(row, (128, n)).T
    lanes = lax.broadcasted_iota(jnp.int32, (n, 128), 1)
    parts = [
        jnp.where(lanes + at == columns, 1.0, 0.0).astype(jnp.bfloat16)
        for at in range(0, width, 128)
    ]
    return jnp.concatenate(parts, axis=1) if len(parts) > 1 else parts[0]


def hot_columns(row, height):
    subs = lax.broadcasted_iota(jnp.int32, (height, row.shape[1]), 0)
    return jnp.where(subs == row, 1.0, 0.0).astype(jnp.bfloat16)


def bf(v):
    return v.astype(jnp.bfloat16)


def pre_kernel(grid_ref, ws_ref, dr_ref, s_ref, r_ref):
    g = grid_ref[...]
    s_ref[...] = bf(dot(g, ws_ref[...]))
    r_ref[...] = bf(dot(g, dr_ref[...]))


def pre(grid_latent, ws, dr):
    n, d = grid_latent.shape
    tile = pl.BlockSpec((PRE_ROWS, d), lambda i: (i, 0))
    whole = pl.BlockSpec((d, d), lambda i: (0, 0))
    return pl.pallas_call(
        pre_kernel,
        grid=(n // PRE_ROWS,),
        in_specs=[tile, whole, whole],
        out_specs=[tile, tile],
        out_shape=[jax.ShapeDtypeStruct((n, d), jnp.bfloat16)] * 2,
        name="pre",
    )(grid_latent, ws, dr)


def block_at(odd_ref, place):
    spots = []
    for axis, at in enumerate((place // SIDE, place % SIDE)):
        odd = odd_ref[axis]
        spots.append((1, 2 - 2 * odd, 2 * odd)[at])
    return spots[0] * SIDE + spots[1]


def enc_kernel(odd_ref, s_ref, slots_ref, n0, n1, n2, wr_ref, o0, o1, o2, near, acc, hid):
    step = pl.program_id(0)
    rows = s_ref.shape[0]
    owned = n0.shape[0] // SIDE
    height = near.shape[0]
    slots = SIDE * SIDE * owned

    def block(k, at):
        start = pl.multiple_of(block_at(odd_ref, k * SIDE + at) * owned, 16)
        return pl.ds(start, owned)

    @pl.when(step == 0)
    def _():
        w = wr_ref[...]
        for k, ref in enumerate((n0, n1, n2)):
            v = bf(dot(ref[...], w))
            for at in range(SIDE):
                near[block(k, at), :] = v[at * owned : (at + 1) * owned]
        near[slots:] = jnp.zeros((height - slots, near.shape[1]), jnp.bfloat16)
        acc[...] = jnp.zeros_like(acc)

    s = s_ref[...].astype(jnp.float32)
    for f in range(ENC_FAN):
        v = dot(hot_rows(slots_ref[f : f + 1, :], height), near[...]) + s
        hid[f * rows : (f + 1) * rows] = bf(silu(v))
    chosen = jnp.concatenate(
        [hot_columns(slots_ref[f : f + 1, :], slots) for f in range(ENC_FAN)], axis=1
    )
    acc[...] += dot(chosen, hid[...])

    @pl.when(step == pl.num_programs(0) - 1)
    def _():
        for k, ref in enumerate((o0, o1, o2)):
            for at in range(SIDE):
                ref[at * owned : (at + 1) * owned] = bf(acc[block(k, at), :])


def encode(odd, s, slot_rows, near, wr):
    n, d = s.shape
    third = near[0].shape[0]
    height = up128(SIDE * third)
    whole = pl.BlockSpec((third, d), lambda i: (0, 0))
    return pl.pallas_call(
        enc_kernel,
        grid=(n // ENC_ROWS,),
        in_specs=[
            pl.BlockSpec(memory_space=pltpu.SMEM),
            pl.BlockSpec((ENC_ROWS, d), lambda i: (i, 0)),
            pl.BlockSpec((ENC_FAN, ENC_ROWS), lambda i: (0, i)),
            whole,
            whole,
            whole,
            pl.BlockSpec((d, d), lambda i: (0, 0)),
        ],
        out_specs=[whole] * SIDE,
        out_shape=[jax.ShapeDtypeStruct((third, d), jnp.bfloat16)] * SIDE,
        scratch_shapes=[
            pltpu.VMEM((height, d), jnp.bfloat16),
            pltpu.VMEM((SIDE * third, d), jnp.float32),
            pltpu.VMEM((ENC_FAN * ENC_ROWS, d), jnp.bfloat16),
        ],
        name="encode",
    )(odd, s, slot_rows, *near, wr)


def pack(rows, wide, out_ref):
    n, d = rows.shape
    parts = d // 128
    for c in range(parts):
        wide[pl.ds(c, n, stride=parts), :] = rows[:, c * 128 : (c + 1) * 128]
    out_ref[...] = bf(wide[...])


def unpack(in_ref, wide, d):
    parts = d // 128
    n = in_ref.shape[0] // parts
    wide[...] = in_ref[...].astype(jnp.float32)
    return jnp.concatenate(
        [bf(wide[pl.ds(c, n, stride=parts), :]) for c in range(parts)], axis=1
    )


def padded_rows(rows):
    extra = up128(rows.shape[0]) - rows.shape[0]
    return jnp.concatenate([rows, jnp.zeros((extra, rows.shape[1]), rows.dtype)], axis=0)


def merge_kernel(
    o_ref, a_ref, b_ref, mesh_ref, asked_ref, wo, wm, wself, ws, state_ref, out_ref, wide
):
    mesh = mesh_ref[...]
    total = o_ref[...] + a_ref[...].astype(jnp.float32) + b_ref[...].astype(jnp.float32)
    summed = bf(dot(bf(total), wo[...]))
    update = dot(summed, wm[...]) + dot(mesh, wself[...])
    state = bf(mesh.astype(jnp.float32) + norm(silu(update)))
    state_ref[...] = state
    sent = padded_rows(bf(dot(state, ws[0])))
    pack(dot(hot_rows(asked_ref[...], sent.shape[0]), sent), wide, out_ref)


def whole_spec(shape):
    return pl.BlockSpec(shape, lambda i: (0,) * len(shape))


def depth_spec(shape, depth):
    return pl.BlockSpec((1,) + shape[1:], lambda i: (depth,) + (0,) * (len(shape) - 1))


def merge(own, a, b, mesh, asked, wo, wm, wself, ws):
    rows, d = mesh.shape
    entries = asked.shape[1]
    args = (own, a, b, mesh, asked, wo, wm, wself)
    packed = (entries * d // 128, 128)
    return pl.pallas_call(
        merge_kernel,
        grid=(1,),
        in_specs=[whole_spec(x.shape) for x in args] + [depth_spec(ws.shape, 0)],
        out_specs=[whole_spec((rows, d)), whole_spec(packed)],
        out_shape=[
            jax.ShapeDtypeStruct((rows, d), jnp.bfloat16),
            jax.ShapeDtypeStruct(packed, jnp.bfloat16),
        ],
        scratch_shapes=[pltpu.VMEM(packed, jnp.float32)],
        name="merge",
    )(*args, ws)


def ready_kernel(state_ref, tgt_ref, wr, wself, base_ref, self_ref):
    state = state_ref[...]
    received = padded_rows(bf(dot(state, wr[0])))
    base_ref[...] = bf(dot(hot_rows(tgt_ref[...], received.shape[0]), received))
    self_ref[...] = dot(state, wself[0])


def ready(depth, state, tgt, wr, wself):
    rows, d = state.shape
    edges = tgt.shape[1]
    return pl.pallas_call(
        ready_kernel,
        grid=(1,),
        in_specs=[
            whole_spec(state.shape),
            whole_spec(tgt.shape),
            depth_spec(wr.shape, depth),
            depth_spec(wself.shape, depth),
        ],
        out_specs=[whole_spec((edges, d)), whole_spec((rows, d))],
        out_shape=[
            jax.ShapeDtypeStruct((edges, d), jnp.bfloat16),
            jax.ShapeDtypeStruct((rows, d), jnp.float32),
        ],
        name="ready",
    )(state, tgt, wr, wself)


def layer_kernel(
    last, in_ref, base_ref, self_ref, state_ref, src_ref, tgt_ref, asked_ref, wo, wm, wn, *rest
):
    outs, wide = rest[:-1], rest[-1]
    owned, d = state_ref.shape
    incoming = unpack(in_ref, wide, d)
    v = dot(hot_rows(src_ref[...], incoming.shape[0]), incoming)
    hidden = bf(silu(v + base_ref[...].astype(jnp.float32)))
    gathered = dot(hot_columns(tgt_ref[...], owned), hidden)
    summed = bf(dot(bf(gathered), wo[0]))
    update = dot(summed, wm[0]) + self_ref[...]
    new = bf(state_ref[...].astype(jnp.float32) + norm(silu(update)))
    if last:
        outs[0][...] = bf(dot(new, wn[...]))
    else:
        outs[0][...] = new
        sent = padded_rows(bf(dot(new, wn[0])))
        pack(dot(hot_rows(asked_ref[...], sent.shape[0]), sent), wide, outs[1])


def layer(depth, last, incoming, base, own, state, src, tgt, asked, wo, wm, wn):
    rows, d = state.shape
    args = (incoming, base, own, state, src, tgt, asked)
    out = [jax.ShapeDtypeStruct((rows, d), jnp.bfloat16)]
    if not last:
        out.append(jax.ShapeDtypeStruct(incoming.shape, jnp.bfloat16))
    return pl.pallas_call(
        functools.partial(layer_kernel, last),
        grid=(1,),
        in_specs=[whole_spec(x.shape) for x in args]
        + [
            depth_spec(wo.shape, depth),
            depth_spec(wm.shape, depth),
            whole_spec(wn.shape) if last else depth_spec(wn.shape, depth + 1),
        ],
        out_specs=[whole_spec(x.shape) for x in out],
        out_shape=out,
        scratch_shapes=[pltpu.VMEM(incoming.shape, jnp.float32)],
        name="layer_last" if last else "layer_first",
    )(*args, wo, wm, wn)


def dec_kernel(odd_ref, r_ref, grid_ref, slots_ref, n0, n1, n2, wo, out_ref, near):
    owned = n0.shape[0] // SIDE
    height = near.shape[0]
    slots = SIDE * SIDE * owned

    @pl.when(pl.program_id(0) == 0)
    def _():
        for k, ref in enumerate((n0, n1, n2)):
            for at in range(SIDE):
                start = pl.multiple_of(block_at(odd_ref, k * SIDE + at) * owned, 16)
                near[pl.ds(start, owned), :] = ref[at * owned : (at + 1) * owned]
        near[slots:] = jnp.zeros((height - slots, near.shape[1]), jnp.bfloat16)

    r = r_ref[...].astype(jnp.float32)
    total = None
    for f in range(DEC_FAN):
        v = dot(hot_rows(slots_ref[f : f + 1, :], height), near[...]) + r
        h = bf(silu(v)).astype(jnp.float32)
        total = h if total is None else total + h
    update = dot(bf(total), wo[...])
    out_ref[...] = bf(grid_ref[...].astype(jnp.float32) + norm(update))


def decode(odd, r, grid_latent, slot_rows, near, wo):
    n, d = r.shape
    third = near[0].shape[0]
    height = up128(SIDE * third)
    whole = pl.BlockSpec((third, d), lambda i: (0, 0))
    tile = pl.BlockSpec((DEC_ROWS, d), lambda i: (i, 0))
    return pl.pallas_call(
        dec_kernel,
        grid=(n // DEC_ROWS,),
        in_specs=[
            pl.BlockSpec(memory_space=pltpu.SMEM),
            tile,
            tile,
            pl.BlockSpec((DEC_FAN, DEC_ROWS), lambda i: (0, i)),
            whole,
            whole,
            whole,
            pl.BlockSpec((d, d), lambda i: (0, 0)),
        ],
        out_specs=tile,
        out_shape=jax.ShapeDtypeStruct((n, d), jnp.bfloat16),
        scratch_shapes=[pltpu.VMEM((height, d), jnp.bfloat16)],
        name="decode",
    )(odd, r, grid_latent, slot_rows, *near, wo)


def swaps(axis):
    count = lax.axis_size(axis)
    first = [(i, i ^ 1) for i in range(count)]
    second = []
    for i in range(1, count - 1, 2):
        second += [(i, i + 1), (i + 1, i)]
    return first, second


def swap_both(axis, to_first, to_second):
    first, second = swaps(axis)
    b = lax.ppermute(to_second, axis, second)
    a = lax.ppermute(to_first, axis, first)
    return a, b


def neighbours(rows):
    a, b = swap_both("lon", rows, rows)
    line = jnp.concatenate([rows, a, b], axis=0)
    c, d = swap_both("lat", line, line)
    return line, c, d


def to_owners(sums, owned):
    a, b = swap_both("lat", sums[1], sums[2])

    def line(at):
        part = slice(at * owned, (at + 1) * owned)
        return (
            sums[0][part].astype(jnp.float32)
            + a[part].astype(jnp.float32)
            + b[part].astype(jnp.float32)
        )

    c, d = swap_both("lon", bf(line(1)), bf(line(2)))
    return line(0), c, d


def local(
    grid_latent,
    mesh_latent,
    encoder_slots,
    decoder_slots,
    peer_rows,
    edge_source,
    edge_target,
    encoder_sender,
    encoder_receiver,
    encoder_output,
    encoder_merge,
    encoder_self,
    process_sender,
    process_receiver,
    process_output,
    process_merge,
    process_self,
    decoder_sender,
    decoder_receiver,
    decoder_output,
):
    owned, width = mesh_latent.shape
    wanted = peer_rows[0]
    tiles = wanted.shape[0]
    odd = jnp.stack([lax.axis_index("lat") % 2, lax.axis_index("lon") % 2]).astype(jnp.int32)
    near = neighbours(mesh_latent)
    asked = lax.all_to_all(wanted, ("lat", "lon"), split_axis=0, concat_axis=0, tiled=True)
    asked = asked.reshape(1, tiles * CAP)
    s, r = pre(grid_latent, encoder_sender, decoder_receiver)
    sums = encode(odd, s, encoder_slots, near, encoder_receiver)
    own, a, b = to_owners(sums, owned)
    state, outgoing = merge(
        own,
        a,
        b,
        mesh_latent,
        asked,
        encoder_output,
        encoder_merge,
        encoder_self,
        process_sender,
    )
    src = edge_source[None, :]
    tgt = edge_target[None, :]
    for depth in range(LAYERS):
        last = depth == LAYERS - 1
        incoming = lax.all_to_all(
            outgoing.reshape(tiles, -1, 128),
            ("lat", "lon"),
            split_axis=0,
            concat_axis=0,
            tiled=True,
        ).reshape(outgoing.shape)
        base, self_part = ready(depth, state, tgt, process_receiver, process_self)
        result = layer(
            depth,
            last,
            incoming,
            base,
            self_part,
            state,
            src,
            tgt,
            asked,
            process_output,
            process_merge,
            decoder_sender if last else process_sender,
        )
        if not last:
            state, outgoing = result
    return decode(odd, r, grid_latent, decoder_slots, neighbours(result[0]), decoder_output)


def solution(mesh):
    return jax.shard_map(
        local,
        mesh=mesh,
        in_specs=(
            P(("lat", "lon"), None),
            P(("lat", "lon"), None),
            P(None, ("lat", "lon")),
            P(None, ("lat", "lon")),
            P(("lat", "lon"), None, None),
            P(("lat", "lon")),
            P(("lat", "lon")),
            P(),
            P(),
            P(),
            P(),
            P(),
            P(),
            P(),
            P(),
            P(),
            P(),
            P(),
            P(),
            P(),
        ),
        out_specs=P(("lat", "lon"), None),
        check_vma=False,
    )
```

time: 158 us -> 146 us (0.924)
  waiting for transfers between devices: 13.9 us -> 34.4 us
  local copies, waits for them, and re-layouts: 22.9 us -> 7.14 us
  other arithmetic: 11.9 us -> 3.98 us
  starting transfers between devices: 45.4 us -> 38.1 us
  blocking collectives: 17.8 us -> 15.6 us
    ppermute x6, waiting for transfers between devices: 5.4 us -> 16.3 us  [swap_both(): b = lax.ppermute(to_second, axis, second)]
    all_to_all x2, waiting for transfers between devices: 8.5 us -> 18 us  [local(): lax.all_to_all(outgoing.reshape(tiles, -1, 128), ('lat', 'lon'), split_ax...]
    all_to_all x2, starting transfers between devices: 17.4 us -> 11.6 us  [local(): lax.all_to_all(outgoing.reshape(tiles, -1, 128), ('lat', 'lon'), split_ax...]
    add x1 -> x0, other arithmetic: 5.27 us -> none  [exchange_slots(): (place(block // 3, 'lat') * 3 + place(block % 3, 'lon')) * owned + row]
    reshape x5 -> x1, local copies, waits for them, and re-layouts: 5.79 us -> 0.7 us  [local(): asked = asked.reshape(1, tiles * CAP)]
    transpose x1 -> x0, other arithmetic: 5 us -> none  [local(): return decode(r, grid_latent, dec.T, neighbours(result[0]), decoder_output)]
    squeeze x4 -> x0, local copies, waits for them, and re-layouts: 4.45 us -> none  [the longest x1 1.4 us: local(): process_self[depth]]
    pallas_call x4 -> x6, Pallas kernels: 26.9 us -> 29.6 us  [the longest x1 12.2 us: decode(): pl.pallas_call(dec_kernel, grid=(n // DEC_ROWS,), in_specs=[pl.BlockSpec(...]
  transfers between devices with their start and end apart: 14 -> 14, of which waited for: 4 -> 7; matrix products, arithmetic and copies ran while one was open for 18% -> 3% of each run, Pallas kernels for 11% -> 7%
where the time goes in v2:
time: 146 us; the launch traced here: 145 us
  Pallas kernels  45.8 us (31%)
  starting transfers between devices  38.1 us (26%)
  waiting for transfers between devices  34.4 us (24%)
  blocking collectives  15.6 us (11%)
  local copies, waits for them, and re-layouts  7.14 us (5%)
  other arithmetic  3.98 us (3%)
    ppermute x6, starting transfers between devices, swap_both(): b = lax.ppermute(to_second, axis, second)  20 us
    all_to_all x2, waiting for transfers between devices, local(): lax.all_to_all(outgoing.reshape(tiles, -1, 128), ('lat', 'lon'), split_ax...  18 us
    ppermute x6, waiting for transfers between devices, swap_both(): b = lax.ppermute(to_second, axis, second)  16.3 us
    all_to_all x1, blocking collectives, local(): lax.all_to_all(wanted, ('lat', 'lon'), split_axis=0, concat_axis=0, tiled...  15.6 us
    pallas_call x1, Pallas kernels, decode(): pl.pallas_call(dec_kernel, grid=(n // DEC_ROWS,), in_specs=[pl.BlockSpec(...  12.2 us
    all_to_all x2, starting transfers between devices, local(): lax.all_to_all(outgoing.reshape(tiles, -1, 128), ('lat', 'lon'), split_ax...  11.6 us
    pallas_call x1, Pallas kernels, encode(): pl.pallas_call(enc_kernel, grid=(n // ENC_ROWS,), in_specs=[pl.BlockSpec(...  11.2 us
    pallas_call x2, Pallas kernels, layer(): pl.pallas_call(functools.partial(layer_kernel, last), grid=(1,), in_specs...  8.59 us
  transfers between devices with their start and end apart: 14, of which 7 were waited for; matrix products, arithmetic and copies ran while one was open for 3% of the time, Pallas kernels for 7%

profile of v2, /device:TPU:3, one launch (start us, length us, event | category | flops | bytes accessed | tf_op | source)
XLA Modules:
  0.0 145.3 jit_solution(5706367219010673773)
XLA Ops:
  1.6 4.1 %collective-permute-start.1 = (bf16[80,512]{1,0:T(8,128)(2,1)}, bf16[80,512]{1,0:T(8,128)(2,1)S(1)}, u32[]{:S(2)}, u32[]{:S(2)}) collective-permute-start(bf16[80,512]{1,0:T(8,128)(2,1)} %mesh_ref.1), channel_id=1, source_target_pairs={{1,2},{2,1},{3,4},{4,3},{5,6},{6,5},{7,8},{8,7},{9,10},{10,9},{11,... | collective-permute-start | bytes 245768 | tf_op jit(solution)/shard_map/ppermute | solution.py:344
  6.7 2.4 %collective-permute-done.1 = bf16[80,512]{1,0:T(8,128)(2,1)S(1)} collective-permute-done((bf16[80,512]{1,0:T(8,128)(2,1)}, bf16[80,512]{1,0:T(8,128)(2,1)S(1)}, u32[]{:S(2)}, u32[]{:S(2)}) %collective-permute-start.1) | collective-permute-done | bytes 81952 | tf_op jit(solution)/shard_map/ppermute | solution.py:344
  9.1 2.2 %collective-permute-start.2 = (bf16[240,512]{1,0:T(8,128)(2,1)S(1)}, bf16[240,512]{1,0:T(8,128)(2,1)S(1)}, u32[]{:S(2)}, u32[]{:S(2)}) collective-permute-start(bf16[240,512]{1,0:T(8,128)(2,1)S(1)} %constant_dynamic-update-slice_fusion.n0), channel_id=1, source_target_pairs={{0,16},{16,0},{32,48},{48,32},{64,80},{80,64},{96,112},{112,96},{1... | collective-permute-start | bytes 737288 | tf_op jit(solution)/shard_map/ppermute | solution.py:345
  11.3 3.1 %collective-permute-start.3 = (bf16[240,512]{1,0:T(8,128)(2,1)S(1)}, bf16[240,512]{1,0:T(8,128)(2,1)S(1)}, u32[]{:S(2)}, u32[]{:S(2)}) collective-permute-start(bf16[240,512]{1,0:T(8,128)(2,1)S(1)} %constant_dynamic-update-slice_fusion.n0), channel_id=1, source_target_pairs={{16,32},{32,16},{48,64},{64,48},{80,96},{96,80},{17,33},{33,17},{4... | collective-permute-start | bytes 737288 | tf_op jit(solution)/shard_map/ppermute | solution.py:344
  14.5 5.0 %pre.1 = (bf16[2048,512]{1,0:T(8,128)(2,1)}, bf16[2048,512]{1,0:T(8,128)(2,1)}) custom-call(bf16[2048,512]{1,0:T(8,128)(2,1)} %grid_ref.3, bf16[512,512]{1,0:T(8,128)(2,1)} %ws_ref.1, bf16[512,512]{1,0:T(8,128)(2,1)} %dr_ref.1), custom_call_target="tpu_custom_call" | custom-call | tf_op jit(solution)/shard_map/pre/pallas_call | solution.py:69
  20.9 11.2 %encode.1 = (bf16[240,512]{1,0:T(8,128)(2,1)}, bf16[240,512]{1,0:T(8,128)(2,1)}, bf16[240,512]{1,0:T(8,128)(2,1)}) custom-call(s32[2]{0:T(128)} %pad_add_fusion.odd_ref, bf16[2048,512]{1,0:T(8,128)(2,1)} %get-tuple-element.19.s_ref, s32[2,2048]{1,0:T(2,128)} %slots_ref.2, bf16[240,512]{1,0:T(8,128)(2,1)} %copy-done.3, bf16[240,512]{1,0:T(8,128)(2,1)} %copy-done.4, ...), custom_call_target="tpu_custom_call" | custom-call | tf_op jit(solution)/shard_map/encode/pallas_call | solution.py:129
  32.1 2.4 %collective-permute-start.5 = (bf16[240,512]{1,0:T(8,128)(2,1)}, bf16[240,512]{1,0:T(8,128)(2,1)S(1)}, u32[]{:S(2)}, u32[]{:S(2)}) collective-permute-start(bf16[240,512]{1,0:T(8,128)(2,1)} %get-tuple-element.22), channel_id=1, source_target_pairs={{16,32},{32,16},{48,64},{64,48},{80,96},{96,80},{17,33},{33,17},{4... | collective-permute-start | bytes 737288 | tf_op jit(solution)/shard_map/ppermute | solution.py:344
  34.6 5.2 %collective-permute-done.5 = bf16[240,512]{1,0:T(8,128)(2,1)S(1)} collective-permute-done((bf16[240,512]{1,0:T(8,128)(2,1)}, bf16[240,512]{1,0:T(8,128)(2,1)S(1)}, u32[]{:S(2)}, u32[]{:S(2)}) %collective-permute-start.5) | collective-permute-done | bytes 245792 | tf_op jit(solution)/shard_map/ppermute | solution.py:344
  41.5 4.1 %collective-permute-start.7 = (bf16[80,512]{1,0:T(8,128)(2,1)S(1)}, bf16[80,512]{1,0:T(8,128)(2,1)S(1)}, u32[]{:S(2)}, u32[]{:S(2)}) collective-permute-start(bf16[80,512]{1,0:T(8,128)(2,1)S(1)} %get-tuple-element.31), channel_id=1, source_target_pairs={{1,2},{2,1},{3,4},{4,3},{5,6},{6,5},{7,8},{8,7},{9,10},{10,9},{11,... | collective-permute-start | bytes 245768 | tf_op jit(solution)/shard_map/ppermute | solution.py:344
  45.8 15.6 %all_to_all.19 = s32[128,1,4]{2,1,0:T(1,128)S(1)} all-to-all(s32[128,1,4]{2,1,0:T(1,128)S(1)} %bitcast.11), channel_id=1, replica_groups=mesh['lat'=8,'lon'=16] {'lat','lon'}, dimensions={0} | all-to-all | bytes 4096 | tf_op jit(solution)/shard_map/all_to_all | solution.py:398
  64.0 3.6 %merge.1 = (bf16[80,512]{1,0:T(8,128)(2,1)}, bf16[2048,128]{1,0:T(8,128)(2,1)}) custom-call(f32[80,512]{1,0:T(8,128)} %get-tuple-element.33.o_ref, bf16[80,512]{1,0:T(8,128)(2,1)} %copy-done.8, bf16[80,512]{1,0:T(8,128)(2,1)} %copy-done.9, bf16[80,512]{1,0:T(8,128)(2,1)} %mesh_ref.1, s32[1,512]{1,0:T(1,128)} %reshape.19.asked_ref, bf16[512,512]{1,0:T(8,128)(2,1)} %wo.4, ...), custom_call_target="tpu_custom_call" | custom-call | tf_op jit(solution)/shard_map/merge/pallas_call | solution.py:200
  67.5 5.7 %all-to-all-start.1 = ((bf16[128,16,128]{2,1,0:T(8,128)(2,1)}), bf16[128,16,128]{2,1,0:T(8,128)(2,1)S(1)}, u32[]{:S(2)}, u32[]{:S(2)}) async-start(bf16[128,16,128]{2,1,0:T(8,128)(2,1)} %bitcast.9), calls=%async_computation.1 | async-start | bytes 1048576 | tf_op jit(solution)/shard_map/all_to_all | solution.py:418
  74.5 2.7 %ready.2 = (bf16[640,512]{1,0:T(8,128)(2,1)}, f32[80,512]{1,0:T(8,128)}) custom-call(bf16[80,512]{1,0:T(8,128)(2,1)} %get-tuple-element.24.state_ref, s32[1,640]{1,0:T(1,128)} %broadcast_in_dim.6.tgt_ref, bf16[2,512,512]{2,1,0:T(8,128)(2,1)} %wr.3, bf16[2,512,512]{2,1,0:T(8,128)(2,1)} %wself.5), custom_call_target="tpu_custom_call" | custom-call | tf_op jit(solution)/shard_map/ready/pallas_call | solution.py:224
  77.1 8.3 %all-to-all-done.1 = bf16[128,16,128]{2,1,0:T(8,128)(2,1)S(1)} async-done(((bf16[128,16,128]{2,1,0:T(8,128)(2,1)}), bf16[128,16,128]{2,1,0:T(8,128)(2,1)S(1)}, u32[]{:S(2)}, u32[]{:S(2)}) %all-to-all-start.1) | async-done | bytes 524320 | tf_op jit(solution)/shard_map/all_to_all | solution.py:418
  86.3 4.5 %layer_first.1 = (bf16[80,512]{1,0:T(8,128)(2,1)}, bf16[2048,128]{1,0:T(8,128)(2,1)}) custom-call(bf16[2048,128]{1,0:T(8,128)(2,1)} %bitcast.8, bf16[640,512]{1,0:T(8,128)(2,1)} %get-tuple-element.25.base_ref, f32[80,512]{1,0:T(8,128)} %get-tuple-element.26.self_ref, bf16[80,512]{1,0:T(8,128)(2,1)} %get-tuple-element.24.state_ref, ...), custom_call_target="tpu_custom_call" | custom-call | tf_op jit(solution)/shard_map/layer_first/pallas_call | solution.py:268
  90.8 5.9 %all-to-all-start.2 = ((bf16[128,16,128]{2,1,0:T(8,128)(2,1)}), bf16[128,16,128]{2,1,0:T(8,128)(2,1)S(1)}, u32[]{:S(2)}, u32[]{:S(2)}) async-start(bf16[128,16,128]{2,1,0:T(8,128)(2,1)} %bitcast.10), calls=%async_computation.2 | async-start | bytes 1048576 | tf_op jit(solution)/shard_map/all_to_all | solution.py:418
  96.7 2.6 %ready.3 = (bf16[640,512]{1,0:T(8,128)(2,1)}, f32[80,512]{1,0:T(8,128)}) custom-call(bf16[80,512]{1,0:T(8,128)(2,1)} %get-tuple-element.28.state_ref, s32[1,640]{1,0:T(1,128)} %broadcast_in_dim.6.tgt_ref, bf16[2,512,512]{2,1,0:T(8,128)(2,1)} %wr.3, bf16[2,512,512]{2,1,0:T(8,128)(2,1)} %wself.5), custom_call_target="tpu_custom_call" | custom-call | tf_op jit(solution)/shard_map/ready/pallas_call | solution.py:224
  99.4 9.6 %all-to-all-done.2 = bf16[128,16,128]{2,1,0:T(8,128)(2,1)S(1)} async-done(((bf16[128,16,128]{2,1,0:T(8,128)(2,1)}), bf16[128,16,128]{2,1,0:T(8,128)(2,1)S(1)}, u32[]{:S(2)}, u32[]{:S(2)}) %all-to-all-start.2) | async-done | bytes 524320 | tf_op jit(solution)/shard_map/all_to_all | solution.py:418
  109.8 4.0 %layer_last.1 = bf16[80,512]{1,0:T(8,128)(2,1)} custom-call(bf16[2048,128]{1,0:T(8,128)(2,1)} %bitcast.7, bf16[640,512]{1,0:T(8,128)(2,1)} %get-tuple-element.29.base_ref, f32[80,512]{1,0:T(8,128)} %get-tuple-element.30.self_ref, bf16[80,512]{1,0:T(8,128)(2,1)} %get-tuple-element.28.state_ref, s32[1,640]{1,0:T(1,128)} %broadcast_in_dim.7.src_ref, ...), custom_call_target="tpu_custom_call" | custom-call | tf_op jit(solution)/shard_map/layer_last/pallas_call | solution.py:268
  113.9 4.0 %collective-permute-start.9 = (bf16[80,512]{1,0:T(8,128)(2,1)}, bf16[80,512]{1,0:T(8,128)(2,1)S(1)}, u32[]{:S(2)}, u32[]{:S(2)}) collective-permute-start(bf16[80,512]{1,0:T(8,128)(2,1)} %layer_last.1), channel_id=1, source_target_pairs={{1,2},{2,1},{3,4},{4,3},{5,6},{6,5},{7,8},{8,7},{9,10},{10,9},{11,... | collective-permute-start | bytes 245768 | tf_op jit(solution)/shard_map/ppermute | solution.py:344
  118.0 3.3 %collective-permute-done.9 = bf16[80,512]{1,0:T(8,128)(2,1)S(1)} collective-permute-done((bf16[80,512]{1,0:T(8,128)(2,1)}, bf16[80,512]{1,0:T(8,128)(2,1)S(1)}, u32[]{:S(2)}, u32[]{:S(2)}) %collective-permute-start.9) | collective-permute-done | bytes 81952 | tf_op jit(solution)/shard_map/ppermute | solution.py:344
  122.4 2.5 %collective-permute-start.10 = (bf16[240,512]{1,0:T(8,128)(2,1)S(1)}, bf16[240,512]{1,0:T(8,128)(2,1)S(1)}, u32[]{:S(2)}, u32[]{:S(2)}) collective-permute-start(bf16[240,512]{1,0:T(8,128)(2,1)S(1)} %pad_maximum_fusion.n0), channel_id=1, source_target_pairs={{0,16},{16,0},{32,48},{48,32},{64,80},{80,64},{96,112},{112,96},{1... | collective-permute-start | bytes 737288 | tf_op jit(solution)/shard_map/ppermute | solution.py:345
  127.1 5.3 %collective-permute-done.11.n2 = bf16[240,512]{1,0:T(8,128)(2,1)S(1)} collective-permute-done((bf16[240,512]{1,0:T(8,128)(2,1)S(1)}, bf16[240,512]{1,0:T(8,128)(2,1)S(1)}, u32[]{:S(2)}, u32[]{:S(2)}) %collective-permute-start.11) | collective-permute-done | bytes 245792 | tf_op jit(solution)/shard_map/ppermute | solution.py:344
  133.1 12.2 %decode.1 = bf16[2048,512]{1,0:T(8,128)(2,1)} custom-call(s32[2]{0:T(128)} %pad_add_fusion.odd_ref, bf16[2048,512]{1,0:T(8,128)(2,1)} %get-tuple-element.18.r_ref, bf16[2048,512]{1,0:T(8,128)(2,1)} %grid_ref.3, s32[3,2048]{1,0:T(4,128)} %slots_ref.3, bf16[240,512]{1,0:T(8,128)(2,1)} %copy-done.2, bf16[240,512]{1,0:T(8,128)(2,1)} %copy-done.6, ...), custom_call_target="tpu_custom_call" | custom-call | tf_op jit(solution)/shard_map/decode/pallas_call | solution.py:313
  (51 shorter events, 15.2 us)
Async XLA Ops:
  0.0 6.7 %collective-permute-start = (bf16[80,512]{1,0:T(8,128)(2,1)}, bf16[80,512]{1,0:T(8,128)(2,1)S(1)}, u32[]{:S(2)}, u32[]{:S(2)}) collective-permute-start(bf16[80,512]{1,0:T(8,128)(2,1)} %mesh_ref.1), channel_id=1, source_target_pairs={{0,1},{1,0},{2,3},{3,2},{4,5},{5,4},{6,7},{7,6},{8,9},{9,8},{10,11... | collective-permute-start | bytes 245768 | tf_op jit(solution)/shard_map/ppermute | solution.py:345
  1.6 7.5 %collective-permute-start.1 = (bf16[80,512]{1,0:T(8,128)(2,1)}, bf16[80,512]{1,0:T(8,128)(2,1)S(1)}, u32[]{:S(2)}, u32[]{:S(2)}) collective-permute-start(bf16[80,512]{1,0:T(8,128)(2,1)} %mesh_ref.1), channel_id=1, source_target_pairs={{1,2},{2,1},{3,4},{4,3},{5,6},{6,5},{7,8},{8,7},{9,10},{10,9},{11,... | collective-permute-start | bytes 245768 | tf_op jit(solution)/shard_map/ppermute | solution.py:344
  9.1 11.0 %copy-start.3 = (bf16[240,512]{1,0:T(8,128)(2,1)}, bf16[240,512]{1,0:T(8,128)(2,1)S(1)}, u32[]{:S(2)}) copy-start(bf16[240,512]{1,0:T(8,128)(2,1)S(1)} %constant_dynamic-update-slice_fusion.n0) | copy-start | bytes 737284
  9.1 11.0 %collective-permute-start.2 = (bf16[240,512]{1,0:T(8,128)(2,1)S(1)}, bf16[240,512]{1,0:T(8,128)(2,1)S(1)}, u32[]{:S(2)}, u32[]{:S(2)}) collective-permute-start(bf16[240,512]{1,0:T(8,128)(2,1)S(1)} %constant_dynamic-update-slice_fusion.n0), channel_id=1, source_target_pairs={{0,16},{16,0},{32,48},{48,32},{64,80},{80,64},{96,112},{112,96},{1... | collective-permute-start | bytes 737288 | tf_op jit(solution)/shard_map/ppermute | solution.py:345
  11.3 8.8 %collective-permute-start.3 = (bf16[240,512]{1,0:T(8,128)(2,1)S(1)}, bf16[240,512]{1,0:T(8,128)(2,1)S(1)}, u32[]{:S(2)}, u32[]{:S(2)}) collective-permute-start(bf16[240,512]{1,0:T(8,128)(2,1)S(1)} %constant_dynamic-update-slice_fusion.n0), channel_id=1, source_target_pairs={{16,32},{32,16},{48,64},{64,48},{80,96},{96,80},{17,33},{33,17},{4... | collective-permute-start | bytes 737288 | tf_op jit(solution)/shard_map/ppermute | solution.py:344
  20.1 0.7 copy-start.4
  20.1 0.8 copy-start.5
  20.9 24.7 %copy-start.12 = (s32[1,128,4]{1,2,0:T(4,128)S(1)}, s32[1,128,4]{1,2,0:T(4,128)}, u32[]{:S(2)}) copy-start(s32[1,128,4]{1,2,0:T(4,128)} %param.24) | copy-start | bytes 6148
  32.1 7.7 %collective-permute-start.5 = (bf16[240,512]{1,0:T(8,128)(2,1)}, bf16[240,512]{1,0:T(8,128)(2,1)S(1)}, u32[]{:S(2)}, u32[]{:S(2)}) collective-permute-start(bf16[240,512]{1,0:T(8,128)(2,1)} %get-tuple-element.22), channel_id=1, source_target_pairs={{16,32},{32,16},{48,64},{64,48},{80,96},{96,80},{17,33},{33,17},{4... | collective-permute-start | bytes 737288 | tf_op jit(solution)/shard_map/ppermute | solution.py:344
  34.5 5.3 %collective-permute-start.4 = (bf16[240,512]{1,0:T(8,128)(2,1)}, bf16[240,512]{1,0:T(8,128)(2,1)S(1)}, u32[]{:S(2)}, u32[]{:S(2)}) collective-permute-start(bf16[240,512]{1,0:T(8,128)(2,1)} %get-tuple-element.21), channel_id=1, source_target_pairs={{0,16},{16,0},{32,48},{48,32},{64,80},{80,64},{96,112},{112,96},{1... | collective-permute-start | bytes 737288 | tf_op jit(solution)/shard_map/ppermute | solution.py:345
  41.5 21.8 %collective-permute-start.6 = (bf16[80,512]{1,0:T(8,128)(2,1)S(1)}, bf16[80,512]{1,0:T(8,128)(2,1)S(1)}, u32[]{:S(2)}, u32[]{:S(2)}) collective-permute-start(bf16[80,512]{1,0:T(8,128)(2,1)S(1)} %get-tuple-element.32), channel_id=1, source_target_pairs={{0,1},{1,0},{2,3},{3,2},{4,5},{5,4},{6,7},{7,6},{8,9},{9,8},{10,11... | collective-permute-start | bytes 245768 | tf_op jit(solution)/shard_map/ppermute | solution.py:345
  41.5 21.8 %collective-permute-start.7 = (bf16[80,512]{1,0:T(8,128)(2,1)S(1)}, bf16[80,512]{1,0:T(8,128)(2,1)S(1)}, u32[]{:S(2)}, u32[]{:S(2)}) collective-permute-start(bf16[80,512]{1,0:T(8,128)(2,1)S(1)} %get-tuple-element.31), channel_id=1, source_target_pairs={{1,2},{2,1},{3,4},{4,3},{5,6},{6,5},{7,8},{8,7},{9,10},{10,9},{11,... | collective-permute-start | bytes 245768 | tf_op jit(solution)/shard_map/ppermute | solution.py:344
  62.6 10.7 %copy-start.10 = (s32[640]{0:T(1024)S(1)}, s32[640]{0:T(1024)}, u32[]{:S(2)}) copy-start(s32[640]{0:T(1024)} %param.26) | copy-start | bytes 7684
  62.6 11.3 %copy-start.11 = (s32[640]{0:T(1024)S(1)}, s32[640]{0:T(1024)}, u32[]{:S(2)}) copy-start(s32[640]{0:T(1024)} %param.25) | copy-start | bytes 7684
  67.5 17.9 %all-to-all-start.1 = ((bf16[128,16,128]{2,1,0:T(8,128)(2,1)}), bf16[128,16,128]{2,1,0:T(8,128)(2,1)S(1)}, u32[]{:S(2)}, u32[]{:S(2)}) async-start(bf16[128,16,128]{2,1,0:T(8,128)(2,1)} %bitcast.9), calls=%async_computation.1 | async-start | bytes 1048576 | tf_op jit(solution)/shard_map/all_to_all | solution.py:418
  85.5 0.8 copy-start.1
  90.8 18.2 %all-to-all-start.2 = ((bf16[128,16,128]{2,1,0:T(8,128)(2,1)}), bf16[128,16,128]{2,1,0:T(8,128)(2,1)S(1)}, u32[]{:S(2)}, u32[]{:S(2)}) async-start(bf16[128,16,128]{2,1,0:T(8,128)(2,1)} %bitcast.10), calls=%async_computation.2 | async-start | bytes 1048576 | tf_op jit(solution)/shard_map/all_to_all | solution.py:418
  109.0 0.8 copy-start
  113.9 7.5 %collective-permute-start.9 = (bf16[80,512]{1,0:T(8,128)(2,1)}, bf16[80,512]{1,0:T(8,128)(2,1)S(1)}, u32[]{:S(2)}, u32[]{:S(2)}) collective-permute-start(bf16[80,512]{1,0:T(8,128)(2,1)} %layer_last.1), channel_id=1, source_target_pairs={{1,2},{2,1},{3,4},{4,3},{5,6},{6,5},{7,8},{8,7},{9,10},{10,9},{11,... | collective-permute-start | bytes 245768 | tf_op jit(solution)/shard_map/ppermute | solution.py:344
  117.9 3.6 %collective-permute-start.8 = (bf16[80,512]{1,0:T(8,128)(2,1)}, bf16[80,512]{1,0:T(8,128)(2,1)S(1)}, u32[]{:S(2)}, u32[]{:S(2)}) collective-permute-start(bf16[80,512]{1,0:T(8,128)(2,1)} %layer_last.1), channel_id=1, source_target_pairs={{0,1},{1,0},{2,3},{3,2},{4,5},{5,4},{6,7},{7,6},{8,9},{9,8},{10,11... | collective-permute-start | bytes 245768 | tf_op jit(solution)/shard_map/ppermute | solution.py:345
  122.4 10.0 %copy-start.2 = (bf16[240,512]{1,0:T(8,128)(2,1)}, bf16[240,512]{1,0:T(8,128)(2,1)S(1)}, u32[]{:S(2)}) copy-start(bf16[240,512]{1,0:T(8,128)(2,1)S(1)} %pad_maximum_fusion.n0) | copy-start | bytes 737284
  122.4 4.7 %collective-permute-start.10 = (bf16[240,512]{1,0:T(8,128)(2,1)S(1)}, bf16[240,512]{1,0:T(8,128)(2,1)S(1)}, u32[]{:S(2)}, u32[]{:S(2)}) collective-permute-start(bf16[240,512]{1,0:T(8,128)(2,1)S(1)} %pad_maximum_fusion.n0), channel_id=1, source_target_pairs={{0,16},{16,0},{32,48},{48,32},{64,80},{80,64},{96,112},{112,96},{1... | collective-permute-start | bytes 737288 | tf_op jit(solution)/shard_map/ppermute | solution.py:345
  124.9 7.5 %collective-permute-start.11 = (bf16[240,512]{1,0:T(8,128)(2,1)S(1)}, bf16[240,512]{1,0:T(8,128)(2,1)S(1)}, u32[]{:S(2)}, u32[]{:S(2)}) collective-permute-start(bf16[240,512]{1,0:T(8,128)(2,1)S(1)} %pad_maximum_fusion.n0), channel_id=1, source_target_pairs={{16,32},{32,16},{48,64},{64,48},{80,96},{96,80},{17,33},{33,17},{4... | collective-permute-start | bytes 737288 | tf_op jit(solution)/shard_map/ppermute | solution.py:344
  127.1 5.3 %copy-start.6 = (bf16[240,512]{1,0:T(8,128)(2,1)}, bf16[240,512]{1,0:T(8,128)(2,1)S(1)}, u32[]{:S(2)}) copy-start(bf16[240,512]{1,0:T(8,128)(2,1)S(1)} %collective-permute-done.10.n1) | copy-start | bytes 737284
  (3 other events, 2.0 us)

commit v3 on v2

v3 whole, which is shorter than its diff:
```python
import functools

import jax
import jax.numpy as jnp
from jax import lax
from jax.experimental import pallas as pl
from jax.experimental.pallas import tpu as pltpu
from jax.sharding import PartitionSpec as P


LAYERS = 2
ENC_FAN = 2
DEC_FAN = 3
SIDE = 3
ENC_ROWS = 1024
DEC_ROWS = 512
PRE_ROWS = 512


def up128(n):
    return -(-n // 128) * 128


def dot(left, right):
    return jnp.dot(left, right, preferred_element_type=jnp.float32)


def silu(v):
    half = 0.5 * v
    return half + half * jnp.tanh(half)


def norm(v):
    centre = v - jnp.mean(v, axis=-1, keepdims=True)
    spread = jnp.mean(centre * centre, axis=-1, keepdims=True)
    return centre * lax.rsqrt(spread + 1e-05)


def hot_rows(row, width):
    n = row.shape[1]
    columns = jnp.broadcast_to(row, (128, n)).T
    lanes = lax.broadcasted_iota(jnp.int32, (n, 128), 1)
    parts = [
        jnp.where(lanes + at == columns, 1.0, 0.0).astype(jnp.bfloat16)
        for at in range(0, width, 128)
    ]
    return jnp.concatenate(parts, axis=1) if len(parts) > 1 else parts[0]


def hot_columns(row, height):
    subs = lax.broadcasted_iota(jnp.int32, (height, row.shape[1]), 0)
    return jnp.where(subs == row, 1.0, 0.0).astype(jnp.bfloat16)


def bf(v):
    return v.astype(jnp.bfloat16)


VMEM = pl.BlockSpec(memory_space=pltpu.VMEM)
HBM = pl.BlockSpec(memory_space=pltpu.HBM)


def near_to(space, arrays):
    return [pltpu.with_memory_space_constraint(x, space) for x in arrays]


def on_chip(kernel, args, outs, far=(), scratch=(), odd=None, limit=16):
    args = near_to(pltpu.VMEM, args)
    specs = [VMEM] * len(args) + [HBM] * len(far)
    args += near_to(pltpu.HBM, far)
    if odd is not None:
        args = [odd] + args
        specs = [pl.BlockSpec(memory_space=pltpu.SMEM)] + specs
    return pl.pallas_call(
        kernel,
        in_specs=specs,
        out_specs=[VMEM] * len(outs),
        out_shape=[pltpu.VMEM(shape, dtype) for shape, dtype in outs],
        scratch_shapes=list(scratch),
        compiler_params=pltpu.CompilerParams(vmem_limit_bytes=limit << 20),
    )(*args)


def fetch(pairs, sems):
    copies = [pltpu.make_async_copy(x, y, sems.at[i]) for i, (x, y) in enumerate(pairs)]
    for copy in copies:
        copy.start()
    return copies


def pre_kernel(
    grid_ref, ws_ref, dr_ref, wr_ref, slots_ref, s_ref, wr_out, slots_out, r_ref, w, g, r, sems
):
    rows = PRE_ROWS
    count = grid_ref.shape[0] // rows
    parts = [slice(i * rows, (i + 1) * rows) for i in range(count)]
    pairs = [(ws_ref, w.at[0]), (dr_ref, w.at[1])]
    pairs += [(grid_ref.at[part], g.at[part]) for part in parts]
    pairs += [(wr_ref, wr_out), (slots_ref, slots_out)]
    copies = fetch(pairs, sems)
    copies[0].wait()
    copies[1].wait()
    backs = []
    for i, part in enumerate(parts):
        copies[2 + i].wait()
        x = g[part]
        s_ref[part] = bf(dot(x, w[0]))
        r[part] = bf(dot(x, w[1]))
        backs.append(
            pltpu.make_async_copy(r.at[part], r_ref.at[part], sems.at[len(pairs) + i])
        )
        backs[-1].start()
    for copy in copies[2 + count :] + backs:
        copy.wait()


def pre(grid_latent, ws, dr, wr, slots):
    n, d = grid_latent.shape
    args = near_to(pltpu.HBM, [grid_latent, ws, dr, wr, slots])
    return pl.pallas_call(
        pre_kernel,
        in_specs=[HBM] * len(args),
        out_specs=[VMEM] * 3 + [HBM],
        out_shape=[
            pltpu.VMEM((n, d), jnp.bfloat16),
            pltpu.VMEM((d, d), jnp.bfloat16),
            pltpu.VMEM(slots.shape, jnp.int32),
            pltpu.HBM((n, d), jnp.bfloat16),
        ],
        scratch_shapes=[
            pltpu.VMEM((2, d, d), jnp.bfloat16),
            pltpu.VMEM((n, d), jnp.bfloat16),
            pltpu.VMEM((n, d), jnp.bfloat16),
            pltpu.SemaphoreType.DMA((4 + 2 * (n // PRE_ROWS),)),
        ],
        compiler_params=pltpu.CompilerParams(vmem_limit_bytes=20 << 20),
        name="pre",
    )(*args)


def block_at(odd_ref, place):
    spots = []
    for axis, at in enumerate((place // SIDE, place % SIDE)):
        odd = odd_ref[axis]
        spots.append((1, 2 - 2 * odd, 2 * odd)[at])
    return spots[0] * SIDE + spots[1]


def enc_kernel(odd_ref, s_ref, slots_ref, n0, n1, n2, wr_ref, o0, o1, o2, near, acc, hid):
    rows = hid.shape[0] // ENC_FAN
    owned = n0.shape[0] // SIDE
    height = near.shape[0]
    slots = SIDE * SIDE * owned

    def block(k, at):
        start = pl.multiple_of(block_at(odd_ref, k * SIDE + at) * owned, 16)
        return pl.ds(start, owned)

    w = wr_ref[...]
    for k, ref in enumerate((n0, n1, n2)):
        v = bf(dot(ref[...], w))
        for at in range(SIDE):
            near[block(k, at), :] = v[at * owned : (at + 1) * owned]
    near[slots:] = jnp.zeros((height - slots, near.shape[1]), jnp.bfloat16)

    for step in range(s_ref.shape[0] // rows):
        part = slice(step * rows, (step + 1) * rows)
        s = s_ref[part].astype(jnp.float32)
        for f in range(ENC_FAN):
            v = dot(hot_rows(slots_ref[f : f + 1, part], height), near[...]) + s
            hid[f * rows : (f + 1) * rows] = bf(silu(v))
        chosen = jnp.concatenate(
            [hot_columns(slots_ref[f : f + 1, part], slots) for f in range(ENC_FAN)], axis=1
        )
        sums = dot(chosen, hid[...])
        acc[...] = sums if step == 0 else acc[...] + sums

    for k, ref in enumerate((o0, o1, o2)):
        for at in range(SIDE):
            ref[at * owned : (at + 1) * owned] = bf(acc[block(k, at), :])


def encode(odd, s, slot_rows, near, wr):
    _, d = s.shape
    third = near[0].shape[0]
    height = up128(SIDE * third)
    return on_chip(
        enc_kernel,
        [s, slot_rows, *near, wr],
        [((third, d), jnp.bfloat16)] * SIDE,
        scratch=[
            pltpu.VMEM((height, d), jnp.bfloat16),
            pltpu.VMEM((SIDE * third, d), jnp.float32),
            pltpu.VMEM((ENC_FAN * ENC_ROWS, d), jnp.bfloat16),
        ],
        odd=odd,
        limit=28,
    )


def pack(sent, asked_ref, wide, out_ref):
    sent = padded_rows(bf(sent))
    tiles, cap = asked_ref.shape
    parts = sent.shape[1] // 128
    lanes = lax.broadcasted_iota(jnp.int32, (tiles, sent.shape[0]), 1)
    for k in range(cap):
        chosen = bf(jnp.where(lanes == asked_ref[:, k : k + 1], 1.0, 0.0))
        rows = dot(chosen, sent)
        for c in range(parts):
            wide[pl.ds(k * parts + c, tiles, stride=cap * parts), :] = rows[
                :, c * 128 : (c + 1) * 128
            ]
    out_ref[...] = bf(wide[...])


def unpack(in_ref, wide, d):
    parts = d // 128
    n = in_ref.shape[0] // parts
    wide[...] = in_ref[...].astype(jnp.float32)
    return jnp.concatenate(
        [bf(wide[pl.ds(c, n, stride=parts), :]) for c in range(parts)], axis=1
    )


def padded_rows(rows):
    extra = up128(rows.shape[0]) - rows.shape[0]
    return jnp.concatenate([rows, jnp.zeros((extra, rows.shape[1]), rows.dtype)], axis=0)


def stage_kernel(mesh, wo, wm, wself, ws, wo_out, wm_out, ws_out, self_ref, w, sems):
    copies = fetch([(wself, w), (wo, wo_out), (wm, wm_out), (ws.at[0], ws_out)], sems)
    copies[0].wait()
    self_ref[...] = dot(mesh[...], w[...])
    for copy in copies[1:]:
        copy.wait()


def stage(mesh, wo, wm, wself, ws):
    rows, d = mesh.shape
    return on_chip(
        stage_kernel,
        [mesh],
        [((d, d), jnp.bfloat16)] * 3 + [((rows, d), jnp.float32)],
        far=[wo, wm, wself, ws],
        scratch=[pltpu.VMEM((d, d), jnp.bfloat16), pltpu.SemaphoreType.DMA((4,))],
    )


def merge_kernel(
    o_ref, a_ref, b_ref, mesh_ref, asked_ref, wo, wm, ws, self_ref, state_ref, out_ref, wide
):
    total = o_ref[...] + a_ref[...].astype(jnp.float32) + b_ref[...].astype(jnp.float32)
    summed = bf(dot(bf(total), wo[...]))
    update = dot(summed, wm[...]) + self_ref[...]
    state = bf(mesh_ref[...].astype(jnp.float32) + norm(silu(update)))
    state_ref[...] = state
    pack(dot(state, ws[...]), asked_ref, wide, out_ref)


def merge(own, a, b, mesh, asked, staged):
    packed = (asked.size * mesh.shape[1] // 128, 128)
    return on_chip(
        merge_kernel,
        [own, a, b, mesh, asked, *staged],
        [(mesh.shape, jnp.bfloat16), (packed, jnp.bfloat16)],
        scratch=[pltpu.VMEM(packed, jnp.float32)],
    )


def ready_kernel(depth, state_ref, tgt_ref, wr, wself, base_ref, self_ref, w, sems):
    copies = fetch([(wr.at[depth], w.at[0]), (wself.at[depth], w.at[1])], sems)
    state = state_ref[...]
    chosen = hot_rows(tgt_ref[...], up128(state.shape[0]))
    copies[0].wait()
    received = padded_rows(bf(dot(state, w[0])))
    base_ref[...] = bf(dot(chosen, received))
    copies[1].wait()
    self_ref[...] = dot(state, w[1])


def ready(depth, state, tgt, wr, wself):
    rows, d = state.shape
    return on_chip(
        functools.partial(ready_kernel, depth),
        [state, tgt],
        [((tgt.shape[1], d), jnp.bfloat16), ((rows, d), jnp.float32)],
        far=[wr, wself],
        scratch=[pltpu.VMEM((2, d, d), jnp.bfloat16), pltpu.SemaphoreType.DMA((2,))],
    )


def layer_kernel(
    depth, last, in_ref, base_ref, self_ref, state_ref, src_ref, tgt_ref, asked_ref, *rest
):
    wo, wm, wn = rest[:3]
    outs, (wide, w, sems) = rest[3:-3], rest[-3:]
    after = wn if last else wn.at[depth + 1]
    copies = fetch([(wo.at[depth], w.at[0]), (wm.at[depth], w.at[1]), (after, w.at[2])], sems)
    owned, d = state_ref.shape
    incoming = unpack(in_ref, wide, d)
    v = dot(hot_rows(src_ref[...], incoming.shape[0]), incoming)
    hidden = bf(silu(v + base_ref[...].astype(jnp.float32)))
    gathered = dot(hot_columns(tgt_ref[...], owned), hidden)
    copies[0].wait()
    summed = bf(dot(bf(gathered), w[0]))
    copies[1].wait()
    update = dot(summed, w[1]) + self_ref[...]
    new = bf(state_ref[...].astype(jnp.float32) + norm(silu(update)))
    copies[2].wait()
    if last:
        outs[0][...] = bf(dot(new, w[2]))
    else:
        outs[0][...] = new
        pack(dot(new, w[2]), asked_ref, wide, outs[1])


def layer(depth, last, incoming, base, own, state, src, tgt, asked, wo, wm, wn):
    out = [(state.shape, jnp.bfloat16)]
    if not last:
        out.append((incoming.shape, jnp.bfloat16))
    d = state.shape[1]
    return on_chip(
        functools.partial(layer_kernel, depth, last),
        [incoming, base, own, state, src, tgt, asked],
        out,
        far=[wo, wm, wn],
        scratch=[
            pltpu.VMEM(incoming.shape, jnp.float32),
            pltpu.VMEM((3, d, d), jnp.bfloat16),
            pltpu.SemaphoreType.DMA((3,)),
        ],
    )


def dec_kernel(
    odd_ref, n0, n1, n2, slots_ref, wo_ref, r_ref, grid_ref, out_ref, near, slots_in, w, r, g, sems
):
    owned = n0.shape[0] // SIDE
    height = near.shape[0]
    slots = SIDE * SIDE * owned
    rows = out_ref.shape[0]
    steps = r_ref.shape[0] // rows
    step = pl.program_id(0)
    small = [
        pltpu.make_async_copy(slots_ref, slots_in, sems.at[0]),
        pltpu.make_async_copy(wo_ref, w, sems.at[1]),
    ]

    def tile(i):
        part = pl.ds(pl.multiple_of(i * rows, rows), rows)
        return (
            pltpu.make_async_copy(r_ref.at[part], r.at[part], sems.at[2 + i]),
            pltpu.make_async_copy(grid_ref.at[part], g.at[part], sems.at[2 + steps + i]),
        )

    @pl.when(step == 0)
    def _():
        for copy in small:
            copy.start()
        for i in range(steps):
            for copy in tile(i):
                copy.start()
        for k, ref in enumerate((n0, n1, n2)):
            for at in range(SIDE):
                start = pl.multiple_of(block_at(odd_ref, k * SIDE + at) * owned, 16)
                near[pl.ds(start, owned), :] = ref[at * owned : (at + 1) * owned]
        near[slots:] = jnp.zeros((height - slots, near.shape[1]), jnp.bfloat16)
        for copy in small:
            copy.wait()

    for copy in tile(step):
        copy.wait()
    part = pl.ds(pl.multiple_of(step * rows, rows), rows)
    own = r[part, :].astype(jnp.float32)
    total = None
    for f in range(DEC_FAN):
        v = dot(hot_rows(slots_in[f : f + 1, part], height), near[...]) + own
        h = bf(silu(v)).astype(jnp.float32)
        total = h if total is None else total + h
    update = dot(bf(total), w[...])
    out_ref[...] = bf(g[part, :].astype(jnp.float32) + norm(update))


def decode(odd, r, grid_latent, slot_rows, near, wo):
    n, d = r.shape
    height = up128(SIDE * near[0].shape[0])
    args = near_to(pltpu.VMEM, near) + near_to(pltpu.HBM, [slot_rows, wo, r, grid_latent])
    return pl.pallas_call(
        dec_kernel,
        grid=(n // DEC_ROWS,),
        in_specs=[pl.BlockSpec(memory_space=pltpu.SMEM)] + [VMEM] * 3 + [HBM] * 4,
        out_specs=pl.BlockSpec((DEC_ROWS, d), lambda i: (i, 0)),
        out_shape=jax.ShapeDtypeStruct((n, d), jnp.bfloat16),
        scratch_shapes=[
            pltpu.VMEM((height, d), jnp.bfloat16),
            pltpu.VMEM(slot_rows.shape, jnp.int32),
            pltpu.VMEM((d, d), jnp.bfloat16),
            pltpu.VMEM((n, d), jnp.bfloat16),
            pltpu.VMEM((n, d), jnp.bfloat16),
            pltpu.SemaphoreType.DMA((2 + 2 * (n // DEC_ROWS),)),
        ],
        compiler_params=pltpu.CompilerParams(vmem_limit_bytes=28 << 20),
        name="decode",
    )(odd, *args)


def swaps(axis):
    count = lax.axis_size(axis)
    first = [(i, i ^ 1) for i in range(count)]
    second = []
    for i in range(1, count - 1, 2):
        second += [(i, i + 1), (i + 1, i)]
    return first, second


def swap_both(axis, to_first, to_second):
    first, second = swaps(axis)
    b = lax.ppermute(to_second, axis, second)
    a = lax.ppermute(to_first, axis, first)
    return a, b


def neighbours(rows):
    a, b = swap_both("lon", rows, rows)
    line = jnp.concatenate([rows, a, b], axis=0)
    c, d = swap_both("lat", line, line)
    return line, c, d


def to_owners(sums, owned):
    a, b = swap_both("lat", sums[1], sums[2])

    def line(at):
        part = slice(at * owned, (at + 1) * owned)
        return (
            sums[0][part].astype(jnp.float32)
            + a[part].astype(jnp.float32)
            + b[part].astype(jnp.float32)
        )

    own, first, second = line(0), bf(line(1)), bf(line(2))
    c, d = swap_both("lon", first, second)
    return own, c, d


def body(
    grid_latent,
    mesh_latent,
    encoder_slots,
    decoder_slots,
    peer_rows,
    edge_source,
    edge_target,
    encoder_sender,
    encoder_receiver,
    encoder_output,
    encoder_merge,
    encoder_self,
    process_sender,
    process_receiver,
    process_output,
    process_merge,
    process_self,
    decoder_sender,
    decoder_receiver,
    decoder_output,
):
    owned = mesh_latent.shape[0]
    wanted = peer_rows[0]
    tiles = wanted.shape[0]
    odd = jnp.stack([lax.axis_index("lat") % 2, lax.axis_index("lon") % 2]).astype(jnp.int32)
    near = neighbours(mesh_latent)
    asked = lax.all_to_all(wanted, ("lat", "lon"), split_axis=0, concat_axis=0, tiled=True)
    s, e_receiver, e_slots, r = pre(
        grid_latent, encoder_sender, decoder_receiver, encoder_receiver, encoder_slots
    )
    sums = encode(odd, s, e_slots, near, e_receiver)
    own, a, b = to_owners(sums, owned)
    staged = stage(mesh_latent, encoder_output, encoder_merge, encoder_self, process_sender)
    state, outgoing = merge(own, a, b, mesh_latent, asked, staged)
    src = edge_source[None, :]
    tgt = edge_target[None, :]
    for depth in range(LAYERS):
        last = depth == LAYERS - 1
        incoming = lax.all_to_all(
            outgoing.reshape(tiles, -1, 128),
            ("lat", "lon"),
            split_axis=0,
            concat_axis=0,
            tiled=True,
        ).reshape(outgoing.shape)
        base, self_part = ready(depth, state, tgt, process_receiver, process_self)
        result = layer(
            depth,
            last,
            incoming,
            base,
            self_part,
            state,
            src,
            tgt,
            asked,
            process_output,
            process_merge,
            decoder_sender if last else process_sender,
        )
        if not last:
            state, outgoing = result
    near = neighbours(result[0])
    return decode(odd, r, grid_latent, decoder_slots, near, decoder_output)


def solution(mesh):
    return jax.shard_map(
        body,
        mesh=mesh,
        in_specs=(
            P(("lat", "lon"), None),
            P(("lat", "lon"), None),
            P(None, ("lat", "lon")),
            P(None, ("lat", "lon")),
            P(("lat", "lon"), None, None),
            P(("lat", "lon")),
            P(("lat", "lon")),
            P(),
            P(),
            P(),
            P(),
            P(),
            P(),
            P(),
            P(),
            P(),
            P(),
            P(),
            P(),
            P(),
        ),
        out_specs=P(("lat", "lon"), None),
        check_vma=False,
    )
```

time: 146 us -> 134 us (0.918)
  blocking collectives: 15.6 us -> 0 us
  starting transfers between devices: 38.1 us -> 48.4 us
  waiting for transfers between devices: 34.4 us -> 42.7 us
  Pallas kernels: 45.8 us -> 40.2 us
  local copies, waits for them, and re-layouts: 7.14 us -> 1.69 us
  other arithmetic: 3.98 us -> 0.18 us
    all_to_all x1 -> x0, blocking collectives: 15.6 us -> none  [local(): lax.all_to_all(wanted, ('lat', 'lon'), split_axis=0, concat_axis=0, tiled...]
    all_to_all x2 -> x3, waiting for transfers between devices: 18 us -> 27.6 us  [the longest x2 20.9 us: body(): lax.all_to_all(outgoing.reshape(tiles, -1, 128), ('lat', 'lon'), split_ax...]
    all_to_all x2 -> x3, starting transfers between devices: 11.6 us -> 19.9 us  [the longest x2 11.8 us: body(): lax.all_to_all(outgoing.reshape(tiles, -1, 128), ('lat', 'lon'), split_ax...]
    pallas_call x7 -> x8, Pallas kernels: 33.6 us -> 27.9 us  [the longest x7 22.8 us: on_chip(): pl.pallas_call(kernel, in_specs=specs, out_specs=[VMEM] * len(outs), out_...]
    unnamed x29 -> x11, local copies, waits for them, and re-layouts: 4.75 us -> 1.68 us
    convert_element_type x1, other arithmetic: 1.72 us -> 0.09 us  [bf(): return v.astype(jnp.bfloat16)]
  transfers between devices with their start and end apart: 14 -> 15, of which waited for: 7 -> 7; matrix products, arithmetic and copies ran while one was open for 3% -> 1% of each run, Pallas kernels for 7% -> 8%
where the time goes in v3:
time: 134 us
  starting transfers between devices  48.4 us (36%)
  waiting for transfers between devices  42.7 us (32%)
  Pallas kernels  40.2 us (30%)
  local copies, waits for them, and re-layouts  1.69 us (1%)
    pallas_call x7, Pallas kernels, on_chip(): pl.pallas_call(kernel, in_specs=specs, out_specs=[VMEM] * len(outs), out_...  22.8 us
    ppermute x6, starting transfers between devices, swap_both(): b = lax.ppermute(to_second, axis, second)  21 us
    all_to_all x2, waiting for transfers between devices, body(): lax.all_to_all(outgoing.reshape(tiles, -1, 128), ('lat', 'lon'), split_ax...  20.9 us
    ppermute x6, waiting for transfers between devices, swap_both(): b = lax.ppermute(to_second, axis, second)  15.1 us
    pallas_call x1, Pallas kernels, decode(): pl.pallas_call(dec_kernel, grid=(n // DEC_ROWS,), in_specs=[pl.BlockSpec(...  12.2 us
    all_to_all x2, starting transfers between devices, body(): lax.all_to_all(outgoing.reshape(tiles, -1, 128), ('lat', 'lon'), split_ax...  11.8 us
    all_to_all x1, starting transfers between devices, body(): lax.all_to_all(wanted, ('lat', 'lon'), split_axis=0, concat_axis=0, tiled...  8.14 us
    ppermute x6, starting transfers between devices, swap_both(): a = lax.ppermute(to_first, axis, first)  7.53 us
  transfers between devices with their start and end apart: 15, of which 7 were waited for; matrix products, arithmetic and copies ran while one was open for 1% of the time, Pallas kernels for 8%

profile of v3, /device:TPU:3, one launch (start us, length us, event | category | flops | bytes accessed | tf_op | source)
XLA Modules:
  0.0 133.6 jit_solution(17899119450625023813)
XLA Ops:
  1.6 4.1 %collective-permute-start.1 = (bf16[80,512]{1,0:T(8,128)(2,1)}, bf16[80,512]{1,0:T(8,128)(2,1)S(1)}, u32[]{:S(2)}, u32[]{:S(2)}) collective-permute-start(bf16[80,512]{1,0:T(8,128)(2,1)} %mesh_ref.1), channel_id=1, source_target_pairs={{1,2},{2,1},{3,4},{4,3},{5,6},{6,5},{7,8},{8,7},{9,10},{10,9},{11,... | collective-permute-start | bytes 245768 | tf_op jit(solution)/shard_map/ppermute | solution.py:418
  6.7 2.4 %collective-permute-done.1 = bf16[80,512]{1,0:T(8,128)(2,1)S(1)} collective-permute-done((bf16[80,512]{1,0:T(8,128)(2,1)}, bf16[80,512]{1,0:T(8,128)(2,1)S(1)}, u32[]{:S(2)}, u32[]{:S(2)}) %collective-permute-start.1) | collective-permute-done | bytes 81952 | tf_op jit(solution)/shard_map/ppermute | solution.py:418
  9.1 2.1 %collective-permute-start.2 = (bf16[240,512]{1,0:T(8,128)(2,1)S(1)}, bf16[240,512]{1,0:T(8,128)(2,1)S(1)}, u32[]{:S(2)}, u32[]{:S(2)}) collective-permute-start(bf16[240,512]{1,0:T(8,128)(2,1)S(1)} %constant_dynamic-update-slice_fusion.n0), channel_id=1, source_target_pairs={{0,16},{16,0},{32,48},{48,32},{64,80},{80,64},{96,112},{112,96},{1... | collective-permute-start | bytes 737288 | tf_op jit(solution)/shard_map/ppermute | solution.py:419
  11.2 3.1 %collective-permute-start.3 = (bf16[240,512]{1,0:T(8,128)(2,1)S(1)}, bf16[240,512]{1,0:T(8,128)(2,1)S(1)}, u32[]{:S(2)}, u32[]{:S(2)}) collective-permute-start(bf16[240,512]{1,0:T(8,128)(2,1)S(1)} %constant_dynamic-update-slice_fusion.n0), channel_id=1, source_target_pairs={{16,32},{32,16},{48,64},{64,48},{80,96},{96,80},{17,33},{33,17},{4... | collective-permute-start | bytes 737288 | tf_op jit(solution)/shard_map/ppermute | solution.py:418
  14.4 5.1 %pre.1 = (bf16[2048,512]{1,0:T(8,128)(2,1)S(1)}, bf16[512,512]{1,0:T(8,128)(2,1)S(1)}, s32[2,2048]{1,0:T(2,128)S(1)}, bf16[2048,512]{1,0:T(8,128)(2,1)}) custom-call(bf16[2048,512]{1,0:T(8,128)(2,1)} %grid_ref.3, bf16[512,512]{1,0:T(8,128)(2,1)} %ws_ref.1, bf16[512,512]{1,0:T(8,128)(2,1)} %dr_ref.1, bf16[512,512]{1,0:T(8,128)(2,1)} %wr_ref.1, ...), custom_call_target="tpu_custom_call" | custom-call | tf_op jit(solution)/shard_map/pre/pallas_call | solution.py:120
  19.6 8.9 %shard_map.190 = (bf16[240,512]{1,0:T(8,128)(2,1)S(1)}, bf16[240,512]{1,0:T(8,128)(2,1)S(1)}, bf16[240,512]{1,0:T(8,128)(2,1)S(1)}) custom-call(s32[2]{0:T(128)S(1)} %pad_add_fusion.odd_ref, bf16[2048,512]{1,0:T(8,128)(2,1)S(1)} %get-tuple-element.24.s_ref, s32[2,2048]{1,0:T(2,128)S(1)} %get-tuple-element.25.slots_ref, ...), custom_call_target="tpu_custom_call" | custom-call | tf_op jit(solution)/shard_map/pallas_call | solution.py:74
  28.6 3.6 %collective-permute-start.5 = (bf16[240,512]{1,0:T(8,128)(2,1)S(1)}, bf16[240,512]{1,0:T(8,128)(2,1)S(1)}, u32[]{:S(2)}, u32[]{:S(2)}) collective-permute-start(bf16[240,512]{1,0:T(8,128)(2,1)S(1)} %get-tuple-element.29), channel_id=1, source_target_pairs={{16,32},{32,16},{48,64},{64,48},{80,96},{96,80},{17,33},{33,17},{4... | collective-permute-start | bytes 737288 | tf_op jit(solution)/shard_map/ppermute | solution.py:418
  32.2 3.9 %collective-permute-done.5 = bf16[240,512]{1,0:T(8,128)(2,1)S(1)} collective-permute-done((bf16[240,512]{1,0:T(8,128)(2,1)S(1)}, bf16[240,512]{1,0:T(8,128)(2,1)S(1)}, u32[]{:S(2)}, u32[]{:S(2)}) %collective-permute-start.5) | collective-permute-done | bytes 245792 | tf_op jit(solution)/shard_map/ppermute | solution.py:418
  36.3 4.1 %collective-permute-start.7 = (bf16[80,512]{1,0:T(8,128)(2,1)S(1)}, bf16[80,512]{1,0:T(8,128)(2,1)S(1)}, u32[]{:S(2)}, u32[]{:S(2)}) collective-permute-start(bf16[80,512]{1,0:T(8,128)(2,1)S(1)} %get-tuple-element.43), channel_id=1, source_target_pairs={{1,2},{2,1},{3,4},{4,3},{5,6},{6,5},{7,8},{8,7},{9,10},{10,9},{11,... | collective-permute-start | bytes 245768 | tf_op jit(solution)/shard_map/ppermute | solution.py:418
  41.2 8.1 %all-to-all-start = ((s32[128,1,4]{2,1,0:T(1,128)}), s32[128,1,4]{2,1,0:T(1,128)S(1)}, u32[]{:S(2)}, u32[]{:S(2)}) async-start(s32[128,1,4]{2,1,0:T(1,128)} %bitcast.2), calls=%async_computation | async-start | bytes 131072 | tf_op jit(solution)/shard_map/all_to_all | solution.py:473
  51.0 6.7 %all-to-all-done = s32[128,1,4]{2,1,0:T(1,128)S(1)} async-done(((s32[128,1,4]{2,1,0:T(1,128)}), s32[128,1,4]{2,1,0:T(1,128)S(1)}, u32[]{:S(2)}, u32[]{:S(2)}) %all-to-all-start) | async-done | bytes 2080 | tf_op jit(solution)/shard_map/all_to_all | solution.py:473
  57.6 2.0 %shard_map.192 = (bf16[80,512]{1,0:T(8,128)(2,1)S(1)}, bf16[2048,128]{1,0:T(8,128)(2,1)}) custom-call(f32[80,512]{1,0:T(8,128)S(1)} %get-tuple-element.45.o_ref, bf16[80,512]{1,0:T(8,128)(2,1)S(1)} %collective-permute-done.6.a_ref, bf16[80,512]{1,0:T(8,128)(2,1)S(1)} %collective-permute-done.7.b_ref, bf16[80,512]{1,0:T(8,128)(2,1)S(1)} %copy-done, ...), custom_call_target="tpu_custom_call" | custom-call | tf_op jit(solution)/shard_map/pallas_call | solution.py:74
  59.7 5.8 %all-to-all-start.1 = ((bf16[128,16,128]{2,1,0:T(8,128)(2,1)}), bf16[128,16,128]{2,1,0:T(8,128)(2,1)S(1)}, u32[]{:S(2)}, u32[]{:S(2)}) async-start(bf16[128,16,128]{2,1,0:T(8,128)(2,1)} %bitcast.4), calls=%async_computation.1 | async-start | bytes 1048576 | tf_op jit(solution)/shard_map/all_to_all | solution.py:485
  67.4 10.4 %all-to-all-done.1 = bf16[128,16,128]{2,1,0:T(8,128)(2,1)S(1)} async-done(((bf16[128,16,128]{2,1,0:T(8,128)(2,1)}), bf16[128,16,128]{2,1,0:T(8,128)(2,1)S(1)}, u32[]{:S(2)}, u32[]{:S(2)}) %all-to-all-start.1) | async-done | bytes 524320 | tf_op jit(solution)/shard_map/all_to_all | solution.py:485
  77.8 4.0 %shard_map.194 = (bf16[80,512]{1,0:T(8,128)(2,1)S(1)}, bf16[2048,128]{1,0:T(8,128)(2,1)}) custom-call(bf16[2048,128]{1,0:T(8,128)(2,1)S(1)} %bitcast.8, bf16[640,512]{1,0:T(8,128)(2,1)S(1)} %get-tuple-element.36.base_ref, f32[80,512]{1,0:T(8,128)S(1)} %get-tuple-element.37.self_ref, bf16[80,512]{1,0:T(8,128)(2,1)S(1)} %get-tuple-element.35.state_ref, ...), custom_call_target="tpu_custom_call" | custom-call | tf_op jit(solution)/shard_map/pallas_call | solution.py:74
  81.8 5.9 %all-to-all-start.2 = ((bf16[128,16,128]{2,1,0:T(8,128)(2,1)}), bf16[128,16,128]{2,1,0:T(8,128)(2,1)S(1)}, u32[]{:S(2)}, u32[]{:S(2)}) async-start(bf16[128,16,128]{2,1,0:T(8,128)(2,1)} %bitcast.6), calls=%async_computation.2 | async-start | bytes 1048576 | tf_op jit(solution)/shard_map/all_to_all | solution.py:485
  89.6 10.5 %all-to-all-done.2 = bf16[128,16,128]{2,1,0:T(8,128)(2,1)S(1)} async-done(((bf16[128,16,128]{2,1,0:T(8,128)(2,1)}), bf16[128,16,128]{2,1,0:T(8,128)(2,1)S(1)}, u32[]{:S(2)}, u32[]{:S(2)}) %all-to-all-start.2) | async-done | bytes 524320 | tf_op jit(solution)/shard_map/all_to_all | solution.py:485
  100.0 2.7 %shard_map.196 = bf16[80,512]{1,0:T(8,128)(2,1)S(1)} custom-call(bf16[2048,128]{1,0:T(8,128)(2,1)S(1)} %bitcast.9, bf16[640,512]{1,0:T(8,128)(2,1)S(1)} %get-tuple-element.40.base_ref, f32[80,512]{1,0:T(8,128)S(1)} %get-tuple-element.41.self_ref, bf16[80,512]{1,0:T(8,128)(2,1)S(1)} %get-tuple-element.39.state_ref, s32[1,640]{1,0:T(1,128)S(1)} %broadcast_in_dim.7.src_ref, ...), custom_call_target="tpu_custom_call" | custom-call | tf_op jit(solution)/shard_map/pallas_call | solution.py:74
  103.5 3.9 %collective-permute-start.9 = (bf16[80,512]{1,0:T(8,128)(2,1)S(1)}, bf16[80,512]{1,0:T(8,128)(2,1)S(1)}, u32[]{:S(2)}, u32[]{:S(2)}) collective-permute-start(bf16[80,512]{1,0:T(8,128)(2,1)S(1)} %shard_map.196), channel_id=1, source_target_pairs={{1,2},{2,1},{3,4},{4,3},{5,6},{6,5},{7,8},{8,7},{9,10},{10,9},{11,... | collective-permute-start | bytes 245768 | tf_op jit(solution)/shard_map/ppermute | solution.py:418
  107.4 3.4 %collective-permute-done.9 = bf16[80,512]{1,0:T(8,128)(2,1)S(1)} collective-permute-done((bf16[80,512]{1,0:T(8,128)(2,1)S(1)}, bf16[80,512]{1,0:T(8,128)(2,1)S(1)}, u32[]{:S(2)}, u32[]{:S(2)}) %collective-permute-start.9) | collective-permute-done | bytes 81952 | tf_op jit(solution)/shard_map/ppermute | solution.py:418
  110.8 2.9 %collective-permute-start.10 = (bf16[240,512]{1,0:T(8,128)(2,1)S(1)}, bf16[240,512]{1,0:T(8,128)(2,1)S(1)}, u32[]{:S(2)}, u32[]{:S(2)}) collective-permute-start(bf16[240,512]{1,0:T(8,128)(2,1)S(1)} %pad_maximum_fusion.n0), channel_id=1, source_target_pairs={{0,16},{16,0},{32,48},{48,32},{64,80},{80,64},{96,112},{112,96},{1... | collective-permute-start | bytes 737288 | tf_op jit(solution)/shard_map/ppermute | solution.py:419
  113.7 2.2 %collective-permute-start.11 = (bf16[240,512]{1,0:T(8,128)(2,1)S(1)}, bf16[240,512]{1,0:T(8,128)(2,1)S(1)}, u32[]{:S(2)}, u32[]{:S(2)}) collective-permute-start(bf16[240,512]{1,0:T(8,128)(2,1)S(1)} %pad_maximum_fusion.n0), channel_id=1, source_target_pairs={{16,32},{32,16},{48,64},{64,48},{80,96},{96,80},{17,33},{33,17},{4... | collective-permute-start | bytes 737288 | tf_op jit(solution)/shard_map/ppermute | solution.py:418
  115.9 5.3 %collective-permute-done.11.n2 = bf16[240,512]{1,0:T(8,128)(2,1)S(1)} collective-permute-done((bf16[240,512]{1,0:T(8,128)(2,1)S(1)}, bf16[240,512]{1,0:T(8,128)(2,1)S(1)}, u32[]{:S(2)}, u32[]{:S(2)}) %collective-permute-start.11) | collective-permute-done | bytes 245792 | tf_op jit(solution)/shard_map/ppermute | solution.py:418
  121.2 12.2 %decode.1 = bf16[2048,512]{1,0:T(8,128)(2,1)} custom-call(s32[2]{0:T(128)S(1)} %pad_add_fusion.odd_ref, bf16[240,512]{1,0:T(8,128)(2,1)S(1)} %pad_maximum_fusion.n0, bf16[240,512]{1,0:T(8,128)(2,1)S(1)} %collective-permute-done.10.n1, bf16[240,512]{1,0:T(8,128)(2,1)S(1)} %collective-permute-done.11.n2, s32[3,2048]{1,0:T(4,128)} %slots_ref.3, ...), custom_call_target="tpu_custom_call" | custom-call | tf_op jit(solution)/shard_map/decode/pallas_call | solution.py:388
  (32 shorter events, 9.6 us)
Async XLA Ops:
  0.0 6.7 %collective-permute-start = (bf16[80,512]{1,0:T(8,128)(2,1)}, bf16[80,512]{1,0:T(8,128)(2,1)S(1)}, u32[]{:S(2)}, u32[]{:S(2)}) collective-permute-start(bf16[80,512]{1,0:T(8,128)(2,1)} %mesh_ref.1), channel_id=1, source_target_pairs={{0,1},{1,0},{2,3},{3,2},{4,5},{5,4},{6,7},{7,6},{8,9},{9,8},{10,11... | collective-permute-start | bytes 245768 | tf_op jit(solution)/shard_map/ppermute | solution.py:419
  1.6 7.5 %collective-permute-start.1 = (bf16[80,512]{1,0:T(8,128)(2,1)}, bf16[80,512]{1,0:T(8,128)(2,1)S(1)}, u32[]{:S(2)}, u32[]{:S(2)}) collective-permute-start(bf16[80,512]{1,0:T(8,128)(2,1)} %mesh_ref.1), channel_id=1, source_target_pairs={{1,2},{2,1},{3,4},{4,3},{5,6},{6,5},{7,8},{8,7},{9,10},{10,9},{11,... | collective-permute-start | bytes 245768 | tf_op jit(solution)/shard_map/ppermute | solution.py:418
  9.1 10.4 %collective-permute-start.2 = (bf16[240,512]{1,0:T(8,128)(2,1)S(1)}, bf16[240,512]{1,0:T(8,128)(2,1)S(1)}, u32[]{:S(2)}, u32[]{:S(2)}) collective-permute-start(bf16[240,512]{1,0:T(8,128)(2,1)S(1)} %constant_dynamic-update-slice_fusion.n0), channel_id=1, source_target_pairs={{0,16},{16,0},{32,48},{48,32},{64,80},{80,64},{96,112},{112,96},{1... | collective-permute-start | bytes 737288 | tf_op jit(solution)/shard_map/ppermute | solution.py:419
  11.2 8.3 %collective-permute-start.3 = (bf16[240,512]{1,0:T(8,128)(2,1)S(1)}, bf16[240,512]{1,0:T(8,128)(2,1)S(1)}, u32[]{:S(2)}, u32[]{:S(2)}) collective-permute-start(bf16[240,512]{1,0:T(8,128)(2,1)S(1)} %constant_dynamic-update-slice_fusion.n0), channel_id=1, source_target_pairs={{16,32},{32,16},{48,64},{64,48},{80,96},{96,80},{17,33},{33,17},{4... | collective-permute-start | bytes 737288 | tf_op jit(solution)/shard_map/ppermute | solution.py:418
  19.6 20.9 %copy-start.3 = (s32[1,128,4]{1,2,0:T(4,128)S(1)}, s32[1,128,4]{1,2,0:T(4,128)}, u32[]{:S(2)}) copy-start(s32[1,128,4]{1,2,0:T(4,128)} %param.24) | copy-start | bytes 6148
  19.6 29.8 %copy-start = (bf16[80,512]{1,0:T(8,128)(2,1)S(1)}, bf16[80,512]{1,0:T(8,128)(2,1)}, u32[]{:S(2)}) copy-start(bf16[80,512]{1,0:T(8,128)(2,1)} %mesh_ref.1) | copy-start | bytes 245764
  28.5 3.7 %collective-permute-start.4 = (bf16[240,512]{1,0:T(8,128)(2,1)S(1)}, bf16[240,512]{1,0:T(8,128)(2,1)S(1)}, u32[]{:S(2)}, u32[]{:S(2)}) collective-permute-start(bf16[240,512]{1,0:T(8,128)(2,1)S(1)} %get-tuple-element.28), channel_id=1, source_target_pairs={{0,16},{16,0},{32,48},{48,32},{64,80},{80,64},{96,112},{112,96},{1... | collective-permute-start | bytes 737288 | tf_op jit(solution)/shard_map/ppermute | solution.py:419
  28.6 7.5 %collective-permute-start.5 = (bf16[240,512]{1,0:T(8,128)(2,1)S(1)}, bf16[240,512]{1,0:T(8,128)(2,1)S(1)}, u32[]{:S(2)}, u32[]{:S(2)}) collective-permute-start(bf16[240,512]{1,0:T(8,128)(2,1)S(1)} %get-tuple-element.29), channel_id=1, source_target_pairs={{16,32},{32,16},{48,64},{64,48},{80,96},{96,80},{17,33},{33,17},{4... | collective-permute-start | bytes 737288 | tf_op jit(solution)/shard_map/ppermute | solution.py:418
  36.2 21.4 %collective-permute-start.6 = (bf16[80,512]{1,0:T(8,128)(2,1)S(1)}, bf16[80,512]{1,0:T(8,128)(2,1)S(1)}, u32[]{:S(2)}, u32[]{:S(2)}) collective-permute-start(bf16[80,512]{1,0:T(8,128)(2,1)S(1)} %get-tuple-element.44), channel_id=1, source_target_pairs={{0,1},{1,0},{2,3},{3,2},{4,5},{5,4},{6,7},{7,6},{8,9},{9,8},{10,11... | collective-permute-start | bytes 245768 | tf_op jit(solution)/shard_map/ppermute | solution.py:419
  36.3 21.3 %collective-permute-start.7 = (bf16[80,512]{1,0:T(8,128)(2,1)S(1)}, bf16[80,512]{1,0:T(8,128)(2,1)S(1)}, u32[]{:S(2)}, u32[]{:S(2)}) collective-permute-start(bf16[80,512]{1,0:T(8,128)(2,1)S(1)} %get-tuple-element.43), channel_id=1, source_target_pairs={{1,2},{2,1},{3,4},{4,3},{5,6},{6,5},{7,8},{8,7},{9,10},{10,9},{11,... | collective-permute-start | bytes 245768 | tf_op jit(solution)/shard_map/ppermute | solution.py:418
  41.2 16.4 %all-to-all-start = ((s32[128,1,4]{2,1,0:T(1,128)}), s32[128,1,4]{2,1,0:T(1,128)S(1)}, u32[]{:S(2)}, u32[]{:S(2)}) async-start(s32[128,1,4]{2,1,0:T(1,128)} %bitcast.2), calls=%async_computation | async-start | bytes 131072 | tf_op jit(solution)/shard_map/all_to_all | solution.py:473
  50.9 14.6 %copy-start.1 = (s32[640]{0:T(1024)S(1)}, s32[640]{0:T(1024)}, u32[]{:S(2)}) copy-start(s32[640]{0:T(1024)} %param.26) | copy-start | bytes 7684
  50.9 14.6 %copy-start.2 = (s32[640]{0:T(1024)S(1)}, s32[640]{0:T(1024)}, u32[]{:S(2)}) copy-start(s32[640]{0:T(1024)} %param.25) | copy-start | bytes 7684
  59.7 18.1 %all-to-all-start.1 = ((bf16[128,16,128]{2,1,0:T(8,128)(2,1)}), bf16[128,16,128]{2,1,0:T(8,128)(2,1)S(1)}, u32[]{:S(2)}, u32[]{:S(2)}) async-start(bf16[128,16,128]{2,1,0:T(8,128)(2,1)} %bitcast.4), calls=%async_computation.1 | async-start | bytes 1048576 | tf_op jit(solution)/shard_map/all_to_all | solution.py:485
  81.8 18.2 %all-to-all-start.2 = ((bf16[128,16,128]{2,1,0:T(8,128)(2,1)}), bf16[128,16,128]{2,1,0:T(8,128)(2,1)S(1)}, u32[]{:S(2)}, u32[]{:S(2)}) async-start(bf16[128,16,128]{2,1,0:T(8,128)(2,1)} %bitcast.6), calls=%async_computation.2 | async-start | bytes 1048576 | tf_op jit(solution)/shard_map/all_to_all | solution.py:485
  102.8 4.6 %collective-permute-start.8 = (bf16[80,512]{1,0:T(8,128)(2,1)S(1)}, bf16[80,512]{1,0:T(8,128)(2,1)S(1)}, u32[]{:S(2)}, u32[]{:S(2)}) collective-permute-start(bf16[80,512]{1,0:T(8,128)(2,1)S(1)} %shard_map.196), channel_id=1, source_target_pairs={{0,1},{1,0},{2,3},{3,2},{4,5},{5,4},{6,7},{7,6},{8,9},{9,8},{10,11... | collective-permute-start | bytes 245768 | tf_op jit(solution)/shard_map/ppermute | solution.py:419
  103.5 7.3 %collective-permute-start.9 = (bf16[80,512]{1,0:T(8,128)(2,1)S(1)}, bf16[80,512]{1,0:T(8,128)(2,1)S(1)}, u32[]{:S(2)}, u32[]{:S(2)}) collective-permute-start(bf16[80,512]{1,0:T(8,128)(2,1)S(1)} %shard_map.196), channel_id=1, source_target_pairs={{1,2},{2,1},{3,4},{4,3},{5,6},{6,5},{7,8},{8,7},{9,10},{10,9},{11,... | collective-permute-start | bytes 245768 | tf_op jit(solution)/shard_map/ppermute | solution.py:418
  110.8 5.1 %collective-permute-start.10 = (bf16[240,512]{1,0:T(8,128)(2,1)S(1)}, bf16[240,512]{1,0:T(8,128)(2,1)S(1)}, u32[]{:S(2)}, u32[]{:S(2)}) collective-permute-start(bf16[240,512]{1,0:T(8,128)(2,1)S(1)} %pad_maximum_fusion.n0), channel_id=1, source_target_pairs={{0,16},{16,0},{32,48},{48,32},{64,80},{80,64},{96,112},{112,96},{1... | collective-permute-start | bytes 737288 | tf_op jit(solution)/shard_map/ppermute | solution.py:419
  113.7 7.5 %collective-permute-start.11 = (bf16[240,512]{1,0:T(8,128)(2,1)S(1)}, bf16[240,512]{1,0:T(8,128)(2,1)S(1)}, u32[]{:S(2)}, u32[]{:S(2)}) collective-permute-start(bf16[240,512]{1,0:T(8,128)(2,1)S(1)} %pad_maximum_fusion.n0), channel_id=1, source_target_pairs={{16,32},{32,16},{48,64},{64,48},{80,96},{96,80},{17,33},{33,17},{4... | collective-permute-start | bytes 737288 | tf_op jit(solution)/shard_map/ppermute | solution.py:418

commit v4 on v3

--- a/solution.py
+++ b/solution.py
@@ -13,8 +13,10 @@
 DEC_FAN = 3
 SIDE = 3
 ENC_ROWS = 1024
-DEC_ROWS = 512
-PRE_ROWS = 512
+DEC_ROWS = 1024
+FAR_ROWS = 512
+FAR_PART = 512
+PRE_ROWS = 1024
 
 
 def up128(n):
@@ -27,6 +29,10 @@
 
 def silu(v):
     half = 0.5 * v
+    return half + half * jnp.tanh(half)
+
+
+def silu_of_half(half):
     return half + half * jnp.tanh(half)
 
 
@@ -88,54 +94,39 @@
     return copies
 
 
-def pre_kernel(
-    grid_ref, ws_ref, dr_ref, wr_ref, slots_ref, s_ref, wr_out, slots_out, r_ref, w, g, r, sems
-):
-    rows = PRE_ROWS
-    count = grid_ref.shape[0] // rows
-    parts = [slice(i * rows, (i + 1) * rows) for i in range(count)]
-    pairs = [(ws_ref, w.at[0]), (dr_ref, w.at[1])]
-    pairs += [(grid_ref.at[part], g.at[part]) for part in parts]
-    pairs += [(wr_ref, wr_out), (slots_ref, slots_out)]
-    copies = fetch(pairs, sems)
-    copies[0].wait()
-    copies[1].wait()
-    backs = []
-    for i, part in enumerate(parts):
-        copies[2 + i].wait()
-        x = g[part]
-        s_ref[part] = bf(dot(x, w[0]))
-        r[part] = bf(dot(x, w[1]))
-        backs.append(
-            pltpu.make_async_copy(r.at[part], r_ref.at[part], sems.at[len(pairs) + i])
-        )
-        backs[-1].start()
-    for copy in copies[2 + count :] + backs:
-        copy.wait()
-
-
-def pre(grid_latent, ws, dr, wr, slots):
+def receiver_kernel(grid_ref, w_ref, r_ref):
+    r_ref[...] = bf(dot(grid_ref[...], w_ref[...] * jnp.bfloat16(0.5)))
+
+
+def receiver(grid_latent, w):
     n, d = grid_latent.shape
-    args = near_to(pltpu.HBM, [grid_latent, ws, dr, wr, slots])
+    tile = pl.BlockSpec((PRE_ROWS, d), lambda i: (i, 0))
     return pl.pallas_call(
-        pre_kernel,
-        in_specs=[HBM] * len(args),
-        out_specs=[VMEM] * 3 + [HBM],
-        out_shape=[
-            pltpu.VMEM((n, d), jnp.bfloat16),
-            pltpu.VMEM((d, d), jnp.bfloat16),
-            pltpu.VMEM(slots.shape, jnp.int32),
-            pltpu.HBM((n, d), jnp.bfloat16),
-        ],
-        scratch_shapes=[
-            pltpu.VMEM((2, d, d), jnp.bfloat16),
-            pltpu.VMEM((n, d), jnp.bfloat16),
-            pltpu.VMEM((n, d), jnp.bfloat16),
-            pltpu.SemaphoreType.DMA((4 + 2 * (n // PRE_ROWS),)),
-        ],
-        compiler_params=pltpu.CompilerParams(vmem_limit_bytes=20 << 20),
-        name="pre",
-    )(*args)
+        receiver_kernel,
+        grid=(n // PRE_ROWS,),
+        in_specs=[tile, pl.BlockSpec((d, d), lambda i: (0, 0))],
+        out_specs=tile,
+        out_shape=pltpu.HBM((n, d), jnp.bfloat16),
+        compiler_params=pltpu.CompilerParams(vmem_limit_bytes=16 << 20),
+        name="receiver",
+    )(*near_to(pltpu.HBM, [grid_latent, w]))
+
+
+def line_rows(rows, near, start, odd_ref):
+    owned = rows.shape[0] // SIDE
+    odd = odd_ref[1]
+    for at, spot in enumerate((1, 2 - 2 * odd, 2 * odd)):
+        to = pl.multiple_of(start + spot * owned, 16)
+        near[pl.ds(to, owned), :] = rows[at * owned : (at + 1) * owned]
+
+
+def line_start(place, odd_ref, line):
+    odd = odd_ref[0]
+    return (1, 2 - 2 * odd, 2 * odd)[place] * line
+
+
+def up256(n):
+    return -(-n // 256) * 256
 
 
 def block_at(odd_ref, place):
@@ -146,29 +137,69 @@
     return spots[0] * SIDE + spots[1]
 
 
-def enc_kernel(odd_ref, s_ref, slots_ref, n0, n1, n2, wr_ref, o0, o1, o2, near, acc, hid):
+def enc_near_kernel(
+    odd_ref, n0, n1, slots_ref, wr_ref, ws_ref, grid_ref, v_ref, slots, wr, near, ws, g, sems
+):
+    line = n0.shape[0]
+    wide = near.shape[0] // 2
+    rows = ENC_ROWS
+    parts = [slice(i, i + rows) for i in range(0, g.shape[0], rows)]
+    pairs = [(wr_ref, wr), (ws_ref, ws), (slots_ref, slots)]
+    pairs += [(grid_ref.at[part], g.at[part]) for part in parts]
+    copies = fetch(pairs, sems)
+    near[...] = jnp.zeros_like(near)
+    copies[0].wait()
+    for k, ref in enumerate((n0, n1)):
+        line_rows(bf(dot(ref[...], wr[...]) * 0.5), near, k * wide, odd_ref)
+    copies[1].wait()
+    copies[2].wait()
+    for i, part in enumerate(parts):
+        copies[3 + i].wait()
+        s = dot(g[part], ws[...]) * 0.5
+        for f in range(ENC_FAN):
+            slot = slots[f : f + 1, part]
+            chosen = jnp.concatenate(
+                [hot_rows(slot - line_start(k, odd_ref, line), wide) for k in range(2)], axis=1
+            )
+            v_ref[f, part] = dot(chosen, near[...]) + s
+
+
+def encode_near(odd, grid_latent, slot_rows, near, wr, ws):
+    n, d = grid_latent.shape
+    return on_chip(
+        enc_near_kernel,
+        list(near),
+        [
+            ((ENC_FAN, n, d), jnp.float32),
+            (slot_rows.shape, jnp.int32),
+            ((d, d), jnp.bfloat16),
+        ],
+        far=[slot_rows, wr, ws, grid_latent],
+        scratch=[
+            pltpu.VMEM((2 * up256(near[0].shape[0]), d), jnp.bfloat16),
+            pltpu.VMEM((d, d), jnp.bfloat16),
+            pltpu.VMEM((n, d), jnp.bfloat16),
+            pltpu.SemaphoreType.DMA((3 + n // ENC_ROWS,)),
+        ],
+        odd=odd,
+    )
+
+
+def enc_far_kernel(odd_ref, n2, v_ref, slots_ref, wr_ref, o0, o1, o2, near, acc, hid):
+    line = n2.shape[0]
+    owned = line // SIDE
+    slots = SIDE * line
     rows = hid.shape[0] // ENC_FAN
-    owned = n0.shape[0] // SIDE
-    height = near.shape[0]
-    slots = SIDE * SIDE * owned
-
-    def block(k, at):
-        start = pl.multiple_of(block_at(odd_ref, k * SIDE + at) * owned, 16)
-        return pl.ds(start, owned)
-
-    w = wr_ref[...]
-    for k, ref in enumerate((n0, n1, n2)):
-        v = bf(dot(ref[...], w))
-        for at in range(SIDE):
-            near[block(k, at), :] = v[at * owned : (at + 1) * owned]
-    near[slots:] = jnp.zeros((height - slots, near.shape[1]), jnp.bfloat16)
-
-    for step in range(s_ref.shape[0] // rows):
+
+    near[...] = jnp.zeros_like(near)
+    line_rows(bf(dot(n2[...], wr_ref[...]) * 0.5), near, 0, odd_ref)
+    start = line_start(2, odd_ref, line)
+    for step in range(v_ref.shape[1] // rows):
         part = slice(step * rows, (step + 1) * rows)
-        s = s_ref[part].astype(jnp.float32)
         for f in range(ENC_FAN):
-            v = dot(hot_rows(slots_ref[f : f + 1, part], height), near[...]) + s
-            hid[f * rows : (f + 1) * rows] = bf(silu(v))
+            chosen = hot_rows(slots_ref[f : f + 1, part] - start, near.shape[0])
+            v = dot(chosen, near[...]) + v_ref[f, part]
+            hid[f * rows : (f + 1) * rows] = bf(silu_of_half(v))
         chosen = jnp.concatenate(
             [hot_columns(slots_ref[f : f + 1, part], slots) for f in range(ENC_FAN)], axis=1
         )
@@ -177,24 +208,23 @@
 
     for k, ref in enumerate((o0, o1, o2)):
         for at in range(SIDE):
-            ref[at * owned : (at + 1) * owned] = bf(acc[block(k, at), :])
-
-
-def encode(odd, s, slot_rows, near, wr):
-    _, d = s.shape
-    third = near[0].shape[0]
-    height = up128(SIDE * third)
-    return on_chip(
-        enc_kernel,
-        [s, slot_rows, *near, wr],
-        [((third, d), jnp.bfloat16)] * SIDE,
+            first = pl.multiple_of(block_at(odd_ref, k * SIDE + at) * owned, 16)
+            ref[at * owned : (at + 1) * owned] = bf(acc[pl.ds(first, owned), :])
+
+
+def encode_far(odd, near, prepared):
+    v, slots, wr = prepared
+    line, d = near.shape
+    return on_chip(
+        enc_far_kernel,
+        [near, v, slots, wr],
+        [((line, d), jnp.bfloat16)] * SIDE,
         scratch=[
-            pltpu.VMEM((height, d), jnp.bfloat16),
-            pltpu.VMEM((SIDE * third, d), jnp.float32),
+            pltpu.VMEM((up256(line), d), jnp.bfloat16),
+            pltpu.VMEM((SIDE * line, d), jnp.float32),
             pltpu.VMEM((ENC_FAN * ENC_ROWS, d), jnp.bfloat16),
         ],
         odd=odd,
-        limit=28,
     )
 
 
@@ -308,7 +338,7 @@
     new = bf(state_ref[...].astype(jnp.float32) + norm(silu(update)))
     copies[2].wait()
     if last:
-        outs[0][...] = bf(dot(new, w[2]))
+        outs[0][...] = bf(dot(new, w[2]) * 0.5)
     else:
         outs[0][...] = new
         pack(dot(new, w[2]), asked_ref, wide, outs[1])
@@ -332,75 +362,91 @@
     )
 
 
-def dec_kernel(
-    odd_ref, n0, n1, n2, slots_ref, wo_ref, r_ref, grid_ref, out_ref, near, slots_in, w, r, g, sems
+def dec_near_kernel(
+    odd_ref, n0, n1, slots_ref, wo_ref, grid_ref, r_ref, v_ref, slots, w, g, near, r, sems
 ):
-    owned = n0.shape[0] // SIDE
-    height = near.shape[0]
-    slots = SIDE * SIDE * owned
+    line = n0.shape[0]
+    wide = near.shape[0] // 2
+    rows = DEC_ROWS
+    parts = [slice(i, i + rows) for i in range(0, r_ref.shape[0], rows)]
+    pairs = [(slots_ref, slots)] + [(r_ref.at[part], r.at[part]) for part in parts]
+    pairs += [(wo_ref, w), (grid_ref, g)]
+    copies = fetch(pairs, sems)
+    near[...] = jnp.zeros_like(near)
+    for k, ref in enumerate((n0, n1)):
+        line_rows(ref[...], near, k * wide, odd_ref)
+    copies[0].wait()
+    for i, part in enumerate(parts):
+        copies[1 + i].wait()
+        own = r[part].astype(jnp.float32)
+        for f in range(DEC_FAN):
+            slot = slots[f : f + 1, part]
+            chosen = jnp.concatenate(
+                [hot_rows(slot - line_start(k, odd_ref, line), wide) for k in range(2)], axis=1
+            )
+            v_ref[f, part] = dot(chosen, near[...]) + own
+    for copy in copies[1 + len(parts) :]:
+        copy.wait()
+
+
+def dec_far_kernel(odd_ref, n2, v, slots, w, g, out_ref, near):
+    line = n2.shape[0]
     rows = out_ref.shape[0]
-    steps = r_ref.shape[0] // rows
     step = pl.program_id(0)
-    small = [
-        pltpu.make_async_copy(slots_ref, slots_in, sems.at[0]),
-        pltpu.make_async_copy(wo_ref, w, sems.at[1]),
-    ]
-
-    def tile(i):
-        part = pl.ds(pl.multiple_of(i * rows, rows), rows)
-        return (
-            pltpu.make_async_copy(r_ref.at[part], r.at[part], sems.at[2 + i]),
-            pltpu.make_async_copy(grid_ref.at[part], g.at[part], sems.at[2 + steps + i]),
-        )
 
     @pl.when(step == 0)
     def _():
-        for copy in small:
-            copy.start()
-        for i in range(steps):
-            for copy in tile(i):
-                copy.start()
-        for k, ref in enumerate((n0, n1, n2)):
-            for at in range(SIDE):
-                start = pl.multiple_of(block_at(odd_ref, k * SIDE + at) * owned, 16)
-                near[pl.ds(start, owned), :] = ref[at * owned : (at + 1) * owned]
-        near[slots:] = jnp.zeros((height - slots, near.shape[1]), jnp.bfloat16)
-        for copy in small:
-            copy.wait()
-
-    for copy in tile(step):
-        copy.wait()
-    part = pl.ds(pl.multiple_of(step * rows, rows), rows)
-    own = r[part, :].astype(jnp.float32)
-    total = None
-    for f in range(DEC_FAN):
-        v = dot(hot_rows(slots_in[f : f + 1, part], height), near[...]) + own
-        h = bf(silu(v)).astype(jnp.float32)
-        total = h if total is None else total + h
-    update = dot(bf(total), w[...])
-    out_ref[...] = bf(g[part, :].astype(jnp.float32) + norm(update))
-
-
-def decode(odd, r, grid_latent, slot_rows, near, wo):
+        near[...] = jnp.zeros_like(near)
+        line_rows(n2[...], near, 0, odd_ref)
+
+    start = line_start(2, odd_ref, line)
+    for at in range(0, rows, FAR_PART):
+        part = pl.ds(pl.multiple_of(step * rows + at, FAR_PART), FAR_PART)
+        total = None
+        for f in range(DEC_FAN):
+            chosen = hot_rows(slots[f : f + 1, part] - start, near.shape[0])
+            h = silu_of_half(dot(chosen, near[...]) + v[f, part, :])
+            total = h if total is None else total + h
+        update = dot(bf(total), w[...])
+        out_ref[at : at + FAR_PART] = bf(g[part, :].astype(jnp.float32) + norm(update))
+
+
+def decode_near(odd, r, grid_latent, slot_rows, near, wo):
     n, d = r.shape
-    height = up128(SIDE * near[0].shape[0])
-    args = near_to(pltpu.VMEM, near) + near_to(pltpu.HBM, [slot_rows, wo, r, grid_latent])
+    wide = up256(near[0].shape[0])
+    return on_chip(
+        dec_near_kernel,
+        list(near),
+        [
+            ((DEC_FAN, n, d), jnp.float32),
+            (slot_rows.shape, jnp.int32),
+            (wo.shape, jnp.bfloat16),
+            ((n, d), jnp.bfloat16),
+        ],
+        far=[slot_rows, wo, grid_latent, r],
+        scratch=[
+            pltpu.VMEM((2 * wide, d), jnp.bfloat16),
+            pltpu.VMEM((n, d), jnp.bfloat16),
+            pltpu.SemaphoreType.DMA((3 + n // DEC_ROWS,)),
+        ],
+        odd=odd,
+        limit=16,
+    )
+
+
+def decode_far(odd, near, prepared):
+    v, slots, w, g = prepared
+    n, d = g.shape
+    args = near_to(pltpu.VMEM, [near, v, slots, w, g])
     return pl.pallas_call(
-        dec_kernel,
-        grid=(n // DEC_ROWS,),
-        in_specs=[pl.BlockSpec(memory_space=pltpu.SMEM)] + [VMEM] * 3 + [HBM] * 4,
-        out_specs=pl.BlockSpec((DEC_ROWS, d), lambda i: (i, 0)),
+        dec_far_kernel,
+        grid=(n // FAR_ROWS,),
+        in_specs=[pl.BlockSpec(memory_space=pltpu.SMEM)] + [VMEM] * len(args),
+        out_specs=pl.BlockSpec((FAR_ROWS, d), lambda i: (i, 0)),
         out_shape=jax.ShapeDtypeStruct((n, d), jnp.bfloat16),
-        scratch_shapes=[
-            pltpu.VMEM((height, d), jnp.bfloat16),
-            pltpu.VMEM(slot_rows.shape, jnp.int32),
-            pltpu.VMEM((d, d), jnp.bfloat16),
-            pltpu.VMEM((n, d), jnp.bfloat16),
-            pltpu.VMEM((n, d), jnp.bfloat16),
-            pltpu.SemaphoreType.DMA((2 + 2 * (n // DEC_ROWS),)),
-        ],
-        compiler_params=pltpu.CompilerParams(vmem_limit_bytes=28 << 20),
-        name="decode",
+        scratch_shapes=[pltpu.VMEM((up256(near.shape[0]), d), jnp.bfloat16)],
+        compiler_params=pltpu.CompilerParams(vmem_limit_bytes=20 << 20),
+        name="decode_far",
     )(odd, *args)
 
 
@@ -471,13 +517,14 @@
     odd = jnp.stack([lax.axis_index("lat") % 2, lax.axis_index("lon") % 2]).astype(jnp.int32)
     near = neighbours(mesh_latent)
     asked = lax.all_to_all(wanted, ("lat", "lon"), split_axis=0, concat_axis=0, tiled=True)
-    s, e_receiver, e_slots, r = pre(
-        grid_latent, encoder_sender, decoder_receiver, encoder_receiver, encoder_slots
-    )
-    sums = encode(odd, s, e_slots, near, e_receiver)
+    prepared = encode_near(
+        odd, grid_latent, encoder_slots, near[:2], encoder_receiver, encoder_sender
+    )
+    sums = encode_far(odd, near[2], prepared)
     own, a, b = to_owners(sums, owned)
     staged = stage(mesh_latent, encoder_output, encoder_merge, encoder_self, process_sender)
     state, outgoing = merge(own, a, b, mesh_latent, asked, staged)
+    r = receiver(grid_latent, decoder_receiver)
     src = edge_source[None, :]
     tgt = edge_target[None, :]
     for depth in range(LAYERS):
@@ -507,7 +554,8 @@
         if not last:
             state, outgoing = result
     near = neighbours(result[0])
-    return decode(odd, r, grid_latent, decoder_slots, near, decoder_output)
+    prepared = decode_near(odd, r, grid_latent, decoder_slots, near[:2], decoder_output)
+    return decode_far(odd, near[2], prepared)
 
 
 def solution(mesh):

time: 134 us -> 130 us (0.970)
  waiting for transfers between devices: 42.7 us -> 37.3 us
  Pallas kernels: 40.2 us -> 42.2 us
    pallas_call x7 -> x9, Pallas kernels: 22.8 us -> 31.1 us  [on_chip(): pl.pallas_call(kernel, in_specs=specs, out_specs=[VMEM] * len(outs), out_...]
    pallas_call x2, Pallas kernels: 17.3 us -> 11.1 us  [the longest x1 7.28 us: decode_far(): pl.pallas_call(dec_far_kernel, grid=(n // FAR_ROWS,), in_specs=[pl.BlockS...]
    ppermute x6, waiting for transfers between devices: 15.1 us -> 9.74 us  [swap_both(): b = lax.ppermute(to_second, axis, second)]
  transfers between devices with their start and end apart: 15 -> 15, of which waited for: 7 -> 6; matrix products, arithmetic and copies ran while one was open for 1% -> 1% of each run, Pallas kernels for 8% -> 16%
where the time goes in v4:
time: 130 us
  starting transfers between devices  48.3 us (37%)
  Pallas kernels  42.2 us (32%)
  waiting for transfers between devices  37.3 us (29%)
  local copies, waits for them, and re-layouts  1.69 us (1%)
    pallas_call x9, Pallas kernels, on_chip(): pl.pallas_call(kernel, in_specs=specs, out_specs=[VMEM] * len(outs), out_...  31.1 us
    ppermute x6, starting transfers between devices, swap_both(): b = lax.ppermute(to_second, axis, second)  21 us
    all_to_all x2, waiting for transfers between devices, body(): lax.all_to_all(outgoing.reshape(tiles, -1, 128), ('lat', 'lon'), split_ax...  20.9 us
    all_to_all x2, starting transfers between devices, body(): lax.all_to_all(outgoing.reshape(tiles, -1, 128), ('lat', 'lon'), split_ax...  11.7 us
    ppermute x6, waiting for transfers between devices, swap_both(): b = lax.ppermute(to_second, axis, second)  9.74 us
    all_to_all x1, starting transfers between devices, body(): lax.all_to_all(wanted, ('lat', 'lon'), split_axis=0, concat_axis=0, tiled...  8.14 us
    ppermute x6, starting transfers between devices, swap_both(): a = lax.ppermute(to_first, axis, first)  7.53 us
    pallas_call x1, Pallas kernels, decode_far(): pl.pallas_call(dec_far_kernel, grid=(n // FAR_ROWS,), in_specs=[pl.BlockS...  7.28 us
  transfers between devices with their start and end apart: 15, of which 6 were waited for; matrix products, arithmetic and copies ran while one was open for 1% of the time, Pallas kernels for 16%

profile of v4, /device:TPU:3, one launch (start us, length us, event | category | flops | bytes accessed | tf_op | source)
XLA Modules:
  0.0 129.9 jit_solution(6383341506225080026)
XLA Ops:
  1.6 4.1 %collective-permute-start.1 = (bf16[80,512]{1,0:T(8,128)(2,1)}, bf16[80,512]{1,0:T(8,128)(2,1)S(1)}, u32[]{:S(2)}, u32[]{:S(2)}) collective-permute-start(bf16[80,512]{1,0:T(8,128)(2,1)} %mesh_ref.1), channel_id=1, source_target_pairs={{1,2},{2,1},{3,4},{4,3},{5,6},{6,5},{7,8},{8,7},{9,10},{10,9},{11,... | collective-permute-start | bytes 245768 | tf_op jit(solution)/shard_map/ppermute | solution.py:464
  6.7 2.4 %collective-permute-done.1 = bf16[80,512]{1,0:T(8,128)(2,1)S(1)} collective-permute-done((bf16[80,512]{1,0:T(8,128)(2,1)}, bf16[80,512]{1,0:T(8,128)(2,1)S(1)}, u32[]{:S(2)}, u32[]{:S(2)}) %collective-permute-start.1) | collective-permute-done | bytes 81952 | tf_op jit(solution)/shard_map/ppermute | solution.py:464
  9.1 2.1 %collective-permute-start.3 = (bf16[240,512]{1,0:T(8,128)(2,1)S(1)}, bf16[240,512]{1,0:T(8,128)(2,1)S(1)}, u32[]{:S(2)}, u32[]{:S(2)}) collective-permute-start(bf16[240,512]{1,0:T(8,128)(2,1)S(1)} %constant_dynamic-update-slice_fusion.n0), channel_id=1, source_target_pairs={{0,16},{16,0},{32,48},{48,32},{64,80},{80,64},{96,112},{112,96},{1... | collective-permute-start | bytes 737288 | tf_op jit(solution)/shard_map/ppermute | solution.py:465
  11.2 3.1 %collective-permute-start.2 = (bf16[240,512]{1,0:T(8,128)(2,1)S(1)}, bf16[240,512]{1,0:T(8,128)(2,1)S(1)}, u32[]{:S(2)}, u32[]{:S(2)}) collective-permute-start(bf16[240,512]{1,0:T(8,128)(2,1)S(1)} %constant_dynamic-update-slice_fusion.n0), channel_id=1, source_target_pairs={{16,32},{32,16},{48,64},{64,48},{80,96},{96,80},{17,33},{33,17},{4... | collective-permute-start | bytes 737288 | tf_op jit(solution)/shard_map/ppermute | solution.py:464
  14.4 5.7 %shard_map.190 = (f32[2,2048,512]{2,1,0:T(8,128)S(1)}, s32[2,2048]{1,0:T(2,128)S(1)}, bf16[512,512]{1,0:T(8,128)(2,1)S(1)}) custom-call(s32[2]{0:T(128)S(1)} %pad_add_fusion.odd_ref, bf16[240,512]{1,0:T(8,128)(2,1)S(1)} %constant_dynamic-update-slice_fusion.n0, bf16[240,512]{1,0:T(8,128)(2,1)S(1)} %collective-permute-done.3.n1, s32[2,2048]{1,0:T(2,128)} %slots_ref.2, ...), custom_call_target="tpu_custom_call" | custom-call | tf_op jit(solution)/shard_map/pallas_call | solution.py:80
  20.2 5.9 %shard_map.191 = (bf16[240,512]{1,0:T(8,128)(2,1)S(1)}, bf16[240,512]{1,0:T(8,128)(2,1)S(1)}, bf16[240,512]{1,0:T(8,128)(2,1)S(1)}) custom-call(s32[2]{0:T(128)S(1)} %pad_add_fusion.odd_ref, bf16[240,512]{1,0:T(8,128)(2,1)S(1)} %collective-permute-done.2.n2, f32[2,2048,512]{2,1,0:T(8,128)S(1)} %get-tuple-element.27.v_ref, ...), custom_call_target="tpu_custom_call" | custom-call | tf_op jit(solution)/shard_map/pallas_call | solution.py:80
  26.2 3.6 %collective-permute-start.5 = (bf16[240,512]{1,0:T(8,128)(2,1)S(1)}, bf16[240,512]{1,0:T(8,128)(2,1)S(1)}, u32[]{:S(2)}, u32[]{:S(2)}) collective-permute-start(bf16[240,512]{1,0:T(8,128)(2,1)S(1)} %get-tuple-element.32), channel_id=1, source_target_pairs={{16,32},{32,16},{48,64},{64,48},{80,96},{96,80},{17,33},{33,17},{4... | collective-permute-start | bytes 737288 | tf_op jit(solution)/shard_map/ppermute | solution.py:464
  29.8 3.9 %collective-permute-done.5 = bf16[240,512]{1,0:T(8,128)(2,1)S(1)} collective-permute-done((bf16[240,512]{1,0:T(8,128)(2,1)S(1)}, bf16[240,512]{1,0:T(8,128)(2,1)S(1)}, u32[]{:S(2)}, u32[]{:S(2)}) %collective-permute-start.5) | collective-permute-done | bytes 245792 | tf_op jit(solution)/shard_map/ppermute | solution.py:464
  33.9 4.1 %collective-permute-start.7 = (bf16[80,512]{1,0:T(8,128)(2,1)S(1)}, bf16[80,512]{1,0:T(8,128)(2,1)S(1)}, u32[]{:S(2)}, u32[]{:S(2)}) collective-permute-start(bf16[80,512]{1,0:T(8,128)(2,1)S(1)} %get-tuple-element.49), channel_id=1, source_target_pairs={{1,2},{2,1},{3,4},{4,3},{5,6},{6,5},{7,8},{8,7},{9,10},{10,9},{11,... | collective-permute-start | bytes 245768 | tf_op jit(solution)/shard_map/ppermute | solution.py:464
  38.8 8.1 %all-to-all-start = ((s32[128,1,4]{2,1,0:T(1,128)}), s32[128,1,4]{2,1,0:T(1,128)S(1)}, u32[]{:S(2)}, u32[]{:S(2)}) async-start(s32[128,1,4]{2,1,0:T(1,128)} %bitcast.2), calls=%async_computation | async-start | bytes 131072 | tf_op jit(solution)/shard_map/all_to_all | solution.py:519
  48.6 6.7 %all-to-all-done = s32[128,1,4]{2,1,0:T(1,128)S(1)} async-done(((s32[128,1,4]{2,1,0:T(1,128)}), s32[128,1,4]{2,1,0:T(1,128)S(1)}, u32[]{:S(2)}, u32[]{:S(2)}) %all-to-all-start) | async-done | bytes 2080 | tf_op jit(solution)/shard_map/all_to_all | solution.py:519
  57.3 5.7 %all-to-all-start.1 = ((bf16[128,16,128]{2,1,0:T(8,128)(2,1)}), bf16[128,16,128]{2,1,0:T(8,128)(2,1)S(1)}, u32[]{:S(2)}, u32[]{:S(2)}) async-start(bf16[128,16,128]{2,1,0:T(8,128)(2,1)} %bitcast.4), calls=%async_computation.1 | async-start | bytes 1048576 | tf_op jit(solution)/shard_map/all_to_all | solution.py:532
  64.9 10.4 %all-to-all-done.1 = bf16[128,16,128]{2,1,0:T(8,128)(2,1)S(1)} async-done(((bf16[128,16,128]{2,1,0:T(8,128)(2,1)}), bf16[128,16,128]{2,1,0:T(8,128)(2,1)S(1)}, u32[]{:S(2)}, u32[]{:S(2)}) %all-to-all-start.1) | async-done | bytes 524320 | tf_op jit(solution)/shard_map/all_to_all | solution.py:532
  75.2 4.0 %shard_map.195 = (bf16[80,512]{1,0:T(8,128)(2,1)S(1)}, bf16[2048,128]{1,0:T(8,128)(2,1)}) custom-call(bf16[2048,128]{1,0:T(8,128)(2,1)S(1)} %bitcast.8, bf16[640,512]{1,0:T(8,128)(2,1)S(1)} %get-tuple-element.39.base_ref, f32[80,512]{1,0:T(8,128)S(1)} %get-tuple-element.40.self_ref, bf16[80,512]{1,0:T(8,128)(2,1)S(1)} %get-tuple-element.38.state_ref, ...), custom_call_target="tpu_custom_call" | custom-call | tf_op jit(solution)/shard_map/pallas_call | solution.py:80
  79.2 5.9 %all-to-all-start.2 = ((bf16[128,16,128]{2,1,0:T(8,128)(2,1)}), bf16[128,16,128]{2,1,0:T(8,128)(2,1)S(1)}, u32[]{:S(2)}, u32[]{:S(2)}) async-start(bf16[128,16,128]{2,1,0:T(8,128)(2,1)} %bitcast.6), calls=%async_computation.2 | async-start | bytes 1048576 | tf_op jit(solution)/shard_map/all_to_all | solution.py:532
  87.0 10.5 %all-to-all-done.2 = bf16[128,16,128]{2,1,0:T(8,128)(2,1)S(1)} async-done(((bf16[128,16,128]{2,1,0:T(8,128)(2,1)}), bf16[128,16,128]{2,1,0:T(8,128)(2,1)S(1)}, u32[]{:S(2)}, u32[]{:S(2)}) %all-to-all-start.2) | async-done | bytes 524320 | tf_op jit(solution)/shard_map/all_to_all | solution.py:532
  97.5 2.7 %shard_map.197 = bf16[80,512]{1,0:T(8,128)(2,1)S(1)} custom-call(bf16[2048,128]{1,0:T(8,128)(2,1)S(1)} %bitcast.9, bf16[640,512]{1,0:T(8,128)(2,1)S(1)} %get-tuple-element.43.base_ref, f32[80,512]{1,0:T(8,128)S(1)} %get-tuple-element.44.self_ref, bf16[80,512]{1,0:T(8,128)(2,1)S(1)} %get-tuple-element.42.state_ref, s32[1,640]{1,0:T(1,128)S(1)} %broadcast_in_dim.7.src_ref, ...), custom_call_target="tpu_custom_call" | custom-call | tf_op jit(solution)/shard_map/pallas_call | solution.py:80
  100.9 3.9 %collective-permute-start.9 = (bf16[80,512]{1,0:T(8,128)(2,1)S(1)}, bf16[80,512]{1,0:T(8,128)(2,1)S(1)}, u32[]{:S(2)}, u32[]{:S(2)}) collective-permute-start(bf16[80,512]{1,0:T(8,128)(2,1)S(1)} %shard_map.197), channel_id=1, source_target_pairs={{1,2},{2,1},{3,4},{4,3},{5,6},{6,5},{7,8},{8,7},{9,10},{10,9},{11,... | collective-permute-start | bytes 245768 | tf_op jit(solution)/shard_map/ppermute | solution.py:464
  104.8 3.4 %collective-permute-done.9 = bf16[80,512]{1,0:T(8,128)(2,1)S(1)} collective-permute-done((bf16[80,512]{1,0:T(8,128)(2,1)S(1)}, bf16[80,512]{1,0:T(8,128)(2,1)S(1)}, u32[]{:S(2)}, u32[]{:S(2)}) %collective-permute-start.9) | collective-permute-done | bytes 81952 | tf_op jit(solution)/shard_map/ppermute | solution.py:464
  108.2 2.9 %collective-permute-start.11 = (bf16[240,512]{1,0:T(8,128)(2,1)S(1)}, bf16[240,512]{1,0:T(8,128)(2,1)S(1)}, u32[]{:S(2)}, u32[]{:S(2)}) collective-permute-start(bf16[240,512]{1,0:T(8,128)(2,1)S(1)} %pad_maximum_fusion.n0), channel_id=1, source_target_pairs={{0,16},{16,0},{32,48},{48,32},{64,80},{80,64},{96,112},{112,96},{1... | collective-permute-start | bytes 737288 | tf_op jit(solution)/shard_map/ppermute | solution.py:465
  111.1 2.2 %collective-permute-start.10 = (bf16[240,512]{1,0:T(8,128)(2,1)S(1)}, bf16[240,512]{1,0:T(8,128)(2,1)S(1)}, u32[]{:S(2)}, u32[]{:S(2)}) collective-permute-start(bf16[240,512]{1,0:T(8,128)(2,1)S(1)} %pad_maximum_fusion.n0), channel_id=1, source_target_pairs={{16,32},{32,16},{48,64},{64,48},{80,96},{96,80},{17,33},{33,17},{4... | collective-permute-start | bytes 737288 | tf_op jit(solution)/shard_map/ppermute | solution.py:464
  113.3 3.8 %receiver.1.r_ref = bf16[2048,512]{1,0:T(8,128)(2,1)} custom-call(bf16[2048,512]{1,0:T(8,128)(2,1)} %grid_ref.5, bf16[512,512]{1,0:T(8,128)(2,1)} %w_ref.1), custom_call_target="tpu_custom_call" | custom-call | tf_op jit(solution)/shard_map/receiver/pallas_call | solution.py:104
  117.1 5.6 %shard_map.198 = (f32[3,2048,512]{2,1,0:T(8,128)S(1)}, s32[3,2048]{1,0:T(4,128)S(1)}, bf16[512,512]{1,0:T(8,128)(2,1)S(1)}, bf16[2048,512]{1,0:T(8,128)(2,1)S(1)}) custom-call(s32[2]{0:T(128)S(1)} %pad_add_fusion.odd_ref, bf16[240,512]{1,0:T(8,128)(2,1)S(1)} %pad_maximum_fusion.n0, bf16[240,512]{1,0:T(8,128)(2,1)S(1)} %collective-permute-done.11.n1, ...), custom_call_target="tpu_custom_call" | custom-call | tf_op jit(solution)/shard_map/pallas_call | solution.py:80
  122.7 7.3 %decode_far.1 = bf16[2048,512]{1,0:T(8,128)(2,1)} custom-call(s32[2]{0:T(128)S(1)} %pad_add_fusion.odd_ref, bf16[240,512]{1,0:T(8,128)(2,1)S(1)} %collective-permute-done.10.n2, f32[3,2048,512]{2,1,0:T(8,128)S(1)} %get-tuple-element.45.v, s32[3,2048]{1,0:T(4,128)S(1)} %get-tuple-element.46.slots, bf16[512,512]{1,0:T(8,128)(2,1)S(1)} %get-tuple-element.47.w, ...), custom_call_target="tpu_custom_call" | custom-call | tf_op jit(solution)/shard_map/decode_far/pallas_call | solution.py:441
  (34 shorter events, 11.6 us)
Async XLA Ops:
  0.0 6.7 %collective-permute-start = (bf16[80,512]{1,0:T(8,128)(2,1)}, bf16[80,512]{1,0:T(8,128)(2,1)S(1)}, u32[]{:S(2)}, u32[]{:S(2)}) collective-permute-start(bf16[80,512]{1,0:T(8,128)(2,1)} %mesh_ref.1), channel_id=1, source_target_pairs={{0,1},{1,0},{2,3},{3,2},{4,5},{5,4},{6,7},{7,6},{8,9},{9,8},{10,11... | collective-permute-start | bytes 245768 | tf_op jit(solution)/shard_map/ppermute | solution.py:465
  1.6 7.5 %collective-permute-start.1 = (bf16[80,512]{1,0:T(8,128)(2,1)}, bf16[80,512]{1,0:T(8,128)(2,1)S(1)}, u32[]{:S(2)}, u32[]{:S(2)}) collective-permute-start(bf16[80,512]{1,0:T(8,128)(2,1)} %mesh_ref.1), channel_id=1, source_target_pairs={{1,2},{2,1},{3,4},{4,3},{5,6},{6,5},{7,8},{8,7},{9,10},{10,9},{11,... | collective-permute-start | bytes 245768 | tf_op jit(solution)/shard_map/ppermute | solution.py:464
  9.1 5.3 %collective-permute-start.3 = (bf16[240,512]{1,0:T(8,128)(2,1)S(1)}, bf16[240,512]{1,0:T(8,128)(2,1)S(1)}, u32[]{:S(2)}, u32[]{:S(2)}) collective-permute-start(bf16[240,512]{1,0:T(8,128)(2,1)S(1)} %constant_dynamic-update-slice_fusion.n0), channel_id=1, source_target_pairs={{0,16},{16,0},{32,48},{48,32},{64,80},{80,64},{96,112},{112,96},{1... | collective-permute-start | bytes 737288 | tf_op jit(solution)/shard_map/ppermute | solution.py:465
  11.2 9.0 %collective-permute-start.2 = (bf16[240,512]{1,0:T(8,128)(2,1)S(1)}, bf16[240,512]{1,0:T(8,128)(2,1)S(1)}, u32[]{:S(2)}, u32[]{:S(2)}) collective-permute-start(bf16[240,512]{1,0:T(8,128)(2,1)S(1)} %constant_dynamic-update-slice_fusion.n0), channel_id=1, source_target_pairs={{16,32},{32,16},{48,64},{64,48},{80,96},{96,80},{17,33},{33,17},{4... | collective-permute-start | bytes 737288 | tf_op jit(solution)/shard_map/ppermute | solution.py:464
  20.2 17.9 %copy-start.3 = (s32[1,128,4]{1,2,0:T(4,128)S(1)}, s32[1,128,4]{1,2,0:T(4,128)}, u32[]{:S(2)}) copy-start(s32[1,128,4]{1,2,0:T(4,128)} %param.24) | copy-start | bytes 6148
  20.2 26.8 %copy-start = (bf16[80,512]{1,0:T(8,128)(2,1)S(1)}, bf16[80,512]{1,0:T(8,128)(2,1)}, u32[]{:S(2)}) copy-start(bf16[80,512]{1,0:T(8,128)(2,1)} %mesh_ref.1) | copy-start | bytes 245764
  26.1 3.7 %collective-permute-start.4 = (bf16[240,512]{1,0:T(8,128)(2,1)S(1)}, bf16[240,512]{1,0:T(8,128)(2,1)S(1)}, u32[]{:S(2)}, u32[]{:S(2)}) collective-permute-start(bf16[240,512]{1,0:T(8,128)(2,1)S(1)} %get-tuple-element.31), channel_id=1, source_target_pairs={{0,16},{16,0},{32,48},{48,32},{64,80},{80,64},{96,112},{112,96},{1... | collective-permute-start | bytes 737288 | tf_op jit(solution)/shard_map/ppermute | solution.py:465
  26.2 7.5 %collective-permute-start.5 = (bf16[240,512]{1,0:T(8,128)(2,1)S(1)}, bf16[240,512]{1,0:T(8,128)(2,1)S(1)}, u32[]{:S(2)}, u32[]{:S(2)}) collective-permute-start(bf16[240,512]{1,0:T(8,128)(2,1)S(1)} %get-tuple-element.32), channel_id=1, source_target_pairs={{16,32},{32,16},{48,64},{64,48},{80,96},{96,80},{17,33},{33,17},{4... | collective-permute-start | bytes 737288 | tf_op jit(solution)/shard_map/ppermute | solution.py:464
  33.8 21.4 %collective-permute-start.6 = (bf16[80,512]{1,0:T(8,128)(2,1)S(1)}, bf16[80,512]{1,0:T(8,128)(2,1)S(1)}, u32[]{:S(2)}, u32[]{:S(2)}) collective-permute-start(bf16[80,512]{1,0:T(8,128)(2,1)S(1)} %get-tuple-element.50), channel_id=1, source_target_pairs={{0,1},{1,0},{2,3},{3,2},{4,5},{5,4},{6,7},{7,6},{8,9},{9,8},{10,11... | collective-permute-start | bytes 245768 | tf_op jit(solution)/shard_map/ppermute | solution.py:465
  33.9 21.3 %collective-permute-start.7 = (bf16[80,512]{1,0:T(8,128)(2,1)S(1)}, bf16[80,512]{1,0:T(8,128)(2,1)S(1)}, u32[]{:S(2)}, u32[]{:S(2)}) collective-permute-start(bf16[80,512]{1,0:T(8,128)(2,1)S(1)} %get-tuple-element.49), channel_id=1, source_target_pairs={{1,2},{2,1},{3,4},{4,3},{5,6},{6,5},{7,8},{8,7},{9,10},{10,9},{11,... | collective-permute-start | bytes 245768 | tf_op jit(solution)/shard_map/ppermute | solution.py:464
  38.8 16.4 %all-to-all-start = ((s32[128,1,4]{2,1,0:T(1,128)}), s32[128,1,4]{2,1,0:T(1,128)S(1)}, u32[]{:S(2)}, u32[]{:S(2)}) async-start(s32[128,1,4]{2,1,0:T(1,128)} %bitcast.2), calls=%async_computation | async-start | bytes 131072 | tf_op jit(solution)/shard_map/all_to_all | solution.py:519
  48.5 14.5 %copy-start.1 = (s32[640]{0:T(1024)S(1)}, s32[640]{0:T(1024)}, u32[]{:S(2)}) copy-start(s32[640]{0:T(1024)} %param.26) | copy-start | bytes 7684
  48.6 14.5 %copy-start.2 = (s32[640]{0:T(1024)S(1)}, s32[640]{0:T(1024)}, u32[]{:S(2)}) copy-start(s32[640]{0:T(1024)} %param.25) | copy-start | bytes 7684
  57.3 18.0 %all-to-all-start.1 = ((bf16[128,16,128]{2,1,0:T(8,128)(2,1)}), bf16[128,16,128]{2,1,0:T(8,128)(2,1)S(1)}, u32[]{:S(2)}, u32[]{:S(2)}) async-start(bf16[128,16,128]{2,1,0:T(8,128)(2,1)} %bitcast.4), calls=%async_computation.1 | async-start | bytes 1048576 | tf_op jit(solution)/shard_map/all_to_all | solution.py:532
  79.2 18.2 %all-to-all-start.2 = ((bf16[128,16,128]{2,1,0:T(8,128)(2,1)}), bf16[128,16,128]{2,1,0:T(8,128)(2,1)S(1)}, u32[]{:S(2)}, u32[]{:S(2)}) async-start(bf16[128,16,128]{2,1,0:T(8,128)(2,1)} %bitcast.6), calls=%async_computation.2 | async-start | bytes 1048576 | tf_op jit(solution)/shard_map/all_to_all | solution.py:532
  100.2 4.6 %collective-permute-start.8 = (bf16[80,512]{1,0:T(8,128)(2,1)S(1)}, bf16[80,512]{1,0:T(8,128)(2,1)S(1)}, u32[]{:S(2)}, u32[]{:S(2)}) collective-permute-start(bf16[80,512]{1,0:T(8,128)(2,1)S(1)} %shard_map.197), channel_id=1, source_target_pairs={{0,1},{1,0},{2,3},{3,2},{4,5},{5,4},{6,7},{7,6},{8,9},{9,8},{10,11... | collective-permute-start | bytes 245768 | tf_op jit(solution)/shard_map/ppermute | solution.py:465
  100.9 7.3 %collective-permute-start.9 = (bf16[80,512]{1,0:T(8,128)(2,1)S(1)}, bf16[80,512]{1,0:T(8,128)(2,1)S(1)}, u32[]{:S(2)}, u32[]{:S(2)}) collective-permute-start(bf16[80,512]{1,0:T(8,128)(2,1)S(1)} %shard_map.197), channel_id=1, source_target_pairs={{1,2},{2,1},{3,4},{4,3},{5,6},{6,5},{7,8},{8,7},{9,10},{10,9},{11,... | collective-permute-start | bytes 245768 | tf_op jit(solution)/shard_map/ppermute | solution.py:464
  108.2 8.9 %collective-permute-start.11 = (bf16[240,512]{1,0:T(8,128)(2,1)S(1)}, bf16[240,512]{1,0:T(8,128)(2,1)S(1)}, u32[]{:S(2)}, u32[]{:S(2)}) collective-permute-start(bf16[240,512]{1,0:T(8,128)(2,1)S(1)} %pad_maximum_fusion.n0), channel_id=1, source_target_pairs={{0,16},{16,0},{32,48},{48,32},{64,80},{80,64},{96,112},{112,96},{1... | collective-permute-start | bytes 737288 | tf_op jit(solution)/shard_map/ppermute | solution.py:465
  111.1 11.5 %collective-permute-start.10 = (bf16[240,512]{1,0:T(8,128)(2,1)S(1)}, bf16[240,512]{1,0:T(8,128)(2,1)S(1)}, u32[]{:S(2)}, u32[]{:S(2)}) collective-permute-start(bf16[240,512]{1,0:T(8,128)(2,1)S(1)} %pad_maximum_fusion.n0), channel_id=1, source_target_pairs={{16,32},{32,16},{48,64},{64,48},{80,96},{96,80},{17,33},{33,17},{4... | collective-permute-start | bytes 737288 | tf_op jit(solution)/shard_map/ppermute | solution.py:464

commit v5 on v4

--- a/solution.py
+++ b/solution.py
@@ -33,6 +33,7 @@
 
 
 def silu_of_half(half):
+    half = bf(half)
     return half + half * jnp.tanh(half)
 
 
@@ -199,7 +200,7 @@
         for f in range(ENC_FAN):
             chosen = hot_rows(slots_ref[f : f + 1, part] - start, near.shape[0])
             v = dot(chosen, near[...]) + v_ref[f, part]
-            hid[f * rows : (f + 1) * rows] = bf(silu_of_half(v))
+            hid[f * rows : (f + 1) * rows] = silu_of_half(v)
         chosen = jnp.concatenate(
             [hot_columns(slots_ref[f : f + 1, part], slots) for f in range(ENC_FAN)], axis=1
         )
@@ -257,12 +258,14 @@
     return jnp.concatenate([rows, jnp.zeros((extra, rows.shape[1]), rows.dtype)], axis=0)
 
 
-def stage_kernel(mesh, wo, wm, wself, ws, wo_out, wm_out, ws_out, self_ref, w, sems):
-    copies = fetch([(wself, w), (wo, wo_out), (wm, wm_out), (ws.at[0], ws_out)], sems)
+def stage_kernel(mesh, wo, wm, wself, ws, wom_out, ws_out, self_ref, w, sems):
+    copies = fetch([(wself, w.at[0]), (wo, w.at[1]), (wm, w.at[2]), (ws.at[0], ws_out)], sems)
     copies[0].wait()
-    self_ref[...] = dot(mesh[...], w[...])
-    for copy in copies[1:]:
-        copy.wait()
+    self_ref[...] = dot(mesh[...], w[0])
+    copies[1].wait()
+    copies[2].wait()
+    wom_out[...] = bf(dot(w[1], w[2]))
+    copies[3].wait()
 
 
 def stage(mesh, wo, wm, wself, ws):
@@ -270,18 +273,17 @@
     return on_chip(
         stage_kernel,
         [mesh],
-        [((d, d), jnp.bfloat16)] * 3 + [((rows, d), jnp.float32)],
+        [((d, d), jnp.bfloat16)] * 2 + [((rows, d), jnp.float32)],
         far=[wo, wm, wself, ws],
-        scratch=[pltpu.VMEM((d, d), jnp.bfloat16), pltpu.SemaphoreType.DMA((4,))],
+        scratch=[pltpu.VMEM((3, d, d), jnp.bfloat16), pltpu.SemaphoreType.DMA((4,))],
     )
 
 
 def merge_kernel(
-    o_ref, a_ref, b_ref, mesh_ref, asked_ref, wo, wm, ws, self_ref, state_ref, out_ref, wide
+    o_ref, a_ref, b_ref, mesh_ref, asked_ref, wom, ws, self_ref, state_ref, out_ref, wide
 ):
     total = o_ref[...] + a_ref[...].astype(jnp.float32) + b_ref[...].astype(jnp.float32)
-    summed = bf(dot(bf(total), wo[...]))
-    update = dot(summed, wm[...]) + self_ref[...]
+    update = dot(bf(total), wom[...]) + self_ref[...]
     state = bf(mesh_ref[...].astype(jnp.float32) + norm(silu(update)))
     state_ref[...] = state
     pack(dot(state, ws[...]), asked_ref, wide, out_ref)
@@ -297,8 +299,11 @@
     )
 
 
-def ready_kernel(depth, state_ref, tgt_ref, wr, wself, base_ref, self_ref, w, sems):
-    copies = fetch([(wr.at[depth], w.at[0]), (wself.at[depth], w.at[1])], sems)
+def ready_kernel(
+    depth, last, state_ref, tgt_ref, wr, wself, wo, wm, wn, base_ref, self_ref, wom, wn_out, w, sems
+):
+    pairs = [(x.at[depth], w.at[i]) for i, x in enumerate((wr, wself, wo, wm))]
+    copies = fetch(pairs + [(wn if last else wn.at[depth + 1], wn_out)], sems)
     state = state_ref[...]
     chosen = hot_rows(tgt_ref[...], up128(state.shape[0]))
     copies[0].wait()
@@ -306,59 +311,51 @@
     base_ref[...] = bf(dot(chosen, received))
     copies[1].wait()
     self_ref[...] = dot(state, w[1])
-
-
-def ready(depth, state, tgt, wr, wself):
+    copies[2].wait()
+    copies[3].wait()
+    wom[...] = bf(dot(w[2], w[3]))
+    copies[4].wait()
+
+
+def ready(depth, last, state, tgt, wr, wself, wo, wm, wn):
     rows, d = state.shape
     return on_chip(
-        functools.partial(ready_kernel, depth),
+        functools.partial(ready_kernel, depth, last),
         [state, tgt],
-        [((tgt.shape[1], d), jnp.bfloat16), ((rows, d), jnp.float32)],
-        far=[wr, wself],
-        scratch=[pltpu.VMEM((2, d, d), jnp.bfloat16), pltpu.SemaphoreType.DMA((2,))],
+        [((tgt.shape[1], d), jnp.bfloat16), ((rows, d), jnp.float32)]
+        + [((d, d), jnp.bfloat16)] * 2,
+        far=[wr, wself, wo, wm, wn],
+        scratch=[pltpu.VMEM((4, d, d), jnp.bfloat16), pltpu.SemaphoreType.DMA((5,))],
     )
 
 
 def layer_kernel(
-    depth, last, in_ref, base_ref, self_ref, state_ref, src_ref, tgt_ref, asked_ref, *rest
+    last, in_ref, base_ref, self_ref, wom, wn, state_ref, src_ref, tgt_ref, asked_ref, *rest
 ):
-    wo, wm, wn = rest[:3]
-    outs, (wide, w, sems) = rest[3:-3], rest[-3:]
-    after = wn if last else wn.at[depth + 1]
-    copies = fetch([(wo.at[depth], w.at[0]), (wm.at[depth], w.at[1]), (after, w.at[2])], sems)
+    outs, wide = rest[:-1], rest[-1]
     owned, d = state_ref.shape
     incoming = unpack(in_ref, wide, d)
     v = dot(hot_rows(src_ref[...], incoming.shape[0]), incoming)
     hidden = bf(silu(v + base_ref[...].astype(jnp.float32)))
     gathered = dot(hot_columns(tgt_ref[...], owned), hidden)
-    copies[0].wait()
-    summed = bf(dot(bf(gathered), w[0]))
-    copies[1].wait()
-    update = dot(summed, w[1]) + self_ref[...]
+    update = dot(bf(gathered), wom[...]) + self_ref[...]
     new = bf(state_ref[...].astype(jnp.float32) + norm(silu(update)))
-    copies[2].wait()
     if last:
-        outs[0][...] = bf(dot(new, w[2]) * 0.5)
+        outs[0][...] = bf(dot(new, wn[...]) * 0.5)
     else:
         outs[0][...] = new
-        pack(dot(new, w[2]), asked_ref, wide, outs[1])
-
-
-def layer(depth, last, incoming, base, own, state, src, tgt, asked, wo, wm, wn):
+        pack(dot(new, wn[...]), asked_ref, wide, outs[1])
+
+
+def layer(last, incoming, prepared, state, src, tgt, asked):
     out = [(state.shape, jnp.bfloat16)]
     if not last:
         out.append((incoming.shape, jnp.bfloat16))
-    d = state.shape[1]
-    return on_chip(
-        functools.partial(layer_kernel, depth, last),
-        [incoming, base, own, state, src, tgt, asked],
+    return on_chip(
+        functools.partial(layer_kernel, last),
+        [incoming, *prepared, state, src, tgt, asked],
         out,
-        far=[wo, wm, wn],
-        scratch=[
-            pltpu.VMEM(incoming.shape, jnp.float32),
-            pltpu.VMEM((3, d, d), jnp.bfloat16),
-            pltpu.SemaphoreType.DMA((3,)),
-        ],
+        scratch=[pltpu.VMEM(incoming.shape, jnp.float32)],
     )
 
 
@@ -405,7 +402,7 @@
         total = None
         for f in range(DEC_FAN):
             chosen = hot_rows(slots[f : f + 1, part] - start, near.shape[0])
-            h = silu_of_half(dot(chosen, near[...]) + v[f, part, :])
+            h = silu_of_half(dot(chosen, near[...]) + v[f, part, :]).astype(jnp.float32)
             total = h if total is None else total + h
         update = dot(bf(total), w[...])
         out_ref[at : at + FAR_PART] = bf(g[part, :].astype(jnp.float32) + norm(update))
@@ -512,14 +509,13 @@
     decoder_output,
 ):
     owned = mesh_latent.shape[0]
-    wanted = peer_rows[0]
-    tiles = wanted.shape[0]
+    tiles = peer_rows.shape[1]
     odd = jnp.stack([lax.axis_index("lat") % 2, lax.axis_index("lon") % 2]).astype(jnp.int32)
     near = neighbours(mesh_latent)
-    asked = lax.all_to_all(wanted, ("lat", "lon"), split_axis=0, concat_axis=0, tiled=True)
     prepared = encode_near(
         odd, grid_latent, encoder_slots, near[:2], encoder_receiver, encoder_sender
     )
+    asked = lax.all_to_all(peer_rows[0], ("lat", "lon"), split_axis=0, concat_axis=0, tiled=True)
     sums = encode_far(odd, near[2], prepared)
     own, a, b = to_owners(sums, owned)
     staged = stage(mesh_latent, encoder_output, encoder_merge, encoder_self, process_sender)
@@ -536,21 +532,18 @@
             concat_axis=0,
             tiled=True,
         ).reshape(outgoing.shape)
-        base, self_part = ready(depth, state, tgt, process_receiver, process_self)
-        result = layer(
+        prepared = ready(
             depth,
             last,
-            incoming,
-            base,
-            self_part,
             state,
-            src,
             tgt,
-            asked,
+            process_receiver,
+            process_self,
             process_output,
             process_merge,
             decoder_sender if last else process_sender,
         )
+        result = layer(last, incoming, prepared, state, src, tgt, asked)
         if not last:
             state, outgoing = result
     near = neighbours(result[0])

time: 130 us -> 127 us (0.977)
  Pallas kernels: 42.2 us -> 39.8 us
    pallas_call x9, Pallas kernels: 31.1 us -> 29.2 us  [on_chip(): pl.pallas_call(kernel, in_specs=specs, out_specs=[VMEM] * len(outs), out_...]
  transfers between devices with their start and end apart: 15 -> 15, of which waited for: 6 -> 6; matrix products, arithmetic and copies ran while one was open for 1% -> 1% of each run, Pallas kernels for 16% -> 17%
where the time goes in v5:
time: 127 us; the launch traced here: 126 us
  starting transfers between devices  48.3 us (38%)
  Pallas kernels  39.8 us (31%)
  waiting for transfers between devices  36.1 us (28%)
  local copies, waits for them, and re-layouts  1.69 us (1%)
    pallas_call x9, Pallas kernels, on_chip(): pl.pallas_call(kernel, in_specs=specs, out_specs=[VMEM] * len(outs), out_...  29.2 us
    ppermute x6, starting transfers between devices, swap_both(): b = lax.ppermute(to_second, axis, second)  21 us
    all_to_all x2, waiting for transfers between devices, body(): lax.all_to_all(outgoing.reshape(tiles, -1, 128), ('lat', 'lon'), split_ax...  19.9 us
    all_to_all x2, starting transfers between devices, body(): lax.all_to_all(outgoing.reshape(tiles, -1, 128), ('lat', 'lon'), split_ax...  11.7 us
    ppermute x6, waiting for transfers between devices, swap_both(): b = lax.ppermute(to_second, axis, second)  9.75 us
    all_to_all x1, starting transfers between devices, body(): lax.all_to_all(peer_rows[0], ('lat', 'lon'), split_axis=0, concat_axis=0,...  8.14 us
    ppermute x6, starting transfers between devices, swap_both(): a = lax.ppermute(to_first, axis, first)  7.53 us
    pallas_call x1, Pallas kernels, decode_far(): pl.pallas_call(dec_far_kernel, grid=(n // FAR_ROWS,), in_specs=[pl.BlockS...  6.87 us
  transfers between devices with their start and end apart: 15, of which 6 were waited for; matrix products, arithmetic and copies ran while one was open for 1% of the time, Pallas kernels for 17%

profile of v5, /device:TPU:3, one launch (start us, length us, event | category | flops | bytes accessed | tf_op | source)
XLA Modules:
  0.0 126.4 jit_solution(5555249343823000464)
XLA Ops:
  1.6 4.1 %collective-permute-start.1 = (bf16[80,512]{1,0:T(8,128)(2,1)}, bf16[80,512]{1,0:T(8,128)(2,1)S(1)}, u32[]{:S(2)}, u32[]{:S(2)}) collective-permute-start(bf16[80,512]{1,0:T(8,128)(2,1)} %mesh_ref.1), channel_id=1, source_target_pairs={{1,2},{2,1},{3,4},{4,3},{5,6},{6,5},{7,8},{8,7},{9,10},{10,9},{11,... | collective-permute-start | bytes 245768 | tf_op jit(solution)/shard_map/ppermute | solution.py:461
  6.7 2.4 %collective-permute-done.1 = bf16[80,512]{1,0:T(8,128)(2,1)S(1)} collective-permute-done((bf16[80,512]{1,0:T(8,128)(2,1)}, bf16[80,512]{1,0:T(8,128)(2,1)S(1)}, u32[]{:S(2)}, u32[]{:S(2)}) %collective-permute-start.1) | collective-permute-done | bytes 81952 | tf_op jit(solution)/shard_map/ppermute | solution.py:461
  11.2 3.1 %collective-permute-start.2 = (bf16[240,512]{1,0:T(8,128)(2,1)S(1)}, bf16[240,512]{1,0:T(8,128)(2,1)S(1)}, u32[]{:S(2)}, u32[]{:S(2)}) collective-permute-start(bf16[240,512]{1,0:T(8,128)(2,1)S(1)} %constant_dynamic-update-slice_fusion.n0), channel_id=1, source_target_pairs={{16,32},{32,16},{48,64},{64,48},{80,96},{96,80},{17,33},{33,17},{4... | collective-permute-start | bytes 737288 | tf_op jit(solution)/shard_map/ppermute | solution.py:461
  14.4 5.7 %shard_map.190 = (f32[2,2048,512]{2,1,0:T(8,128)S(1)}, s32[2,2048]{1,0:T(2,128)S(1)}, bf16[512,512]{1,0:T(8,128)(2,1)S(1)}) custom-call(s32[2]{0:T(128)S(1)} %pad_add_fusion.odd_ref, bf16[240,512]{1,0:T(8,128)(2,1)S(1)} %constant_dynamic-update-slice_fusion.n0, bf16[240,512]{1,0:T(8,128)(2,1)S(1)} %collective-permute-done.3.n1, s32[2,2048]{1,0:T(2,128)} %slots_ref.2, ...), custom_call_target="tpu_custom_call" | custom-call | tf_op jit(solution)/shard_map/pallas_call | solution.py:81
  20.2 5.4 %shard_map.191 = (bf16[240,512]{1,0:T(8,128)(2,1)S(1)}, bf16[240,512]{1,0:T(8,128)(2,1)S(1)}, bf16[240,512]{1,0:T(8,128)(2,1)S(1)}) custom-call(s32[2]{0:T(128)S(1)} %pad_add_fusion.odd_ref, bf16[240,512]{1,0:T(8,128)(2,1)S(1)} %collective-permute-done.2.n2, f32[2,2048,512]{2,1,0:T(8,128)S(1)} %get-tuple-element.30.v_ref, ...), custom_call_target="tpu_custom_call" | custom-call | tf_op jit(solution)/shard_map/pallas_call | solution.py:81
  25.8 3.6 %collective-permute-start.5 = (bf16[240,512]{1,0:T(8,128)(2,1)S(1)}, bf16[240,512]{1,0:T(8,128)(2,1)S(1)}, u32[]{:S(2)}, u32[]{:S(2)}) collective-permute-start(bf16[240,512]{1,0:T(8,128)(2,1)S(1)} %get-tuple-element.35), channel_id=1, source_target_pairs={{16,32},{32,16},{48,64},{64,48},{80,96},{96,80},{17,33},{33,17},{4... | collective-permute-start | bytes 737288 | tf_op jit(solution)/shard_map/ppermute | solution.py:461
  29.4 3.9 %collective-permute-done.5 = bf16[240,512]{1,0:T(8,128)(2,1)S(1)} collective-permute-done((bf16[240,512]{1,0:T(8,128)(2,1)S(1)}, bf16[240,512]{1,0:T(8,128)(2,1)S(1)}, u32[]{:S(2)}, u32[]{:S(2)}) %collective-permute-start.5) | collective-permute-done | bytes 245792 | tf_op jit(solution)/shard_map/ppermute | solution.py:461
  33.5 4.1 %collective-permute-start.7 = (bf16[80,512]{1,0:T(8,128)(2,1)S(1)}, bf16[80,512]{1,0:T(8,128)(2,1)S(1)}, u32[]{:S(2)}, u32[]{:S(2)}) collective-permute-start(bf16[80,512]{1,0:T(8,128)(2,1)S(1)} %get-tuple-element.55), channel_id=1, source_target_pairs={{1,2},{2,1},{3,4},{4,3},{5,6},{6,5},{7,8},{8,7},{9,10},{10,9},{11,... | collective-permute-start | bytes 245768 | tf_op jit(solution)/shard_map/ppermute | solution.py:461
  38.3 8.1 %all-to-all-start = ((s32[128,1,4]{2,1,0:T(1,128)}), s32[128,1,4]{2,1,0:T(1,128)S(1)}, u32[]{:S(2)}, u32[]{:S(2)}) async-start(s32[128,1,4]{2,1,0:T(1,128)} %bitcast.2), calls=%async_computation | async-start | bytes 131072 | tf_op jit(solution)/shard_map/all_to_all | solution.py:518
  48.4 6.4 %all-to-all-done = s32[128,1,4]{2,1,0:T(1,128)S(1)} async-done(((s32[128,1,4]{2,1,0:T(1,128)}), s32[128,1,4]{2,1,0:T(1,128)S(1)}, u32[]{:S(2)}, u32[]{:S(2)}) %all-to-all-start) | async-done | bytes 2080 | tf_op jit(solution)/shard_map/all_to_all | solution.py:518
  56.6 5.7 %all-to-all-start.1 = ((bf16[128,16,128]{2,1,0:T(8,128)(2,1)}), bf16[128,16,128]{2,1,0:T(8,128)(2,1)S(1)}, u32[]{:S(2)}, u32[]{:S(2)}) async-start(bf16[128,16,128]{2,1,0:T(8,128)(2,1)} %bitcast.4), calls=%async_computation.1 | async-start | bytes 1048576 | tf_op jit(solution)/shard_map/all_to_all | solution.py:528
  62.4 2.3 %shard_map.194 = (bf16[640,512]{1,0:T(8,128)(2,1)S(1)}, f32[80,512]{1,0:T(8,128)S(1)}, bf16[512,512]{1,0:T(8,128)(2,1)S(1)}, bf16[512,512]{1,0:T(8,128)(2,1)S(1)}) custom-call(bf16[80,512]{1,0:T(8,128)(2,1)S(1)} %get-tuple-element.40.state_ref, s32[1,640]{1,0:T(1,128)S(1)} %broadcast_in_dim.6.tgt_ref, bf16[2,512,512]{2,1,0:T(8,128)(2,1)} %wr.3, ...), custom_call_target="tpu_custom_call" | custom-call | tf_op jit(solution)/shard_map/pallas_call | solution.py:81
  64.7 9.9 %all-to-all-done.1 = bf16[128,16,128]{2,1,0:T(8,128)(2,1)S(1)} async-done(((bf16[128,16,128]{2,1,0:T(8,128)(2,1)}), bf16[128,16,128]{2,1,0:T(8,128)(2,1)S(1)}, u32[]{:S(2)}, u32[]{:S(2)}) %all-to-all-start.1) | async-done | bytes 524320 | tf_op jit(solution)/shard_map/all_to_all | solution.py:528
  74.6 2.7 %shard_map.195 = (bf16[80,512]{1,0:T(8,128)(2,1)S(1)}, bf16[2048,128]{1,0:T(8,128)(2,1)}) custom-call(bf16[2048,128]{1,0:T(8,128)(2,1)S(1)} %bitcast.9, bf16[640,512]{1,0:T(8,128)(2,1)S(1)} %get-tuple-element.41.base_ref, f32[80,512]{1,0:T(8,128)S(1)} %get-tuple-element.42.self_ref, bf16[512,512]{1,0:T(8,128)(2,1)S(1)} %get-tuple-element.43.wom, ...), custom_call_target="tpu_custom_call" | custom-call | tf_op jit(solution)/shard_map/pallas_call | solution.py:81
  77.3 5.9 %all-to-all-start.2 = ((bf16[128,16,128]{2,1,0:T(8,128)(2,1)}), bf16[128,16,128]{2,1,0:T(8,128)(2,1)S(1)}, u32[]{:S(2)}, u32[]{:S(2)}) async-start(bf16[128,16,128]{2,1,0:T(8,128)(2,1)} %bitcast.6), calls=%async_computation.2 | async-start | bytes 1048576 | tf_op jit(solution)/shard_map/all_to_all | solution.py:528
  83.3 2.3 %shard_map.196 = (bf16[640,512]{1,0:T(8,128)(2,1)S(1)}, f32[80,512]{1,0:T(8,128)S(1)}, bf16[512,512]{1,0:T(8,128)(2,1)S(1)}, bf16[512,512]{1,0:T(8,128)(2,1)S(1)}) custom-call(bf16[80,512]{1,0:T(8,128)(2,1)S(1)} %get-tuple-element.46.state_ref, s32[1,640]{1,0:T(1,128)S(1)} %broadcast_in_dim.6.tgt_ref, bf16[2,512,512]{2,1,0:T(8,128)(2,1)} %wr.3, ...), custom_call_target="tpu_custom_call" | custom-call | tf_op jit(solution)/shard_map/pallas_call | solution.py:81
  85.5 10.0 %all-to-all-done.2 = bf16[128,16,128]{2,1,0:T(8,128)(2,1)S(1)} async-done(((bf16[128,16,128]{2,1,0:T(8,128)(2,1)}), bf16[128,16,128]{2,1,0:T(8,128)(2,1)S(1)}, u32[]{:S(2)}, u32[]{:S(2)}) %all-to-all-start.2) | async-done | bytes 524320 | tf_op jit(solution)/shard_map/all_to_all | solution.py:528
  97.7 3.9 %collective-permute-start.9 = (bf16[80,512]{1,0:T(8,128)(2,1)S(1)}, bf16[80,512]{1,0:T(8,128)(2,1)S(1)}, u32[]{:S(2)}, u32[]{:S(2)}) collective-permute-start(bf16[80,512]{1,0:T(8,128)(2,1)S(1)} %shard_map.197), channel_id=1, source_target_pairs={{1,2},{2,1},{3,4},{4,3},{5,6},{6,5},{7,8},{8,7},{9,10},{10,9},{11,... | collective-permute-start | bytes 245768 | tf_op jit(solution)/shard_map/ppermute | solution.py:461
  101.6 3.4 %collective-permute-done.9 = bf16[80,512]{1,0:T(8,128)(2,1)S(1)} collective-permute-done((bf16[80,512]{1,0:T(8,128)(2,1)S(1)}, bf16[80,512]{1,0:T(8,128)(2,1)S(1)}, u32[]{:S(2)}, u32[]{:S(2)}) %collective-permute-start.9) | collective-permute-done | bytes 81952 | tf_op jit(solution)/shard_map/ppermute | solution.py:461
  105.0 2.9 %collective-permute-start.11 = (bf16[240,512]{1,0:T(8,128)(2,1)S(1)}, bf16[240,512]{1,0:T(8,128)(2,1)S(1)}, u32[]{:S(2)}, u32[]{:S(2)}) collective-permute-start(bf16[240,512]{1,0:T(8,128)(2,1)S(1)} %pad_maximum_fusion.n0), channel_id=1, source_target_pairs={{0,16},{16,0},{32,48},{48,32},{64,80},{80,64},{96,112},{112,96},{1... | collective-permute-start | bytes 737288 | tf_op jit(solution)/shard_map/ppermute | solution.py:462
  107.9 2.2 %collective-permute-start.10 = (bf16[240,512]{1,0:T(8,128)(2,1)S(1)}, bf16[240,512]{1,0:T(8,128)(2,1)S(1)}, u32[]{:S(2)}, u32[]{:S(2)}) collective-permute-start(bf16[240,512]{1,0:T(8,128)(2,1)S(1)} %pad_maximum_fusion.n0), channel_id=1, source_target_pairs={{16,32},{32,16},{48,64},{64,48},{80,96},{96,80},{17,33},{33,17},{4... | collective-permute-start | bytes 737288 | tf_op jit(solution)/shard_map/ppermute | solution.py:461
  110.1 3.8 %receiver.1.r_ref = bf16[2048,512]{1,0:T(8,128)(2,1)} custom-call(bf16[2048,512]{1,0:T(8,128)(2,1)} %grid_ref.5, bf16[512,512]{1,0:T(8,128)(2,1)} %w_ref.1), custom_call_target="tpu_custom_call" | custom-call | tf_op jit(solution)/shard_map/receiver/pallas_call | solution.py:105
  113.9 5.6 %shard_map.198 = (f32[3,2048,512]{2,1,0:T(8,128)S(1)}, s32[3,2048]{1,0:T(4,128)S(1)}, bf16[512,512]{1,0:T(8,128)(2,1)S(1)}, bf16[2048,512]{1,0:T(8,128)(2,1)S(1)}) custom-call(s32[2]{0:T(128)S(1)} %pad_add_fusion.odd_ref, bf16[240,512]{1,0:T(8,128)(2,1)S(1)} %pad_maximum_fusion.n0, bf16[240,512]{1,0:T(8,128)(2,1)S(1)} %collective-permute-done.11.n1, ...), custom_call_target="tpu_custom_call" | custom-call | tf_op jit(solution)/shard_map/pallas_call | solution.py:81
  119.5 6.9 %decode_far.1 = bf16[2048,512]{1,0:T(8,128)(2,1)} custom-call(s32[2]{0:T(128)S(1)} %pad_add_fusion.odd_ref, bf16[240,512]{1,0:T(8,128)(2,1)S(1)} %collective-permute-done.10.n2, f32[3,2048,512]{2,1,0:T(8,128)S(1)} %get-tuple-element.51.v, s32[3,2048]{1,0:T(4,128)S(1)} %get-tuple-element.52.slots, bf16[512,512]{1,0:T(8,128)(2,1)S(1)} %get-tuple-element.53.w, ...), custom_call_target="tpu_custom_call" | custom-call | tf_op jit(solution)/shard_map/decode_far/pallas_call | solution.py:438
  (34 shorter events, 11.7 us)
Async XLA Ops:
  0.0 6.7 %collective-permute-start = (bf16[80,512]{1,0:T(8,128)(2,1)}, bf16[80,512]{1,0:T(8,128)(2,1)S(1)}, u32[]{:S(2)}, u32[]{:S(2)}) collective-permute-start(bf16[80,512]{1,0:T(8,128)(2,1)} %mesh_ref.1), channel_id=1, source_target_pairs={{0,1},{1,0},{2,3},{3,2},{4,5},{5,4},{6,7},{7,6},{8,9},{9,8},{10,11... | collective-permute-start | bytes 245768 | tf_op jit(solution)/shard_map/ppermute | solution.py:462
  1.6 7.5 %collective-permute-start.1 = (bf16[80,512]{1,0:T(8,128)(2,1)}, bf16[80,512]{1,0:T(8,128)(2,1)S(1)}, u32[]{:S(2)}, u32[]{:S(2)}) collective-permute-start(bf16[80,512]{1,0:T(8,128)(2,1)} %mesh_ref.1), channel_id=1, source_target_pairs={{1,2},{2,1},{3,4},{4,3},{5,6},{6,5},{7,8},{8,7},{9,10},{10,9},{11,... | collective-permute-start | bytes 245768 | tf_op jit(solution)/shard_map/ppermute | solution.py:461
  9.1 5.3 %collective-permute-start.3 = (bf16[240,512]{1,0:T(8,128)(2,1)S(1)}, bf16[240,512]{1,0:T(8,128)(2,1)S(1)}, u32[]{:S(2)}, u32[]{:S(2)}) collective-permute-start(bf16[240,512]{1,0:T(8,128)(2,1)S(1)} %constant_dynamic-update-slice_fusion.n0), channel_id=1, source_target_pairs={{0,16},{16,0},{32,48},{48,32},{64,80},{80,64},{96,112},{112,96},{1... | collective-permute-start | bytes 737288 | tf_op jit(solution)/shard_map/ppermute | solution.py:462
  11.2 9.0 %collective-permute-start.2 = (bf16[240,512]{1,0:T(8,128)(2,1)S(1)}, bf16[240,512]{1,0:T(8,128)(2,1)S(1)}, u32[]{:S(2)}, u32[]{:S(2)}) collective-permute-start(bf16[240,512]{1,0:T(8,128)(2,1)S(1)} %constant_dynamic-update-slice_fusion.n0), channel_id=1, source_target_pairs={{16,32},{32,16},{48,64},{64,48},{80,96},{96,80},{17,33},{33,17},{4... | collective-permute-start | bytes 737288 | tf_op jit(solution)/shard_map/ppermute | solution.py:461
  20.2 17.4 %copy-start.3 = (s32[1,128,4]{1,2,0:T(4,128)S(1)}, s32[1,128,4]{1,2,0:T(4,128)}, u32[]{:S(2)}) copy-start(s32[1,128,4]{1,2,0:T(4,128)} %param.24) | copy-start | bytes 6148
  20.2 26.3 %copy-start = (bf16[80,512]{1,0:T(8,128)(2,1)S(1)}, bf16[80,512]{1,0:T(8,128)(2,1)}, u32[]{:S(2)}) copy-start(bf16[80,512]{1,0:T(8,128)(2,1)} %mesh_ref.1) | copy-start | bytes 245764
  25.7 3.7 %collective-permute-start.4 = (bf16[240,512]{1,0:T(8,128)(2,1)S(1)}, bf16[240,512]{1,0:T(8,128)(2,1)S(1)}, u32[]{:S(2)}, u32[]{:S(2)}) collective-permute-start(bf16[240,512]{1,0:T(8,128)(2,1)S(1)} %get-tuple-element.34), channel_id=1, source_target_pairs={{0,16},{16,0},{32,48},{48,32},{64,80},{80,64},{96,112},{112,96},{1... | collective-permute-start | bytes 737288 | tf_op jit(solution)/shard_map/ppermute | solution.py:462
  25.8 7.5 %collective-permute-start.5 = (bf16[240,512]{1,0:T(8,128)(2,1)S(1)}, bf16[240,512]{1,0:T(8,128)(2,1)S(1)}, u32[]{:S(2)}, u32[]{:S(2)}) collective-permute-start(bf16[240,512]{1,0:T(8,128)(2,1)S(1)} %get-tuple-element.35), channel_id=1, source_target_pairs={{16,32},{32,16},{48,64},{64,48},{80,96},{96,80},{17,33},{33,17},{4... | collective-permute-start | bytes 737288 | tf_op jit(solution)/shard_map/ppermute | solution.py:461
  33.4 21.4 %collective-permute-start.6 = (bf16[80,512]{1,0:T(8,128)(2,1)S(1)}, bf16[80,512]{1,0:T(8,128)(2,1)S(1)}, u32[]{:S(2)}, u32[]{:S(2)}) collective-permute-start(bf16[80,512]{1,0:T(8,128)(2,1)S(1)} %get-tuple-element.56), channel_id=1, source_target_pairs={{0,1},{1,0},{2,3},{3,2},{4,5},{5,4},{6,7},{7,6},{8,9},{9,8},{10,11... | collective-permute-start | bytes 245768 | tf_op jit(solution)/shard_map/ppermute | solution.py:462
  33.5 21.3 %collective-permute-start.7 = (bf16[80,512]{1,0:T(8,128)(2,1)S(1)}, bf16[80,512]{1,0:T(8,128)(2,1)S(1)}, u32[]{:S(2)}, u32[]{:S(2)}) collective-permute-start(bf16[80,512]{1,0:T(8,128)(2,1)S(1)} %get-tuple-element.55), channel_id=1, source_target_pairs={{1,2},{2,1},{3,4},{4,3},{5,6},{6,5},{7,8},{8,7},{9,10},{10,9},{11,... | collective-permute-start | bytes 245768 | tf_op jit(solution)/shard_map/ppermute | solution.py:461
  38.3 16.4 %all-to-all-start = ((s32[128,1,4]{2,1,0:T(1,128)}), s32[128,1,4]{2,1,0:T(1,128)S(1)}, u32[]{:S(2)}, u32[]{:S(2)}) async-start(s32[128,1,4]{2,1,0:T(1,128)} %bitcast.2), calls=%async_computation | async-start | bytes 131072 | tf_op jit(solution)/shard_map/all_to_all | solution.py:518
  46.5 15.9 %copy-start.1 = (s32[640]{0:T(1024)S(1)}, s32[640]{0:T(1024)}, u32[]{:S(2)}) copy-start(s32[640]{0:T(1024)} %param.26) | copy-start | bytes 7684
  46.5 15.9 %copy-start.2 = (s32[640]{0:T(1024)S(1)}, s32[640]{0:T(1024)}, u32[]{:S(2)}) copy-start(s32[640]{0:T(1024)} %param.25) | copy-start | bytes 7684
  56.6 18.0 %all-to-all-start.1 = ((bf16[128,16,128]{2,1,0:T(8,128)(2,1)}), bf16[128,16,128]{2,1,0:T(8,128)(2,1)S(1)}, u32[]{:S(2)}, u32[]{:S(2)}) async-start(bf16[128,16,128]{2,1,0:T(8,128)(2,1)} %bitcast.4), calls=%async_computation.1 | async-start | bytes 1048576 | tf_op jit(solution)/shard_map/all_to_all | solution.py:528
  77.3 18.2 %all-to-all-start.2 = ((bf16[128,16,128]{2,1,0:T(8,128)(2,1)}), bf16[128,16,128]{2,1,0:T(8,128)(2,1)S(1)}, u32[]{:S(2)}, u32[]{:S(2)}) async-start(bf16[128,16,128]{2,1,0:T(8,128)(2,1)} %bitcast.6), calls=%async_computation.2 | async-start | bytes 1048576 | tf_op jit(solution)/shard_map/all_to_all | solution.py:528
  97.0 4.6 %collective-permute-start.8 = (bf16[80,512]{1,0:T(8,128)(2,1)S(1)}, bf16[80,512]{1,0:T(8,128)(2,1)S(1)}, u32[]{:S(2)}, u32[]{:S(2)}) collective-permute-start(bf16[80,512]{1,0:T(8,128)(2,1)S(1)} %shard_map.197), channel_id=1, source_target_pairs={{0,1},{1,0},{2,3},{3,2},{4,5},{5,4},{6,7},{7,6},{8,9},{9,8},{10,11... | collective-permute-start | bytes 245768 | tf_op jit(solution)/shard_map/ppermute | solution.py:462
  97.7 7.3 %collective-permute-start.9 = (bf16[80,512]{1,0:T(8,128)(2,1)S(1)}, bf16[80,512]{1,0:T(8,128)(2,1)S(1)}, u32[]{:S(2)}, u32[]{:S(2)}) collective-permute-start(bf16[80,512]{1,0:T(8,128)(2,1)S(1)} %shard_map.197), channel_id=1, source_target_pairs={{1,2},{2,1},{3,4},{4,3},{5,6},{6,5},{7,8},{8,7},{9,10},{10,9},{11,... | collective-permute-start | bytes 245768 | tf_op jit(solution)/shard_map/ppermute | solution.py:461
  105.0 8.9 %collective-permute-start.11 = (bf16[240,512]{1,0:T(8,128)(2,1)S(1)}, bf16[240,512]{1,0:T(8,128)(2,1)S(1)}, u32[]{:S(2)}, u32[]{:S(2)}) collective-permute-start(bf16[240,512]{1,0:T(8,128)(2,1)S(1)} %pad_maximum_fusion.n0), channel_id=1, source_target_pairs={{0,16},{16,0},{32,48},{48,32},{64,80},{80,64},{96,112},{112,96},{1... | collective-permute-start | bytes 737288 | tf_op jit(solution)/shard_map/ppermute | solution.py:462
  107.9 11.5 %collective-permute-start.10 = (bf16[240,512]{1,0:T(8,128)(2,1)S(1)}, bf16[240,512]{1,0:T(8,128)(2,1)S(1)}, u32[]{:S(2)}, u32[]{:S(2)}) collective-permute-start(bf16[240,512]{1,0:T(8,128)(2,1)S(1)} %pad_maximum_fusion.n0), channel_id=1, source_target_pairs={{16,32},{32,16},{48,64},{64,48},{80,96},{96,80},{17,33},{33,17},{4... | collective-permute-start | bytes 737288 | tf_op jit(solution)/shard_map/ppermute | solution.py:461

commit v6 on v5

--- a/solution.py
+++ b/solution.py
@@ -14,8 +14,8 @@
 SIDE = 3
 ENC_ROWS = 1024
 DEC_ROWS = 1024
-FAR_ROWS = 512
-FAR_PART = 512
+FAR_ROWS = 1024
+FAR_PART = 1024
 PRE_ROWS = 1024
 
 
@@ -515,7 +515,8 @@
     prepared = encode_near(
         odd, grid_latent, encoder_slots, near[:2], encoder_receiver, encoder_sender
     )
-    asked = lax.all_to_all(peer_rows[0], ("lat", "lon"), split_axis=0, concat_axis=0, tiled=True)
+    wanted = jnp.maximum(peer_rows[0], 0)
+    asked = lax.all_to_all(wanted, ("lat", "lon"), split_axis=0, concat_axis=0, tiled=True)
     sums = encode_far(odd, near[2], prepared)
     own, a, b = to_owners(sums, owned)
     staged = stage(mesh_latent, encoder_output, encoder_merge, encoder_self, process_sender)

time: 127 us -> 126 us (level)
  no operation moved by 1% of the time
where the time goes in v6:
time: 126 us
  starting transfers between devices  48.3 us (38%)
  Pallas kernels  39.2 us (31%)
  waiting for transfers between devices  36 us (29%)
    pallas_call x9, Pallas kernels, on_chip(): pl.pallas_call(kernel, in_specs=specs, out_specs=[VMEM] * len(outs), out_...  29.2 us
    ppermute x6, starting transfers between devices, swap_both(): b = lax.ppermute(to_second, axis, second)  21 us
    all_to_all x2, waiting for transfers between devices, body(): lax.all_to_all(outgoing.reshape(tiles, -1, 128), ('lat', 'lon'), split_ax...  19.9 us
    all_to_all x2, starting transfers between devices, body(): lax.all_to_all(outgoing.reshape(tiles, -1, 128), ('lat', 'lon'), split_ax...  11.7 us
    ppermute x6, waiting for transfers between devices, swap_both(): b = lax.ppermute(to_second, axis, second)  9.63 us
    all_to_all x1, starting transfers between devices, body(): lax.all_to_all(wanted, ('lat', 'lon'), split_axis=0, concat_axis=0, tiled...  8.14 us
    ppermute x6, starting transfers between devices, swap_both(): a = lax.ppermute(to_first, axis, first)  7.53 us
    all_to_all x1, waiting for transfers between devices, body(): lax.all_to_all(wanted, ('lat', 'lon'), split_axis=0, concat_axis=0, tiled...  6.39 us
  transfers between devices with their start and end apart: 15, of which 6 were waited for; matrix products, arithmetic and copies ran while one was open for 1% of the time, Pallas kernels for 17%

profile of v6, /device:TPU:3, one launch (start us, length us, event | category | flops | bytes accessed | tf_op | source)
XLA Modules:
  0.0 125.6 jit_solution(426540239417819680)
XLA Ops:
  1.6 4.1 %collective-permute-start.1 = (bf16[80,512]{1,0:T(8,128)(2,1)}, bf16[80,512]{1,0:T(8,128)(2,1)S(1)}, u32[]{:S(2)}, u32[]{:S(2)}) collective-permute-start(bf16[80,512]{1,0:T(8,128)(2,1)} %mesh_ref.1), channel_id=1, source_target_pairs={{1,2},{2,1},{3,4},{4,3},{5,6},{6,5},{7,8},{8,7},{9,10},{10,9},{11,... | collective-permute-start | bytes 245768 | tf_op jit(solution)/shard_map/ppermute | solution.py:461
  6.7 2.4 %collective-permute-done.1 = bf16[80,512]{1,0:T(8,128)(2,1)S(1)} collective-permute-done((bf16[80,512]{1,0:T(8,128)(2,1)}, bf16[80,512]{1,0:T(8,128)(2,1)S(1)}, u32[]{:S(2)}, u32[]{:S(2)}) %collective-permute-start.1) | collective-permute-done | bytes 81952 | tf_op jit(solution)/shard_map/ppermute | solution.py:461
  11.2 3.1 %collective-permute-start.2 = (bf16[240,512]{1,0:T(8,128)(2,1)S(1)}, bf16[240,512]{1,0:T(8,128)(2,1)S(1)}, u32[]{:S(2)}, u32[]{:S(2)}) collective-permute-start(bf16[240,512]{1,0:T(8,128)(2,1)S(1)} %constant_dynamic-update-slice_fusion.n0), channel_id=1, source_target_pairs={{16,32},{32,16},{48,64},{64,48},{80,96},{96,80},{17,33},{33,17},{4... | collective-permute-start | bytes 737288 | tf_op jit(solution)/shard_map/ppermute | solution.py:461
  14.4 5.7 %shard_map.190 = (f32[2,2048,512]{2,1,0:T(8,128)S(1)}, s32[2,2048]{1,0:T(2,128)S(1)}, bf16[512,512]{1,0:T(8,128)(2,1)S(1)}) custom-call(s32[2]{0:T(128)S(1)} %pad_add_fusion.odd_ref, bf16[240,512]{1,0:T(8,128)(2,1)S(1)} %constant_dynamic-update-slice_fusion.n0, bf16[240,512]{1,0:T(8,128)(2,1)S(1)} %collective-permute-done.3.n1, s32[2,2048]{1,0:T(2,128)} %slots_ref.2, ...), custom_call_target="tpu_custom_call" | custom-call | tf_op jit(solution)/shard_map/pallas_call | solution.py:81
  20.2 5.4 %shard_map.191 = (bf16[240,512]{1,0:T(8,128)(2,1)S(1)}, bf16[240,512]{1,0:T(8,128)(2,1)S(1)}, bf16[240,512]{1,0:T(8,128)(2,1)S(1)}) custom-call(s32[2]{0:T(128)S(1)} %pad_add_fusion.odd_ref, bf16[240,512]{1,0:T(8,128)(2,1)S(1)} %collective-permute-done.2.n2, f32[2,2048,512]{2,1,0:T(8,128)S(1)} %get-tuple-element.30.v_ref, ...), custom_call_target="tpu_custom_call" | custom-call | tf_op jit(solution)/shard_map/pallas_call | solution.py:81
  25.8 3.6 %collective-permute-start.5 = (bf16[240,512]{1,0:T(8,128)(2,1)S(1)}, bf16[240,512]{1,0:T(8,128)(2,1)S(1)}, u32[]{:S(2)}, u32[]{:S(2)}) collective-permute-start(bf16[240,512]{1,0:T(8,128)(2,1)S(1)} %get-tuple-element.35), channel_id=1, source_target_pairs={{16,32},{32,16},{48,64},{64,48},{80,96},{96,80},{17,33},{33,17},{4... | collective-permute-start | bytes 737288 | tf_op jit(solution)/shard_map/ppermute | solution.py:461
  29.5 3.8 %collective-permute-done.5 = bf16[240,512]{1,0:T(8,128)(2,1)S(1)} collective-permute-done((bf16[240,512]{1,0:T(8,128)(2,1)S(1)}, bf16[240,512]{1,0:T(8,128)(2,1)S(1)}, u32[]{:S(2)}, u32[]{:S(2)}) %collective-permute-start.5) | collective-permute-done | bytes 245792 | tf_op jit(solution)/shard_map/ppermute | solution.py:461
  33.5 4.1 %collective-permute-start.7 = (bf16[80,512]{1,0:T(8,128)(2,1)S(1)}, bf16[80,512]{1,0:T(8,128)(2,1)S(1)}, u32[]{:S(2)}, u32[]{:S(2)}) collective-permute-start(bf16[80,512]{1,0:T(8,128)(2,1)S(1)} %get-tuple-element.55), channel_id=1, source_target_pairs={{1,2},{2,1},{3,4},{4,3},{5,6},{6,5},{7,8},{8,7},{9,10},{10,9},{11,... | collective-permute-start | bytes 245768 | tf_op jit(solution)/shard_map/ppermute | solution.py:461
  38.2 8.1 %all-to-all-start = ((s32[128,1,4]{2,1,0:T(1,128)}), s32[128,1,4]{2,1,0:T(1,128)S(1)}, u32[]{:S(2)}, u32[]{:S(2)}) async-start(s32[128,1,4]{2,1,0:T(1,128)} %bitcast.2), calls=%async_computation | async-start | bytes 131072 | tf_op jit(solution)/shard_map/all_to_all | solution.py:519
  48.3 6.4 %all-to-all-done = s32[128,1,4]{2,1,0:T(1,128)S(1)} async-done(((s32[128,1,4]{2,1,0:T(1,128)}), s32[128,1,4]{2,1,0:T(1,128)S(1)}, u32[]{:S(2)}, u32[]{:S(2)}) %all-to-all-start) | async-done | bytes 2080 | tf_op jit(solution)/shard_map/all_to_all | solution.py:519
  56.5 5.7 %all-to-all-start.1 = ((bf16[128,16,128]{2,1,0:T(8,128)(2,1)}), bf16[128,16,128]{2,1,0:T(8,128)(2,1)S(1)}, u32[]{:S(2)}, u32[]{:S(2)}) async-start(bf16[128,16,128]{2,1,0:T(8,128)(2,1)} %bitcast.4), calls=%async_computation.1 | async-start | bytes 1048576 | tf_op jit(solution)/shard_map/all_to_all | solution.py:529
  62.3 2.3 %shard_map.194 = (bf16[640,512]{1,0:T(8,128)(2,1)S(1)}, f32[80,512]{1,0:T(8,128)S(1)}, bf16[512,512]{1,0:T(8,128)(2,1)S(1)}, bf16[512,512]{1,0:T(8,128)(2,1)S(1)}) custom-call(bf16[80,512]{1,0:T(8,128)(2,1)S(1)} %get-tuple-element.40.state_ref, s32[1,640]{1,0:T(1,128)S(1)} %broadcast_in_dim.6.tgt_ref, bf16[2,512,512]{2,1,0:T(8,128)(2,1)} %wr.3, ...), custom_call_target="tpu_custom_call" | custom-call | tf_op jit(solution)/shard_map/pallas_call | solution.py:81
  64.6 9.9 %all-to-all-done.1 = bf16[128,16,128]{2,1,0:T(8,128)(2,1)S(1)} async-done(((bf16[128,16,128]{2,1,0:T(8,128)(2,1)}), bf16[128,16,128]{2,1,0:T(8,128)(2,1)S(1)}, u32[]{:S(2)}, u32[]{:S(2)}) %all-to-all-start.1) | async-done | bytes 524320 | tf_op jit(solution)/shard_map/all_to_all | solution.py:529
  74.5 2.7 %shard_map.195 = (bf16[80,512]{1,0:T(8,128)(2,1)S(1)}, bf16[2048,128]{1,0:T(8,128)(2,1)}) custom-call(bf16[2048,128]{1,0:T(8,128)(2,1)S(1)} %bitcast.9, bf16[640,512]{1,0:T(8,128)(2,1)S(1)} %get-tuple-element.41.base_ref, f32[80,512]{1,0:T(8,128)S(1)} %get-tuple-element.42.self_ref, bf16[512,512]{1,0:T(8,128)(2,1)S(1)} %get-tuple-element.43.wom, ...), custom_call_target="tpu_custom_call" | custom-call | tf_op jit(solution)/shard_map/pallas_call | solution.py:81
  77.2 5.9 %all-to-all-start.2 = ((bf16[128,16,128]{2,1,0:T(8,128)(2,1)}), bf16[128,16,128]{2,1,0:T(8,128)(2,1)S(1)}, u32[]{:S(2)}, u32[]{:S(2)}) async-start(bf16[128,16,128]{2,1,0:T(8,128)(2,1)} %bitcast.6), calls=%async_computation.2 | async-start | bytes 1048576 | tf_op jit(solution)/shard_map/all_to_all | solution.py:529
  83.1 2.3 %shard_map.196 = (bf16[640,512]{1,0:T(8,128)(2,1)S(1)}, f32[80,512]{1,0:T(8,128)S(1)}, bf16[512,512]{1,0:T(8,128)(2,1)S(1)}, bf16[512,512]{1,0:T(8,128)(2,1)S(1)}) custom-call(bf16[80,512]{1,0:T(8,128)(2,1)S(1)} %get-tuple-element.46.state_ref, s32[1,640]{1,0:T(1,128)S(1)} %broadcast_in_dim.6.tgt_ref, bf16[2,512,512]{2,1,0:T(8,128)(2,1)} %wr.3, ...), custom_call_target="tpu_custom_call" | custom-call | tf_op jit(solution)/shard_map/pallas_call | solution.py:81
  85.4 10.0 %all-to-all-done.2 = bf16[128,16,128]{2,1,0:T(8,128)(2,1)S(1)} async-done(((bf16[128,16,128]{2,1,0:T(8,128)(2,1)}), bf16[128,16,128]{2,1,0:T(8,128)(2,1)S(1)}, u32[]{:S(2)}, u32[]{:S(2)}) %all-to-all-start.2) | async-done | bytes 524320 | tf_op jit(solution)/shard_map/all_to_all | solution.py:529
  97.6 3.9 %collective-permute-start.9 = (bf16[80,512]{1,0:T(8,128)(2,1)S(1)}, bf16[80,512]{1,0:T(8,128)(2,1)S(1)}, u32[]{:S(2)}, u32[]{:S(2)}) collective-permute-start(bf16[80,512]{1,0:T(8,128)(2,1)S(1)} %shard_map.197), channel_id=1, source_target_pairs={{1,2},{2,1},{3,4},{4,3},{5,6},{6,5},{7,8},{8,7},{9,10},{10,9},{11,... | collective-permute-start | bytes 245768 | tf_op jit(solution)/shard_map/ppermute | solution.py:461
  101.5 3.4 %collective-permute-done.9 = bf16[80,512]{1,0:T(8,128)(2,1)S(1)} collective-permute-done((bf16[80,512]{1,0:T(8,128)(2,1)S(1)}, bf16[80,512]{1,0:T(8,128)(2,1)S(1)}, u32[]{:S(2)}, u32[]{:S(2)}) %collective-permute-start.9) | collective-permute-done | bytes 81952 | tf_op jit(solution)/shard_map/ppermute | solution.py:461
  104.9 2.9 %collective-permute-start.11 = (bf16[240,512]{1,0:T(8,128)(2,1)S(1)}, bf16[240,512]{1,0:T(8,128)(2,1)S(1)}, u32[]{:S(2)}, u32[]{:S(2)}) collective-permute-start(bf16[240,512]{1,0:T(8,128)(2,1)S(1)} %pad_maximum_fusion.n0), channel_id=1, source_target_pairs={{0,16},{16,0},{32,48},{48,32},{64,80},{80,64},{96,112},{112,96},{1... | collective-permute-start | bytes 737288 | tf_op jit(solution)/shard_map/ppermute | solution.py:462
  107.8 2.2 %collective-permute-start.10 = (bf16[240,512]{1,0:T(8,128)(2,1)S(1)}, bf16[240,512]{1,0:T(8,128)(2,1)S(1)}, u32[]{:S(2)}, u32[]{:S(2)}) collective-permute-start(bf16[240,512]{1,0:T(8,128)(2,1)S(1)} %pad_maximum_fusion.n0), channel_id=1, source_target_pairs={{16,32},{32,16},{48,64},{64,48},{80,96},{96,80},{17,33},{33,17},{4... | collective-permute-start | bytes 737288 | tf_op jit(solution)/shard_map/ppermute | solution.py:461
  110.0 3.8 %receiver.1.r_ref = bf16[2048,512]{1,0:T(8,128)(2,1)} custom-call(bf16[2048,512]{1,0:T(8,128)(2,1)} %grid_ref.5, bf16[512,512]{1,0:T(8,128)(2,1)} %w_ref.1), custom_call_target="tpu_custom_call" | custom-call | tf_op jit(solution)/shard_map/receiver/pallas_call | solution.py:105
  113.8 5.6 %shard_map.198 = (f32[3,2048,512]{2,1,0:T(8,128)S(1)}, s32[3,2048]{1,0:T(4,128)S(1)}, bf16[512,512]{1,0:T(8,128)(2,1)S(1)}, bf16[2048,512]{1,0:T(8,128)(2,1)S(1)}) custom-call(s32[2]{0:T(128)S(1)} %pad_add_fusion.odd_ref, bf16[240,512]{1,0:T(8,128)(2,1)S(1)} %pad_maximum_fusion.n0, bf16[240,512]{1,0:T(8,128)(2,1)S(1)} %collective-permute-done.11.n1, ...), custom_call_target="tpu_custom_call" | custom-call | tf_op jit(solution)/shard_map/pallas_call | solution.py:81
  119.4 6.2 %decode_far.1 = bf16[2048,512]{1,0:T(8,128)(2,1)} custom-call(s32[2]{0:T(128)S(1)} %pad_add_fusion.odd_ref, bf16[240,512]{1,0:T(8,128)(2,1)S(1)} %collective-permute-done.10.n2, f32[3,2048,512]{2,1,0:T(8,128)S(1)} %get-tuple-element.51.v, s32[3,2048]{1,0:T(4,128)S(1)} %get-tuple-element.52.slots, bf16[512,512]{1,0:T(8,128)(2,1)S(1)} %get-tuple-element.53.w, ...), custom_call_target="tpu_custom_call" | custom-call | tf_op jit(solution)/shard_map/decode_far/pallas_call | solution.py:438
  (35 shorter events, 11.7 us)
Async XLA Ops:
  0.0 6.7 %collective-permute-start = (bf16[80,512]{1,0:T(8,128)(2,1)}, bf16[80,512]{1,0:T(8,128)(2,1)S(1)}, u32[]{:S(2)}, u32[]{:S(2)}) collective-permute-start(bf16[80,512]{1,0:T(8,128)(2,1)} %mesh_ref.1), channel_id=1, source_target_pairs={{0,1},{1,0},{2,3},{3,2},{4,5},{5,4},{6,7},{7,6},{8,9},{9,8},{10,11... | collective-permute-start | bytes 245768 | tf_op jit(solution)/shard_map/ppermute | solution.py:462
  1.6 7.5 %collective-permute-start.1 = (bf16[80,512]{1,0:T(8,128)(2,1)}, bf16[80,512]{1,0:T(8,128)(2,1)S(1)}, u32[]{:S(2)}, u32[]{:S(2)}) collective-permute-start(bf16[80,512]{1,0:T(8,128)(2,1)} %mesh_ref.1), channel_id=1, source_target_pairs={{1,2},{2,1},{3,4},{4,3},{5,6},{6,5},{7,8},{8,7},{9,10},{10,9},{11,... | collective-permute-start | bytes 245768 | tf_op jit(solution)/shard_map/ppermute | solution.py:461
  9.1 5.3 %collective-permute-start.3 = (bf16[240,512]{1,0:T(8,128)(2,1)S(1)}, bf16[240,512]{1,0:T(8,128)(2,1)S(1)}, u32[]{:S(2)}, u32[]{:S(2)}) collective-permute-start(bf16[240,512]{1,0:T(8,128)(2,1)S(1)} %constant_dynamic-update-slice_fusion.n0), channel_id=1, source_target_pairs={{0,16},{16,0},{32,48},{48,32},{64,80},{80,64},{96,112},{112,96},{1... | collective-permute-start | bytes 737288 | tf_op jit(solution)/shard_map/ppermute | solution.py:462
  11.2 9.0 %collective-permute-start.2 = (bf16[240,512]{1,0:T(8,128)(2,1)S(1)}, bf16[240,512]{1,0:T(8,128)(2,1)S(1)}, u32[]{:S(2)}, u32[]{:S(2)}) collective-permute-start(bf16[240,512]{1,0:T(8,128)(2,1)S(1)} %constant_dynamic-update-slice_fusion.n0), channel_id=1, source_target_pairs={{16,32},{32,16},{48,64},{64,48},{80,96},{96,80},{17,33},{33,17},{4... | collective-permute-start | bytes 737288 | tf_op jit(solution)/shard_map/ppermute | solution.py:461
  20.2 9.1 %copy-start.3 = (s32[1,128,4]{1,2,0:T(4,128)S(1)}, s32[1,128,4]{1,2,0:T(4,128)}, u32[]{:S(2)}) copy-start(s32[1,128,4]{1,2,0:T(4,128)} %param.24) | copy-start | bytes 6148
  20.2 26.2 %copy-start = (bf16[80,512]{1,0:T(8,128)(2,1)S(1)}, bf16[80,512]{1,0:T(8,128)(2,1)}, u32[]{:S(2)}) copy-start(bf16[80,512]{1,0:T(8,128)(2,1)} %mesh_ref.1) | copy-start | bytes 245764
  25.7 3.8 %collective-permute-start.4 = (bf16[240,512]{1,0:T(8,128)(2,1)S(1)}, bf16[240,512]{1,0:T(8,128)(2,1)S(1)}, u32[]{:S(2)}, u32[]{:S(2)}) collective-permute-start(bf16[240,512]{1,0:T(8,128)(2,1)S(1)} %get-tuple-element.34), channel_id=1, source_target_pairs={{0,16},{16,0},{32,48},{48,32},{64,80},{80,64},{96,112},{112,96},{1... | collective-permute-start | bytes 737288 | tf_op jit(solution)/shard_map/ppermute | solution.py:462
  25.8 7.5 %collective-permute-start.5 = (bf16[240,512]{1,0:T(8,128)(2,1)S(1)}, bf16[240,512]{1,0:T(8,128)(2,1)S(1)}, u32[]{:S(2)}, u32[]{:S(2)}) collective-permute-start(bf16[240,512]{1,0:T(8,128)(2,1)S(1)} %get-tuple-element.35), channel_id=1, source_target_pairs={{16,32},{32,16},{48,64},{64,48},{80,96},{96,80},{17,33},{33,17},{4... | collective-permute-start | bytes 737288 | tf_op jit(solution)/shard_map/ppermute | solution.py:461
  33.4 21.3 %collective-permute-start.6 = (bf16[80,512]{1,0:T(8,128)(2,1)S(1)}, bf16[80,512]{1,0:T(8,128)(2,1)S(1)}, u32[]{:S(2)}, u32[]{:S(2)}) collective-permute-start(bf16[80,512]{1,0:T(8,128)(2,1)S(1)} %get-tuple-element.56), channel_id=1, source_target_pairs={{0,1},{1,0},{2,3},{3,2},{4,5},{5,4},{6,7},{7,6},{8,9},{9,8},{10,11... | collective-permute-start | bytes 245768 | tf_op jit(solution)/shard_map/ppermute | solution.py:462
  33.5 21.2 %collective-permute-start.7 = (bf16[80,512]{1,0:T(8,128)(2,1)S(1)}, bf16[80,512]{1,0:T(8,128)(2,1)S(1)}, u32[]{:S(2)}, u32[]{:S(2)}) collective-permute-start(bf16[80,512]{1,0:T(8,128)(2,1)S(1)} %get-tuple-element.55), channel_id=1, source_target_pairs={{1,2},{2,1},{3,4},{4,3},{5,6},{6,5},{7,8},{8,7},{9,10},{10,9},{11,... | collective-permute-start | bytes 245768 | tf_op jit(solution)/shard_map/ppermute | solution.py:461
  38.2 16.4 %all-to-all-start = ((s32[128,1,4]{2,1,0:T(1,128)}), s32[128,1,4]{2,1,0:T(1,128)S(1)}, u32[]{:S(2)}, u32[]{:S(2)}) async-start(s32[128,1,4]{2,1,0:T(1,128)} %bitcast.2), calls=%async_computation | async-start | bytes 131072 | tf_op jit(solution)/shard_map/all_to_all | solution.py:519
  46.4 15.9 %copy-start.1 = (s32[640]{0:T(1024)S(1)}, s32[640]{0:T(1024)}, u32[]{:S(2)}) copy-start(s32[640]{0:T(1024)} %param.26) | copy-start | bytes 7684
  46.4 15.9 %copy-start.2 = (s32[640]{0:T(1024)S(1)}, s32[640]{0:T(1024)}, u32[]{:S(2)}) copy-start(s32[640]{0:T(1024)} %param.25) | copy-start | bytes 7684
  56.5 18.0 %all-to-all-start.1 = ((bf16[128,16,128]{2,1,0:T(8,128)(2,1)}), bf16[128,16,128]{2,1,0:T(8,128)(2,1)S(1)}, u32[]{:S(2)}, u32[]{:S(2)}) async-start(bf16[128,16,128]{2,1,0:T(8,128)(2,1)} %bitcast.4), calls=%async_computation.1 | async-start | bytes 1048576 | tf_op jit(solution)/shard_map/all_to_all | solution.py:529
  77.2 18.2 %all-to-all-start.2 = ((bf16[128,16,128]{2,1,0:T(8,128)(2,1)}), bf16[128,16,128]{2,1,0:T(8,128)(2,1)S(1)}, u32[]{:S(2)}, u32[]{:S(2)}) async-start(bf16[128,16,128]{2,1,0:T(8,128)(2,1)} %bitcast.6), calls=%async_computation.2 | async-start | bytes 1048576 | tf_op jit(solution)/shard_map/all_to_all | solution.py:529
  96.9 4.6 %collective-permute-start.8 = (bf16[80,512]{1,0:T(8,128)(2,1)S(1)}, bf16[80,512]{1,0:T(8,128)(2,1)S(1)}, u32[]{:S(2)}, u32[]{:S(2)}) collective-permute-start(bf16[80,512]{1,0:T(8,128)(2,1)S(1)} %shard_map.197), channel_id=1, source_target_pairs={{0,1},{1,0},{2,3},{3,2},{4,5},{5,4},{6,7},{7,6},{8,9},{9,8},{10,11... | collective-permute-start | bytes 245768 | tf_op jit(solution)/shard_map/ppermute | solution.py:462
  97.6 7.3 %collective-permute-start.9 = (bf16[80,512]{1,0:T(8,128)(2,1)S(1)}, bf16[80,512]{1,0:T(8,128)(2,1)S(1)}, u32[]{:S(2)}, u32[]{:S(2)}) collective-permute-start(bf16[80,512]{1,0:T(8,128)(2,1)S(1)} %shard_map.197), channel_id=1, source_target_pairs={{1,2},{2,1},{3,4},{4,3},{5,6},{6,5},{7,8},{8,7},{9,10},{10,9},{11,... | collective-permute-start | bytes 245768 | tf_op jit(solution)/shard_map/ppermute | solution.py:461
  104.9 8.8 %collective-permute-start.11 = (bf16[240,512]{1,0:T(8,128)(2,1)S(1)}, bf16[240,512]{1,0:T(8,128)(2,1)S(1)}, u32[]{:S(2)}, u32[]{:S(2)}) collective-permute-start(bf16[240,512]{1,0:T(8,128)(2,1)S(1)} %pad_maximum_fusion.n0), channel_id=1, source_target_pairs={{0,16},{16,0},{32,48},{48,32},{64,80},{80,64},{96,112},{112,96},{1... | collective-permute-start | bytes 737288 | tf_op jit(solution)/shard_map/ppermute | solution.py:462
  107.8 11.5 %collective-permute-start.10 = (bf16[240,512]{1,0:T(8,128)(2,1)S(1)}, bf16[240,512]{1,0:T(8,128)(2,1)S(1)}, u32[]{:S(2)}, u32[]{:S(2)}) collective-permute-start(bf16[240,512]{1,0:T(8,128)(2,1)S(1)} %pad_maximum_fusion.n0), channel_id=1, source_target_pairs={{16,32},{32,16},{48,64},{64,48},{80,96},{96,80},{17,33},{33,17},{4... | collective-permute-start | bytes 737288 | tf_op jit(solution)/shard_map/ppermute | solution.py:461

commit v7 on v6

--- a/solution.py
+++ b/solution.py
@@ -400,11 +400,14 @@
     for at in range(0, rows, FAR_PART):
         part = pl.ds(pl.multiple_of(step * rows + at, FAR_PART), FAR_PART)
         total = None
+        chosen = jnp.concatenate(
+            [hot_rows(slots[f : f + 1, part] - start, near.shape[0]) for f in range(DEC_FAN)], axis=0
+        )
+        most = dot(chosen, near[...])
         for f in range(DEC_FAN):
-            chosen = hot_rows(slots[f : f + 1, part] - start, near.shape[0])
-            h = silu_of_half(dot(chosen, near[...]) + v[f, part, :]).astype(jnp.float32)
+            h = silu_of_half(most[f * FAR_PART : (f + 1) * FAR_PART] + v[f, part, :])
             total = h if total is None else total + h
-        update = dot(bf(total), w[...])
+        update = dot(total, w[...])
         out_ref[at : at + FAR_PART] = bf(g[part, :].astype(jnp.float32) + norm(update))
 
 

time: 126 us -> 126 us (level)
  no operation moved by 1% of the time
where the time goes in v7:
time: 126 us; the launch traced here: 125 us
  starting transfers between devices  48.3 us (38%)
  Pallas kernels  38.8 us (31%)
  waiting for transfers between devices  36 us (29%)
    pallas_call x9, Pallas kernels, on_chip(): pl.pallas_call(kernel, in_specs=specs, out_specs=[VMEM] * len(outs), out_...  29.2 us
    ppermute x6, starting transfers between devices, swap_both(): b = lax.ppermute(to_second, axis, second)  21 us
    all_to_all x2, waiting for transfers between devices, body(): lax.all_to_all(outgoing.reshape(tiles, -1, 128), ('lat', 'lon'), split_ax...  19.9 us
    all_to_all x2, starting transfers between devices, body(): lax.all_to_all(outgoing.reshape(tiles, -1, 128), ('lat', 'lon'), split_ax...  11.7 us
    ppermute x6, waiting for transfers between devices, swap_both(): b = lax.ppermute(to_second, axis, second)  9.63 us
    all_to_all x1, starting transfers between devices, body(): lax.all_to_all(wanted, ('lat', 'lon'), split_axis=0, concat_axis=0, tiled...  8.14 us
    ppermute x6, starting transfers between devices, swap_both(): a = lax.ppermute(to_first, axis, first)  7.53 us
    all_to_all x1, waiting for transfers between devices, body(): lax.all_to_all(wanted, ('lat', 'lon'), split_axis=0, concat_axis=0, tiled...  6.39 us
  transfers between devices with their start and end apart: 15, of which 6 were waited for; matrix products, arithmetic and copies ran while one was open for 1% of the time, Pallas kernels for 17%

profile of v7, /device:TPU:3, one launch (start us, length us, event | category | flops | bytes accessed | tf_op | source)
XLA Modules:
  0.0 125.2 jit_solution(10090223176588878132)
XLA Ops:
  1.6 4.1 %collective-permute-start.1 = (bf16[80,512]{1,0:T(8,128)(2,1)}, bf16[80,512]{1,0:T(8,128)(2,1)S(1)}, u32[]{:S(2)}, u32[]{:S(2)}) collective-permute-start(bf16[80,512]{1,0:T(8,128)(2,1)} %mesh_ref.1), channel_id=1, source_target_pairs={{1,2},{2,1},{3,4},{4,3},{5,6},{6,5},{7,8},{8,7},{9,10},{10,9},{11,... | collective-permute-start | bytes 245768 | tf_op jit(solution)/shard_map/ppermute | solution.py:464
  6.7 2.4 %collective-permute-done.1 = bf16[80,512]{1,0:T(8,128)(2,1)S(1)} collective-permute-done((bf16[80,512]{1,0:T(8,128)(2,1)}, bf16[80,512]{1,0:T(8,128)(2,1)S(1)}, u32[]{:S(2)}, u32[]{:S(2)}) %collective-permute-start.1) | collective-permute-done | bytes 81952 | tf_op jit(solution)/shard_map/ppermute | solution.py:464
  11.2 3.1 %collective-permute-start.2 = (bf16[240,512]{1,0:T(8,128)(2,1)S(1)}, bf16[240,512]{1,0:T(8,128)(2,1)S(1)}, u32[]{:S(2)}, u32[]{:S(2)}) collective-permute-start(bf16[240,512]{1,0:T(8,128)(2,1)S(1)} %constant_dynamic-update-slice_fusion.n0), channel_id=1, source_target_pairs={{16,32},{32,16},{48,64},{64,48},{80,96},{96,80},{17,33},{33,17},{4... | collective-permute-start | bytes 737288 | tf_op jit(solution)/shard_map/ppermute | solution.py:464
  14.4 5.7 %shard_map.190 = (f32[2,2048,512]{2,1,0:T(8,128)S(1)}, s32[2,2048]{1,0:T(2,128)S(1)}, bf16[512,512]{1,0:T(8,128)(2,1)S(1)}) custom-call(s32[2]{0:T(128)S(1)} %pad_add_fusion.odd_ref, bf16[240,512]{1,0:T(8,128)(2,1)S(1)} %constant_dynamic-update-slice_fusion.n0, bf16[240,512]{1,0:T(8,128)(2,1)S(1)} %collective-permute-done.3.n1, s32[2,2048]{1,0:T(2,128)} %slots_ref.2, ...), custom_call_target="tpu_custom_call" | custom-call | tf_op jit(solution)/shard_map/pallas_call | solution.py:81
  20.2 5.4 %shard_map.191 = (bf16[240,512]{1,0:T(8,128)(2,1)S(1)}, bf16[240,512]{1,0:T(8,128)(2,1)S(1)}, bf16[240,512]{1,0:T(8,128)(2,1)S(1)}) custom-call(s32[2]{0:T(128)S(1)} %pad_add_fusion.odd_ref, bf16[240,512]{1,0:T(8,128)(2,1)S(1)} %collective-permute-done.2.n2, f32[2,2048,512]{2,1,0:T(8,128)S(1)} %get-tuple-element.30.v_ref, ...), custom_call_target="tpu_custom_call" | custom-call | tf_op jit(solution)/shard_map/pallas_call | solution.py:81
  25.8 3.6 %collective-permute-start.5 = (bf16[240,512]{1,0:T(8,128)(2,1)S(1)}, bf16[240,512]{1,0:T(8,128)(2,1)S(1)}, u32[]{:S(2)}, u32[]{:S(2)}) collective-permute-start(bf16[240,512]{1,0:T(8,128)(2,1)S(1)} %get-tuple-element.35), channel_id=1, source_target_pairs={{16,32},{32,16},{48,64},{64,48},{80,96},{96,80},{17,33},{33,17},{4... | collective-permute-start | bytes 737288 | tf_op jit(solution)/shard_map/ppermute | solution.py:464
  29.5 3.8 %collective-permute-done.5 = bf16[240,512]{1,0:T(8,128)(2,1)S(1)} collective-permute-done((bf16[240,512]{1,0:T(8,128)(2,1)S(1)}, bf16[240,512]{1,0:T(8,128)(2,1)S(1)}, u32[]{:S(2)}, u32[]{:S(2)}) %collective-permute-start.5) | collective-permute-done | bytes 245792 | tf_op jit(solution)/shard_map/ppermute | solution.py:464
  33.5 4.1 %collective-permute-start.7 = (bf16[80,512]{1,0:T(8,128)(2,1)S(1)}, bf16[80,512]{1,0:T(8,128)(2,1)S(1)}, u32[]{:S(2)}, u32[]{:S(2)}) collective-permute-start(bf16[80,512]{1,0:T(8,128)(2,1)S(1)} %get-tuple-element.55), channel_id=1, source_target_pairs={{1,2},{2,1},{3,4},{4,3},{5,6},{6,5},{7,8},{8,7},{9,10},{10,9},{11,... | collective-permute-start | bytes 245768 | tf_op jit(solution)/shard_map/ppermute | solution.py:464
  38.2 8.1 %all-to-all-start = ((s32[128,1,4]{2,1,0:T(1,128)}), s32[128,1,4]{2,1,0:T(1,128)S(1)}, u32[]{:S(2)}, u32[]{:S(2)}) async-start(s32[128,1,4]{2,1,0:T(1,128)} %bitcast.2), calls=%async_computation | async-start | bytes 131072 | tf_op jit(solution)/shard_map/all_to_all | solution.py:522
  48.3 6.4 %all-to-all-done = s32[128,1,4]{2,1,0:T(1,128)S(1)} async-done(((s32[128,1,4]{2,1,0:T(1,128)}), s32[128,1,4]{2,1,0:T(1,128)S(1)}, u32[]{:S(2)}, u32[]{:S(2)}) %all-to-all-start) | async-done | bytes 2080 | tf_op jit(solution)/shard_map/all_to_all | solution.py:522
  56.5 5.7 %all-to-all-start.1 = ((bf16[128,16,128]{2,1,0:T(8,128)(2,1)}), bf16[128,16,128]{2,1,0:T(8,128)(2,1)S(1)}, u32[]{:S(2)}, u32[]{:S(2)}) async-start(bf16[128,16,128]{2,1,0:T(8,128)(2,1)} %bitcast.4), calls=%async_computation.1 | async-start | bytes 1048576 | tf_op jit(solution)/shard_map/all_to_all | solution.py:532
  62.3 2.3 %shard_map.194 = (bf16[640,512]{1,0:T(8,128)(2,1)S(1)}, f32[80,512]{1,0:T(8,128)S(1)}, bf16[512,512]{1,0:T(8,128)(2,1)S(1)}, bf16[512,512]{1,0:T(8,128)(2,1)S(1)}) custom-call(bf16[80,512]{1,0:T(8,128)(2,1)S(1)} %get-tuple-element.40.state_ref, s32[1,640]{1,0:T(1,128)S(1)} %broadcast_in_dim.6.tgt_ref, bf16[2,512,512]{2,1,0:T(8,128)(2,1)} %wr.3, ...), custom_call_target="tpu_custom_call" | custom-call | tf_op jit(solution)/shard_map/pallas_call | solution.py:81
  64.6 9.9 %all-to-all-done.1 = bf16[128,16,128]{2,1,0:T(8,128)(2,1)S(1)} async-done(((bf16[128,16,128]{2,1,0:T(8,128)(2,1)}), bf16[128,16,128]{2,1,0:T(8,128)(2,1)S(1)}, u32[]{:S(2)}, u32[]{:S(2)}) %all-to-all-start.1) | async-done | bytes 524320 | tf_op jit(solution)/shard_map/all_to_all | solution.py:532
  74.5 2.7 %shard_map.195 = (bf16[80,512]{1,0:T(8,128)(2,1)S(1)}, bf16[2048,128]{1,0:T(8,128)(2,1)}) custom-call(bf16[2048,128]{1,0:T(8,128)(2,1)S(1)} %bitcast.9, bf16[640,512]{1,0:T(8,128)(2,1)S(1)} %get-tuple-element.41.base_ref, f32[80,512]{1,0:T(8,128)S(1)} %get-tuple-element.42.self_ref, bf16[512,512]{1,0:T(8,128)(2,1)S(1)} %get-tuple-element.43.wom, ...), custom_call_target="tpu_custom_call" | custom-call | tf_op jit(solution)/shard_map/pallas_call | solution.py:81
  77.2 5.9 %all-to-all-start.2 = ((bf16[128,16,128]{2,1,0:T(8,128)(2,1)}), bf16[128,16,128]{2,1,0:T(8,128)(2,1)S(1)}, u32[]{:S(2)}, u32[]{:S(2)}) async-start(bf16[128,16,128]{2,1,0:T(8,128)(2,1)} %bitcast.6), calls=%async_computation.2 | async-start | bytes 1048576 | tf_op jit(solution)/shard_map/all_to_all | solution.py:532
  83.1 2.3 %shard_map.196 = (bf16[640,512]{1,0:T(8,128)(2,1)S(1)}, f32[80,512]{1,0:T(8,128)S(1)}, bf16[512,512]{1,0:T(8,128)(2,1)S(1)}, bf16[512,512]{1,0:T(8,128)(2,1)S(1)}) custom-call(bf16[80,512]{1,0:T(8,128)(2,1)S(1)} %get-tuple-element.46.state_ref, s32[1,640]{1,0:T(1,128)S(1)} %broadcast_in_dim.6.tgt_ref, bf16[2,512,512]{2,1,0:T(8,128)(2,1)} %wr.3, ...), custom_call_target="tpu_custom_call" | custom-call | tf_op jit(solution)/shard_map/pallas_call | solution.py:81
  85.4 10.0 %all-to-all-done.2 = bf16[128,16,128]{2,1,0:T(8,128)(2,1)S(1)} async-done(((bf16[128,16,128]{2,1,0:T(8,128)(2,1)}), bf16[128,16,128]{2,1,0:T(8,128)(2,1)S(1)}, u32[]{:S(2)}, u32[]{:S(2)}) %all-to-all-start.2) | async-done | bytes 524320 | tf_op jit(solution)/shard_map/all_to_all | solution.py:532
  97.6 3.9 %collective-permute-start.9 = (bf16[80,512]{1,0:T(8,128)(2,1)S(1)}, bf16[80,512]{1,0:T(8,128)(2,1)S(1)}, u32[]{:S(2)}, u32[]{:S(2)}) collective-permute-start(bf16[80,512]{1,0:T(8,128)(2,1)S(1)} %shard_map.197), channel_id=1, source_target_pairs={{1,2},{2,1},{3,4},{4,3},{5,6},{6,5},{7,8},{8,7},{9,10},{10,9},{11,... | collective-permute-start | bytes 245768 | tf_op jit(solution)/shard_map/ppermute | solution.py:464
  101.5 3.4 %collective-permute-done.9 = bf16[80,512]{1,0:T(8,128)(2,1)S(1)} collective-permute-done((bf16[80,512]{1,0:T(8,128)(2,1)S(1)}, bf16[80,512]{1,0:T(8,128)(2,1)S(1)}, u32[]{:S(2)}, u32[]{:S(2)}) %collective-permute-start.9) | collective-permute-done | bytes 81952 | tf_op jit(solution)/shard_map/ppermute | solution.py:464
  104.9 2.9 %collective-permute-start.11 = (bf16[240,512]{1,0:T(8,128)(2,1)S(1)}, bf16[240,512]{1,0:T(8,128)(2,1)S(1)}, u32[]{:S(2)}, u32[]{:S(2)}) collective-permute-start(bf16[240,512]{1,0:T(8,128)(2,1)S(1)} %pad_maximum_fusion.n0), channel_id=1, source_target_pairs={{0,16},{16,0},{32,48},{48,32},{64,80},{80,64},{96,112},{112,96},{1... | collective-permute-start | bytes 737288 | tf_op jit(solution)/shard_map/ppermute | solution.py:465
  107.8 2.2 %collective-permute-start.10 = (bf16[240,512]{1,0:T(8,128)(2,1)S(1)}, bf16[240,512]{1,0:T(8,128)(2,1)S(1)}, u32[]{:S(2)}, u32[]{:S(2)}) collective-permute-start(bf16[240,512]{1,0:T(8,128)(2,1)S(1)} %pad_maximum_fusion.n0), channel_id=1, source_target_pairs={{16,32},{32,16},{48,64},{64,48},{80,96},{96,80},{17,33},{33,17},{4... | collective-permute-start | bytes 737288 | tf_op jit(solution)/shard_map/ppermute | solution.py:464
  110.0 3.8 %receiver.1.r_ref = bf16[2048,512]{1,0:T(8,128)(2,1)} custom-call(bf16[2048,512]{1,0:T(8,128)(2,1)} %grid_ref.5, bf16[512,512]{1,0:T(8,128)(2,1)} %w_ref.1), custom_call_target="tpu_custom_call" | custom-call | tf_op jit(solution)/shard_map/receiver/pallas_call | solution.py:105
  113.8 5.6 %shard_map.198 = (f32[3,2048,512]{2,1,0:T(8,128)S(1)}, s32[3,2048]{1,0:T(4,128)S(1)}, bf16[512,512]{1,0:T(8,128)(2,1)S(1)}, bf16[2048,512]{1,0:T(8,128)(2,1)S(1)}) custom-call(s32[2]{0:T(128)S(1)} %pad_add_fusion.odd_ref, bf16[240,512]{1,0:T(8,128)(2,1)S(1)} %pad_maximum_fusion.n0, bf16[240,512]{1,0:T(8,128)(2,1)S(1)} %collective-permute-done.11.n1, ...), custom_call_target="tpu_custom_call" | custom-call | tf_op jit(solution)/shard_map/pallas_call | solution.py:81
  119.4 5.9 %decode_far.1 = bf16[2048,512]{1,0:T(8,128)(2,1)} custom-call(s32[2]{0:T(128)S(1)} %pad_add_fusion.odd_ref, bf16[240,512]{1,0:T(8,128)(2,1)S(1)} %collective-permute-done.10.n2, f32[3,2048,512]{2,1,0:T(8,128)S(1)} %get-tuple-element.51.v, s32[3,2048]{1,0:T(4,128)S(1)} %get-tuple-element.52.slots, bf16[512,512]{1,0:T(8,128)(2,1)S(1)} %get-tuple-element.53.w, ...), custom_call_target="tpu_custom_call" | custom-call | tf_op jit(solution)/shard_map/decode_far/pallas_call | solution.py:441
  (35 shorter events, 11.7 us)
Async XLA Ops:
  0.0 6.7 %collective-permute-start = (bf16[80,512]{1,0:T(8,128)(2,1)}, bf16[80,512]{1,0:T(8,128)(2,1)S(1)}, u32[]{:S(2)}, u32[]{:S(2)}) collective-permute-start(bf16[80,512]{1,0:T(8,128)(2,1)} %mesh_ref.1), channel_id=1, source_target_pairs={{0,1},{1,0},{2,3},{3,2},{4,5},{5,4},{6,7},{7,6},{8,9},{9,8},{10,11... | collective-permute-start | bytes 245768 | tf_op jit(solution)/shard_map/ppermute | solution.py:465
  1.6 7.5 %collective-permute-start.1 = (bf16[80,512]{1,0:T(8,128)(2,1)}, bf16[80,512]{1,0:T(8,128)(2,1)S(1)}, u32[]{:S(2)}, u32[]{:S(2)}) collective-permute-start(bf16[80,512]{1,0:T(8,128)(2,1)} %mesh_ref.1), channel_id=1, source_target_pairs={{1,2},{2,1},{3,4},{4,3},{5,6},{6,5},{7,8},{8,7},{9,10},{10,9},{11,... | collective-permute-start | bytes 245768 | tf_op jit(solution)/shard_map/ppermute | solution.py:464
  9.1 5.3 %collective-permute-start.3 = (bf16[240,512]{1,0:T(8,128)(2,1)S(1)}, bf16[240,512]{1,0:T(8,128)(2,1)S(1)}, u32[]{:S(2)}, u32[]{:S(2)}) collective-permute-start(bf16[240,512]{1,0:T(8,128)(2,1)S(1)} %constant_dynamic-update-slice_fusion.n0), channel_id=1, source_target_pairs={{0,16},{16,0},{32,48},{48,32},{64,80},{80,64},{96,112},{112,96},{1... | collective-permute-start | bytes 737288 | tf_op jit(solution)/shard_map/ppermute | solution.py:465
  11.2 9.0 %collective-permute-start.2 = (bf16[240,512]{1,0:T(8,128)(2,1)S(1)}, bf16[240,512]{1,0:T(8,128)(2,1)S(1)}, u32[]{:S(2)}, u32[]{:S(2)}) collective-permute-start(bf16[240,512]{1,0:T(8,128)(2,1)S(1)} %constant_dynamic-update-slice_fusion.n0), channel_id=1, source_target_pairs={{16,32},{32,16},{48,64},{64,48},{80,96},{96,80},{17,33},{33,17},{4... | collective-permute-start | bytes 737288 | tf_op jit(solution)/shard_map/ppermute | solution.py:464
  20.2 9.1 %copy-start.3 = (s32[1,128,4]{1,2,0:T(4,128)S(1)}, s32[1,128,4]{1,2,0:T(4,128)}, u32[]{:S(2)}) copy-start(s32[1,128,4]{1,2,0:T(4,128)} %param.24) | copy-start | bytes 6148
  20.2 26.2 %copy-start = (bf16[80,512]{1,0:T(8,128)(2,1)S(1)}, bf16[80,512]{1,0:T(8,128)(2,1)}, u32[]{:S(2)}) copy-start(bf16[80,512]{1,0:T(8,128)(2,1)} %mesh_ref.1) | copy-start | bytes 245764
  25.7 3.8 %collective-permute-start.4 = (bf16[240,512]{1,0:T(8,128)(2,1)S(1)}, bf16[240,512]{1,0:T(8,128)(2,1)S(1)}, u32[]{:S(2)}, u32[]{:S(2)}) collective-permute-start(bf16[240,512]{1,0:T(8,128)(2,1)S(1)} %get-tuple-element.34), channel_id=1, source_target_pairs={{0,16},{16,0},{32,48},{48,32},{64,80},{80,64},{96,112},{112,96},{1... | collective-permute-start | bytes 737288 | tf_op jit(solution)/shard_map/ppermute | solution.py:465
  25.8 7.5 %collective-permute-start.5 = (bf16[240,512]{1,0:T(8,128)(2,1)S(1)}, bf16[240,512]{1,0:T(8,128)(2,1)S(1)}, u32[]{:S(2)}, u32[]{:S(2)}) collective-permute-start(bf16[240,512]{1,0:T(8,128)(2,1)S(1)} %get-tuple-element.35), channel_id=1, source_target_pairs={{16,32},{32,16},{48,64},{64,48},{80,96},{96,80},{17,33},{33,17},{4... | collective-permute-start | bytes 737288 | tf_op jit(solution)/shard_map/ppermute | solution.py:464
  33.4 21.3 %collective-permute-start.6 = (bf16[80,512]{1,0:T(8,128)(2,1)S(1)}, bf16[80,512]{1,0:T(8,128)(2,1)S(1)}, u32[]{:S(2)}, u32[]{:S(2)}) collective-permute-start(bf16[80,512]{1,0:T(8,128)(2,1)S(1)} %get-tuple-element.56), channel_id=1, source_target_pairs={{0,1},{1,0},{2,3},{3,2},{4,5},{5,4},{6,7},{7,6},{8,9},{9,8},{10,11... | collective-permute-start | bytes 245768 | tf_op jit(solution)/shard_map/ppermute | solution.py:465
  33.5 21.2 %collective-permute-start.7 = (bf16[80,512]{1,0:T(8,128)(2,1)S(1)}, bf16[80,512]{1,0:T(8,128)(2,1)S(1)}, u32[]{:S(2)}, u32[]{:S(2)}) collective-permute-start(bf16[80,512]{1,0:T(8,128)(2,1)S(1)} %get-tuple-element.55), channel_id=1, source_target_pairs={{1,2},{2,1},{3,4},{4,3},{5,6},{6,5},{7,8},{8,7},{9,10},{10,9},{11,... | collective-permute-start | bytes 245768 | tf_op jit(solution)/shard_map/ppermute | solution.py:464
  38.2 16.4 %all-to-all-start = ((s32[128,1,4]{2,1,0:T(1,128)}), s32[128,1,4]{2,1,0:T(1,128)S(1)}, u32[]{:S(2)}, u32[]{:S(2)}) async-start(s32[128,1,4]{2,1,0:T(1,128)} %bitcast.2), calls=%async_computation | async-start | bytes 131072 | tf_op jit(solution)/shard_map/all_to_all | solution.py:522
  46.4 15.9 %copy-start.1 = (s32[640]{0:T(1024)S(1)}, s32[640]{0:T(1024)}, u32[]{:S(2)}) copy-start(s32[640]{0:T(1024)} %param.26) | copy-start | bytes 7684
  46.4 15.9 %copy-start.2 = (s32[640]{0:T(1024)S(1)}, s32[640]{0:T(1024)}, u32[]{:S(2)}) copy-start(s32[640]{0:T(1024)} %param.25) | copy-start | bytes 7684
  56.5 18.0 %all-to-all-start.1 = ((bf16[128,16,128]{2,1,0:T(8,128)(2,1)}), bf16[128,16,128]{2,1,0:T(8,128)(2,1)S(1)}, u32[]{:S(2)}, u32[]{:S(2)}) async-start(bf16[128,16,128]{2,1,0:T(8,128)(2,1)} %bitcast.4), calls=%async_computation.1 | async-start | bytes 1048576 | tf_op jit(solution)/shard_map/all_to_all | solution.py:532
  77.2 18.2 %all-to-all-start.2 = ((bf16[128,16,128]{2,1,0:T(8,128)(2,1)}), bf16[128,16,128]{2,1,0:T(8,128)(2,1)S(1)}, u32[]{:S(2)}, u32[]{:S(2)}) async-start(bf16[128,16,128]{2,1,0:T(8,128)(2,1)} %bitcast.6), calls=%async_computation.2 | async-start | bytes 1048576 | tf_op jit(solution)/shard_map/all_to_all | solution.py:532
  96.9 4.6 %collective-permute-start.8 = (bf16[80,512]{1,0:T(8,128)(2,1)S(1)}, bf16[80,512]{1,0:T(8,128)(2,1)S(1)}, u32[]{:S(2)}, u32[]{:S(2)}) collective-permute-start(bf16[80,512]{1,0:T(8,128)(2,1)S(1)} %shard_map.197), channel_id=1, source_target_pairs={{0,1},{1,0},{2,3},{3,2},{4,5},{5,4},{6,7},{7,6},{8,9},{9,8},{10,11... | collective-permute-start | bytes 245768 | tf_op jit(solution)/shard_map/ppermute | solution.py:465
  97.6 7.3 %collective-permute-start.9 = (bf16[80,512]{1,0:T(8,128)(2,1)S(1)}, bf16[80,512]{1,0:T(8,128)(2,1)S(1)}, u32[]{:S(2)}, u32[]{:S(2)}) collective-permute-start(bf16[80,512]{1,0:T(8,128)(2,1)S(1)} %shard_map.197), channel_id=1, source_target_pairs={{1,2},{2,1},{3,4},{4,3},{5,6},{6,5},{7,8},{8,7},{9,10},{10,9},{11,... | collective-permute-start | bytes 245768 | tf_op jit(solution)/shard_map/ppermute | solution.py:464
  104.9 8.8 %collective-permute-start.11 = (bf16[240,512]{1,0:T(8,128)(2,1)S(1)}, bf16[240,512]{1,0:T(8,128)(2,1)S(1)}, u32[]{:S(2)}, u32[]{:S(2)}) collective-permute-start(bf16[240,512]{1,0:T(8,128)(2,1)S(1)} %pad_maximum_fusion.n0), channel_id=1, source_target_pairs={{0,16},{16,0},{32,48},{48,32},{64,80},{80,64},{96,112},{112,96},{1... | collective-permute-start | bytes 737288 | tf_op jit(solution)/shard_map/ppermute | solution.py:465
  107.8 11.5 %collective-permute-start.10 = (bf16[240,512]{1,0:T(8,128)(2,1)S(1)}, bf16[240,512]{1,0:T(8,128)(2,1)S(1)}, u32[]{:S(2)}, u32[]{:S(2)}) collective-permute-start(bf16[240,512]{1,0:T(8,128)(2,1)S(1)} %pad_maximum_fusion.n0), channel_id=1, source_target_pairs={{16,32},{32,16},{48,64},{64,48},{80,96},{96,80},{17,33},{33,17},{4... | collective-permute-start | bytes 737288 | tf_op jit(solution)/shard_map/ppermute | solution.py:464

commit v8 on v7

--- a/solution.py
+++ b/solution.py
@@ -14,7 +14,7 @@
 SIDE = 3
 ENC_ROWS = 1024
 DEC_ROWS = 1024
-FAR_ROWS = 1024
+OUT_ROWS = 512
 FAR_PART = 1024
 PRE_ROWS = 1024
 
@@ -386,19 +386,15 @@
         copy.wait()
 
 
-def dec_far_kernel(odd_ref, n2, v, slots, w, g, out_ref, near):
+def dec_far_kernel(odd_ref, n2, v, slots, w, g, out_ref, near, out, sems):
     line = n2.shape[0]
     rows = out_ref.shape[0]
-    step = pl.program_id(0)
-
-    @pl.when(step == 0)
-    def _():
-        near[...] = jnp.zeros_like(near)
-        line_rows(n2[...], near, 0, odd_ref)
-
+    near[...] = jnp.zeros_like(near)
+    line_rows(n2[...], near, 0, odd_ref)
+    backs = []
     start = line_start(2, odd_ref, line)
     for at in range(0, rows, FAR_PART):
-        part = pl.ds(pl.multiple_of(step * rows + at, FAR_PART), FAR_PART)
+        part = pl.ds(at, FAR_PART)
         total = None
         chosen = jnp.concatenate(
             [hot_rows(slots[f : f + 1, part] - start, near.shape[0]) for f in range(DEC_FAN)], axis=0
@@ -408,7 +404,13 @@
             h = silu_of_half(most[f * FAR_PART : (f + 1) * FAR_PART] + v[f, part, :])
             total = h if total is None else total + h
         update = dot(total, w[...])
-        out_ref[at : at + FAR_PART] = bf(g[part, :].astype(jnp.float32) + norm(update))
+        for k in range(0, FAR_PART, OUT_ROWS):
+            to = slice(at + k, at + k + OUT_ROWS)
+            out[to] = bf(g[to].astype(jnp.float32) + norm(update[k : k + OUT_ROWS]))
+            backs.append(pltpu.make_async_copy(out.at[to], out_ref.at[to], sems.at[len(backs)]))
+            backs[-1].start()
+    for back in backs:
+        back.wait()
 
 
 def decode_near(odd, r, grid_latent, slot_rows, near, wo):
@@ -440,11 +442,14 @@
     args = near_to(pltpu.VMEM, [near, v, slots, w, g])
     return pl.pallas_call(
         dec_far_kernel,
-        grid=(n // FAR_ROWS,),
         in_specs=[pl.BlockSpec(memory_space=pltpu.SMEM)] + [VMEM] * len(args),
-        out_specs=pl.BlockSpec((FAR_ROWS, d), lambda i: (i, 0)),
-        out_shape=jax.ShapeDtypeStruct((n, d), jnp.bfloat16),
-        scratch_shapes=[pltpu.VMEM((up256(near.shape[0]), d), jnp.bfloat16)],
+        out_specs=HBM,
+        out_shape=pltpu.HBM((n, d), jnp.bfloat16),
+        scratch_shapes=[
+            pltpu.VMEM((up256(near.shape[0]), d), jnp.bfloat16),
+            pltpu.VMEM((n, d), jnp.bfloat16),
+            pltpu.SemaphoreType.DMA((n // OUT_ROWS,)),
+        ],
         compiler_params=pltpu.CompilerParams(vmem_limit_bytes=20 << 20),
         name="decode_far",
     )(odd, *args)

time: 126 us -> 126 us (level)
  no operation moved by 1% of the time
where the time goes in v8:
time: 126 us; the launch traced here: 125 us
  starting transfers between devices  48.3 us (38%)
  Pallas kernels  38.6 us (31%)
  waiting for transfers between devices  36 us (29%)
    pallas_call x9, Pallas kernels, on_chip(): pl.pallas_call(kernel, in_specs=specs, out_specs=[VMEM] * len(outs), out_...  29.2 us
    ppermute x6, starting transfers between devices, swap_both(): b = lax.ppermute(to_second, axis, second)  21 us
    all_to_all x2, waiting for transfers between devices, body(): lax.all_to_all(outgoing.reshape(tiles, -1, 128), ('lat', 'lon'), split_ax...  19.9 us
    all_to_all x2, starting transfers between devices, body(): lax.all_to_all(outgoing.reshape(tiles, -1, 128), ('lat', 'lon'), split_ax...  11.7 us
    ppermute x6, waiting for transfers between devices, swap_both(): b = lax.ppermute(to_second, axis, second)  9.63 us
    all_to_all x1, starting transfers between devices, body(): lax.all_to_all(wanted, ('lat', 'lon'), split_axis=0, concat_axis=0, tiled...  8.14 us
    ppermute x6, starting transfers between devices, swap_both(): a = lax.ppermute(to_first, axis, first)  7.53 us
    all_to_all x1, waiting for transfers between devices, body(): lax.all_to_all(wanted, ('lat', 'lon'), split_axis=0, concat_axis=0, tiled...  6.39 us
  transfers between devices with their start and end apart: 15, of which 6 were waited for; matrix products, arithmetic and copies ran while one was open for 1% of the time, Pallas kernels for 17%

profile of v8, /device:TPU:3, one launch (start us, length us, event | category | flops | bytes accessed | tf_op | source)
XLA Modules:
  0.0 125.1 jit_solution(5871251542739489219)
XLA Ops:
  1.6 4.1 %collective-permute-start.1 = (bf16[80,512]{1,0:T(8,128)(2,1)}, bf16[80,512]{1,0:T(8,128)(2,1)S(1)}, u32[]{:S(2)}, u32[]{:S(2)}) collective-permute-start(bf16[80,512]{1,0:T(8,128)(2,1)} %mesh_ref.1), channel_id=1, source_target_pairs={{1,2},{2,1},{3,4},{4,3},{5,6},{6,5},{7,8},{8,7},{9,10},{10,9},{11,... | collective-permute-start | bytes 245768 | tf_op jit(solution)/shard_map/ppermute | solution.py:469
  6.7 2.4 %collective-permute-done.1 = bf16[80,512]{1,0:T(8,128)(2,1)S(1)} collective-permute-done((bf16[80,512]{1,0:T(8,128)(2,1)}, bf16[80,512]{1,0:T(8,128)(2,1)S(1)}, u32[]{:S(2)}, u32[]{:S(2)}) %collective-permute-start.1) | collective-permute-done | bytes 81952 | tf_op jit(solution)/shard_map/ppermute | solution.py:469
  11.2 3.1 %collective-permute-start.2 = (bf16[240,512]{1,0:T(8,128)(2,1)S(1)}, bf16[240,512]{1,0:T(8,128)(2,1)S(1)}, u32[]{:S(2)}, u32[]{:S(2)}) collective-permute-start(bf16[240,512]{1,0:T(8,128)(2,1)S(1)} %constant_dynamic-update-slice_fusion.n0), channel_id=1, source_target_pairs={{16,32},{32,16},{48,64},{64,48},{80,96},{96,80},{17,33},{33,17},{4... | collective-permute-start | bytes 737288 | tf_op jit(solution)/shard_map/ppermute | solution.py:469
  14.4 5.7 %shard_map.190 = (f32[2,2048,512]{2,1,0:T(8,128)S(1)}, s32[2,2048]{1,0:T(2,128)S(1)}, bf16[512,512]{1,0:T(8,128)(2,1)S(1)}) custom-call(s32[2]{0:T(128)S(1)} %pad_add_fusion.odd_ref, bf16[240,512]{1,0:T(8,128)(2,1)S(1)} %constant_dynamic-update-slice_fusion.n0, bf16[240,512]{1,0:T(8,128)(2,1)S(1)} %collective-permute-done.3.n1, s32[2,2048]{1,0:T(2,128)} %slots_ref.2, ...), custom_call_target="tpu_custom_call" | custom-call | tf_op jit(solution)/shard_map/pallas_call | solution.py:81
  20.2 5.4 %shard_map.191 = (bf16[240,512]{1,0:T(8,128)(2,1)S(1)}, bf16[240,512]{1,0:T(8,128)(2,1)S(1)}, bf16[240,512]{1,0:T(8,128)(2,1)S(1)}) custom-call(s32[2]{0:T(128)S(1)} %pad_add_fusion.odd_ref, bf16[240,512]{1,0:T(8,128)(2,1)S(1)} %collective-permute-done.2.n2, f32[2,2048,512]{2,1,0:T(8,128)S(1)} %get-tuple-element.30.v_ref, ...), custom_call_target="tpu_custom_call" | custom-call | tf_op jit(solution)/shard_map/pallas_call | solution.py:81
  25.8 3.6 %collective-permute-start.5 = (bf16[240,512]{1,0:T(8,128)(2,1)S(1)}, bf16[240,512]{1,0:T(8,128)(2,1)S(1)}, u32[]{:S(2)}, u32[]{:S(2)}) collective-permute-start(bf16[240,512]{1,0:T(8,128)(2,1)S(1)} %get-tuple-element.35), channel_id=1, source_target_pairs={{16,32},{32,16},{48,64},{64,48},{80,96},{96,80},{17,33},{33,17},{4... | collective-permute-start | bytes 737288 | tf_op jit(solution)/shard_map/ppermute | solution.py:469
  29.5 3.8 %collective-permute-done.5 = bf16[240,512]{1,0:T(8,128)(2,1)S(1)} collective-permute-done((bf16[240,512]{1,0:T(8,128)(2,1)S(1)}, bf16[240,512]{1,0:T(8,128)(2,1)S(1)}, u32[]{:S(2)}, u32[]{:S(2)}) %collective-permute-start.5) | collective-permute-done | bytes 245792 | tf_op jit(solution)/shard_map/ppermute | solution.py:469
  33.5 4.1 %collective-permute-start.7 = (bf16[80,512]{1,0:T(8,128)(2,1)S(1)}, bf16[80,512]{1,0:T(8,128)(2,1)S(1)}, u32[]{:S(2)}, u32[]{:S(2)}) collective-permute-start(bf16[80,512]{1,0:T(8,128)(2,1)S(1)} %get-tuple-element.55), channel_id=1, source_target_pairs={{1,2},{2,1},{3,4},{4,3},{5,6},{6,5},{7,8},{8,7},{9,10},{10,9},{11,... | collective-permute-start | bytes 245768 | tf_op jit(solution)/shard_map/ppermute | solution.py:469
  38.2 8.1 %all-to-all-start = ((s32[128,1,4]{2,1,0:T(1,128)}), s32[128,1,4]{2,1,0:T(1,128)S(1)}, u32[]{:S(2)}, u32[]{:S(2)}) async-start(s32[128,1,4]{2,1,0:T(1,128)} %bitcast.2), calls=%async_computation | async-start | bytes 131072 | tf_op jit(solution)/shard_map/all_to_all | solution.py:527
  48.3 6.4 %all-to-all-done = s32[128,1,4]{2,1,0:T(1,128)S(1)} async-done(((s32[128,1,4]{2,1,0:T(1,128)}), s32[128,1,4]{2,1,0:T(1,128)S(1)}, u32[]{:S(2)}, u32[]{:S(2)}) %all-to-all-start) | async-done | bytes 2080 | tf_op jit(solution)/shard_map/all_to_all | solution.py:527
  56.5 5.7 %all-to-all-start.1 = ((bf16[128,16,128]{2,1,0:T(8,128)(2,1)}), bf16[128,16,128]{2,1,0:T(8,128)(2,1)S(1)}, u32[]{:S(2)}, u32[]{:S(2)}) async-start(bf16[128,16,128]{2,1,0:T(8,128)(2,1)} %bitcast.4), calls=%async_computation.1 | async-start | bytes 1048576 | tf_op jit(solution)/shard_map/all_to_all | solution.py:537
  62.3 2.3 %shard_map.194 = (bf16[640,512]{1,0:T(8,128)(2,1)S(1)}, f32[80,512]{1,0:T(8,128)S(1)}, bf16[512,512]{1,0:T(8,128)(2,1)S(1)}, bf16[512,512]{1,0:T(8,128)(2,1)S(1)}) custom-call(bf16[80,512]{1,0:T(8,128)(2,1)S(1)} %get-tuple-element.40.state_ref, s32[1,640]{1,0:T(1,128)S(1)} %broadcast_in_dim.6.tgt_ref, bf16[2,512,512]{2,1,0:T(8,128)(2,1)} %wr.3, ...), custom_call_target="tpu_custom_call" | custom-call | tf_op jit(solution)/shard_map/pallas_call | solution.py:81
  64.6 9.9 %all-to-all-done.1 = bf16[128,16,128]{2,1,0:T(8,128)(2,1)S(1)} async-done(((bf16[128,16,128]{2,1,0:T(8,128)(2,1)}), bf16[128,16,128]{2,1,0:T(8,128)(2,1)S(1)}, u32[]{:S(2)}, u32[]{:S(2)}) %all-to-all-start.1) | async-done | bytes 524320 | tf_op jit(solution)/shard_map/all_to_all | solution.py:537
  74.5 2.7 %shard_map.195 = (bf16[80,512]{1,0:T(8,128)(2,1)S(1)}, bf16[2048,128]{1,0:T(8,128)(2,1)}) custom-call(bf16[2048,128]{1,0:T(8,128)(2,1)S(1)} %bitcast.9, bf16[640,512]{1,0:T(8,128)(2,1)S(1)} %get-tuple-element.41.base_ref, f32[80,512]{1,0:T(8,128)S(1)} %get-tuple-element.42.self_ref, bf16[512,512]{1,0:T(8,128)(2,1)S(1)} %get-tuple-element.43.wom, ...), custom_call_target="tpu_custom_call" | custom-call | tf_op jit(solution)/shard_map/pallas_call | solution.py:81
  77.2 5.9 %all-to-all-start.2 = ((bf16[128,16,128]{2,1,0:T(8,128)(2,1)}), bf16[128,16,128]{2,1,0:T(8,128)(2,1)S(1)}, u32[]{:S(2)}, u32[]{:S(2)}) async-start(bf16[128,16,128]{2,1,0:T(8,128)(2,1)} %bitcast.6), calls=%async_computation.2 | async-start | bytes 1048576 | tf_op jit(solution)/shard_map/all_to_all | solution.py:537
  83.1 2.3 %shard_map.196 = (bf16[640,512]{1,0:T(8,128)(2,1)S(1)}, f32[80,512]{1,0:T(8,128)S(1)}, bf16[512,512]{1,0:T(8,128)(2,1)S(1)}, bf16[512,512]{1,0:T(8,128)(2,1)S(1)}) custom-call(bf16[80,512]{1,0:T(8,128)(2,1)S(1)} %get-tuple-element.46.state_ref, s32[1,640]{1,0:T(1,128)S(1)} %broadcast_in_dim.6.tgt_ref, bf16[2,512,512]{2,1,0:T(8,128)(2,1)} %wr.3, ...), custom_call_target="tpu_custom_call" | custom-call | tf_op jit(solution)/shard_map/pallas_call | solution.py:81
  85.4 10.0 %all-to-all-done.2 = bf16[128,16,128]{2,1,0:T(8,128)(2,1)S(1)} async-done(((bf16[128,16,128]{2,1,0:T(8,128)(2,1)}), bf16[128,16,128]{2,1,0:T(8,128)(2,1)S(1)}, u32[]{:S(2)}, u32[]{:S(2)}) %all-to-all-start.2) | async-done | bytes 524320 | tf_op jit(solution)/shard_map/all_to_all | solution.py:537
  97.6 3.9 %collective-permute-start.9 = (bf16[80,512]{1,0:T(8,128)(2,1)S(1)}, bf16[80,512]{1,0:T(8,128)(2,1)S(1)}, u32[]{:S(2)}, u32[]{:S(2)}) collective-permute-start(bf16[80,512]{1,0:T(8,128)(2,1)S(1)} %shard_map.197), channel_id=1, source_target_pairs={{1,2},{2,1},{3,4},{4,3},{5,6},{6,5},{7,8},{8,7},{9,10},{10,9},{11,... | collective-permute-start | bytes 245768 | tf_op jit(solution)/shard_map/ppermute | solution.py:469
  101.5 3.4 %collective-permute-done.9 = bf16[80,512]{1,0:T(8,128)(2,1)S(1)} collective-permute-done((bf16[80,512]{1,0:T(8,128)(2,1)S(1)}, bf16[80,512]{1,0:T(8,128)(2,1)S(1)}, u32[]{:S(2)}, u32[]{:S(2)}) %collective-permute-start.9) | collective-permute-done | bytes 81952 | tf_op jit(solution)/shard_map/ppermute | solution.py:469
  104.9 2.9 %collective-permute-start.11 = (bf16[240,512]{1,0:T(8,128)(2,1)S(1)}, bf16[240,512]{1,0:T(8,128)(2,1)S(1)}, u32[]{:S(2)}, u32[]{:S(2)}) collective-permute-start(bf16[240,512]{1,0:T(8,128)(2,1)S(1)} %pad_maximum_fusion.n0), channel_id=1, source_target_pairs={{0,16},{16,0},{32,48},{48,32},{64,80},{80,64},{96,112},{112,96},{1... | collective-permute-start | bytes 737288 | tf_op jit(solution)/shard_map/ppermute | solution.py:470
  107.8 2.2 %collective-permute-start.10 = (bf16[240,512]{1,0:T(8,128)(2,1)S(1)}, bf16[240,512]{1,0:T(8,128)(2,1)S(1)}, u32[]{:S(2)}, u32[]{:S(2)}) collective-permute-start(bf16[240,512]{1,0:T(8,128)(2,1)S(1)} %pad_maximum_fusion.n0), channel_id=1, source_target_pairs={{16,32},{32,16},{48,64},{64,48},{80,96},{96,80},{17,33},{33,17},{4... | collective-permute-start | bytes 737288 | tf_op jit(solution)/shard_map/ppermute | solution.py:469
  110.0 3.8 %receiver.1.r_ref = bf16[2048,512]{1,0:T(8,128)(2,1)} custom-call(bf16[2048,512]{1,0:T(8,128)(2,1)} %grid_ref.5, bf16[512,512]{1,0:T(8,128)(2,1)} %w_ref.1), custom_call_target="tpu_custom_call" | custom-call | tf_op jit(solution)/shard_map/receiver/pallas_call | solution.py:105
  113.8 5.6 %shard_map.198 = (f32[3,2048,512]{2,1,0:T(8,128)S(1)}, s32[3,2048]{1,0:T(4,128)S(1)}, bf16[512,512]{1,0:T(8,128)(2,1)S(1)}, bf16[2048,512]{1,0:T(8,128)(2,1)S(1)}) custom-call(s32[2]{0:T(128)S(1)} %pad_add_fusion.odd_ref, bf16[240,512]{1,0:T(8,128)(2,1)S(1)} %pad_maximum_fusion.n0, bf16[240,512]{1,0:T(8,128)(2,1)S(1)} %collective-permute-done.11.n1, ...), custom_call_target="tpu_custom_call" | custom-call | tf_op jit(solution)/shard_map/pallas_call | solution.py:81
  119.4 5.6 %decode_far.1 = bf16[2048,512]{1,0:T(8,128)(2,1)} custom-call(s32[2]{0:T(128)S(1)} %pad_add_fusion.odd_ref, bf16[240,512]{1,0:T(8,128)(2,1)S(1)} %collective-permute-done.10.n2, f32[3,2048,512]{2,1,0:T(8,128)S(1)} %get-tuple-element.51.v, s32[3,2048]{1,0:T(4,128)S(1)} %get-tuple-element.52.slots, bf16[512,512]{1,0:T(8,128)(2,1)S(1)} %get-tuple-element.53.w, ...), custom_call_target="tpu_custom_call" | custom-call | tf_op jit(solution)/shard_map/decode_far/pallas_call | solution.py:443
  (35 shorter events, 11.7 us)
Async XLA Ops:
  0.0 6.7 %collective-permute-start = (bf16[80,512]{1,0:T(8,128)(2,1)}, bf16[80,512]{1,0:T(8,128)(2,1)S(1)}, u32[]{:S(2)}, u32[]{:S(2)}) collective-permute-start(bf16[80,512]{1,0:T(8,128)(2,1)} %mesh_ref.1), channel_id=1, source_target_pairs={{0,1},{1,0},{2,3},{3,2},{4,5},{5,4},{6,7},{7,6},{8,9},{9,8},{10,11... | collective-permute-start | bytes 245768 | tf_op jit(solution)/shard_map/ppermute | solution.py:470
  1.6 7.5 %collective-permute-start.1 = (bf16[80,512]{1,0:T(8,128)(2,1)}, bf16[80,512]{1,0:T(8,128)(2,1)S(1)}, u32[]{:S(2)}, u32[]{:S(2)}) collective-permute-start(bf16[80,512]{1,0:T(8,128)(2,1)} %mesh_ref.1), channel_id=1, source_target_pairs={{1,2},{2,1},{3,4},{4,3},{5,6},{6,5},{7,8},{8,7},{9,10},{10,9},{11,... | collective-permute-start | bytes 245768 | tf_op jit(solution)/shard_map/ppermute | solution.py:469
  9.1 5.3 %collective-permute-start.3 = (bf16[240,512]{1,0:T(8,128)(2,1)S(1)}, bf16[240,512]{1,0:T(8,128)(2,1)S(1)}, u32[]{:S(2)}, u32[]{:S(2)}) collective-permute-start(bf16[240,512]{1,0:T(8,128)(2,1)S(1)} %constant_dynamic-update-slice_fusion.n0), channel_id=1, source_target_pairs={{0,16},{16,0},{32,48},{48,32},{64,80},{80,64},{96,112},{112,96},{1... | collective-permute-start | bytes 737288 | tf_op jit(solution)/shard_map/ppermute | solution.py:470
  11.2 9.0 %collective-permute-start.2 = (bf16[240,512]{1,0:T(8,128)(2,1)S(1)}, bf16[240,512]{1,0:T(8,128)(2,1)S(1)}, u32[]{:S(2)}, u32[]{:S(2)}) collective-permute-start(bf16[240,512]{1,0:T(8,128)(2,1)S(1)} %constant_dynamic-update-slice_fusion.n0), channel_id=1, source_target_pairs={{16,32},{32,16},{48,64},{64,48},{80,96},{96,80},{17,33},{33,17},{4... | collective-permute-start | bytes 737288 | tf_op jit(solution)/shard_map/ppermute | solution.py:469
  20.2 9.1 %copy-start.3 = (s32[1,128,4]{1,2,0:T(4,128)S(1)}, s32[1,128,4]{1,2,0:T(4,128)}, u32[]{:S(2)}) copy-start(s32[1,128,4]{1,2,0:T(4,128)} %param.24) | copy-start | bytes 6148
  20.2 26.2 %copy-start = (bf16[80,512]{1,0:T(8,128)(2,1)S(1)}, bf16[80,512]{1,0:T(8,128)(2,1)}, u32[]{:S(2)}) copy-start(bf16[80,512]{1,0:T(8,128)(2,1)} %mesh_ref.1) | copy-start | bytes 245764
  25.7 3.8 %collective-permute-start.4 = (bf16[240,512]{1,0:T(8,128)(2,1)S(1)}, bf16[240,512]{1,0:T(8,128)(2,1)S(1)}, u32[]{:S(2)}, u32[]{:S(2)}) collective-permute-start(bf16[240,512]{1,0:T(8,128)(2,1)S(1)} %get-tuple-element.34), channel_id=1, source_target_pairs={{0,16},{16,0},{32,48},{48,32},{64,80},{80,64},{96,112},{112,96},{1... | collective-permute-start | bytes 737288 | tf_op jit(solution)/shard_map/ppermute | solution.py:470
  25.8 7.5 %collective-permute-start.5 = (bf16[240,512]{1,0:T(8,128)(2,1)S(1)}, bf16[240,512]{1,0:T(8,128)(2,1)S(1)}, u32[]{:S(2)}, u32[]{:S(2)}) collective-permute-start(bf16[240,512]{1,0:T(8,128)(2,1)S(1)} %get-tuple-element.35), channel_id=1, source_target_pairs={{16,32},{32,16},{48,64},{64,48},{80,96},{96,80},{17,33},{33,17},{4... | collective-permute-start | bytes 737288 | tf_op jit(solution)/shard_map/ppermute | solution.py:469
  33.4 21.3 %collective-permute-start.6 = (bf16[80,512]{1,0:T(8,128)(2,1)S(1)}, bf16[80,512]{1,0:T(8,128)(2,1)S(1)}, u32[]{:S(2)}, u32[]{:S(2)}) collective-permute-start(bf16[80,512]{1,0:T(8,128)(2,1)S(1)} %get-tuple-element.56), channel_id=1, source_target_pairs={{0,1},{1,0},{2,3},{3,2},{4,5},{5,4},{6,7},{7,6},{8,9},{9,8},{10,11... | collective-permute-start | bytes 245768 | tf_op jit(solution)/shard_map/ppermute | solution.py:470
  33.5 21.2 %collective-permute-start.7 = (bf16[80,512]{1,0:T(8,128)(2,1)S(1)}, bf16[80,512]{1,0:T(8,128)(2,1)S(1)}, u32[]{:S(2)}, u32[]{:S(2)}) collective-permute-start(bf16[80,512]{1,0:T(8,128)(2,1)S(1)} %get-tuple-element.55), channel_id=1, source_target_pairs={{1,2},{2,1},{3,4},{4,3},{5,6},{6,5},{7,8},{8,7},{9,10},{10,9},{11,... | collective-permute-start | bytes 245768 | tf_op jit(solution)/shard_map/ppermute | solution.py:469
  38.2 16.4 %all-to-all-start = ((s32[128,1,4]{2,1,0:T(1,128)}), s32[128,1,4]{2,1,0:T(1,128)S(1)}, u32[]{:S(2)}, u32[]{:S(2)}) async-start(s32[128,1,4]{2,1,0:T(1,128)} %bitcast.2), calls=%async_computation | async-start | bytes 131072 | tf_op jit(solution)/shard_map/all_to_all | solution.py:527
  46.4 15.9 %copy-start.1 = (s32[640]{0:T(1024)S(1)}, s32[640]{0:T(1024)}, u32[]{:S(2)}) copy-start(s32[640]{0:T(1024)} %param.26) | copy-start | bytes 7684
  46.4 15.9 %copy-start.2 = (s32[640]{0:T(1024)S(1)}, s32[640]{0:T(1024)}, u32[]{:S(2)}) copy-start(s32[640]{0:T(1024)} %param.25) | copy-start | bytes 7684
  56.5 18.0 %all-to-all-start.1 = ((bf16[128,16,128]{2,1,0:T(8,128)(2,1)}), bf16[128,16,128]{2,1,0:T(8,128)(2,1)S(1)}, u32[]{:S(2)}, u32[]{:S(2)}) async-start(bf16[128,16,128]{2,1,0:T(8,128)(2,1)} %bitcast.4), calls=%async_computation.1 | async-start | bytes 1048576 | tf_op jit(solution)/shard_map/all_to_all | solution.py:537
  77.2 18.2 %all-to-all-start.2 = ((bf16[128,16,128]{2,1,0:T(8,128)(2,1)}), bf16[128,16,128]{2,1,0:T(8,128)(2,1)S(1)}, u32[]{:S(2)}, u32[]{:S(2)}) async-start(bf16[128,16,128]{2,1,0:T(8,128)(2,1)} %bitcast.6), calls=%async_computation.2 | async-start | bytes 1048576 | tf_op jit(solution)/shard_map/all_to_all | solution.py:537
  96.9 4.6 %collective-permute-start.8 = (bf16[80,512]{1,0:T(8,128)(2,1)S(1)}, bf16[80,512]{1,0:T(8,128)(2,1)S(1)}, u32[]{:S(2)}, u32[]{:S(2)}) collective-permute-start(bf16[80,512]{1,0:T(8,128)(2,1)S(1)} %shard_map.197), channel_id=1, source_target_pairs={{0,1},{1,0},{2,3},{3,2},{4,5},{5,4},{6,7},{7,6},{8,9},{9,8},{10,11... | collective-permute-start | bytes 245768 | tf_op jit(solution)/shard_map/ppermute | solution.py:470
  97.6 7.3 %collective-permute-start.9 = (bf16[80,512]{1,0:T(8,128)(2,1)S(1)}, bf16[80,512]{1,0:T(8,128)(2,1)S(1)}, u32[]{:S(2)}, u32[]{:S(2)}) collective-permute-start(bf16[80,512]{1,0:T(8,128)(2,1)S(1)} %shard_map.197), channel_id=1, source_target_pairs={{1,2},{2,1},{3,4},{4,3},{5,6},{6,5},{7,8},{8,7},{9,10},{10,9},{11,... | collective-permute-start | bytes 245768 | tf_op jit(solution)/shard_map/ppermute | solution.py:469
  104.9 8.8 %collective-permute-start.11 = (bf16[240,512]{1,0:T(8,128)(2,1)S(1)}, bf16[240,512]{1,0:T(8,128)(2,1)S(1)}, u32[]{:S(2)}, u32[]{:S(2)}) collective-permute-start(bf16[240,512]{1,0:T(8,128)(2,1)S(1)} %pad_maximum_fusion.n0), channel_id=1, source_target_pairs={{0,16},{16,0},{32,48},{48,32},{64,80},{80,64},{96,112},{112,96},{1... | collective-permute-start | bytes 737288 | tf_op jit(solution)/shard_map/ppermute | solution.py:470
  107.8 11.5 %collective-permute-start.10 = (bf16[240,512]{1,0:T(8,128)(2,1)S(1)}, bf16[240,512]{1,0:T(8,128)(2,1)S(1)}, u32[]{:S(2)}, u32[]{:S(2)}) collective-permute-start(bf16[240,512]{1,0:T(8,128)(2,1)S(1)} %pad_maximum_fusion.n0), channel_id=1, source_target_pairs={{16,32},{32,16},{48,64},{64,48},{80,96},{96,80},{17,33},{33,17},{4... | collective-permute-start | bytes 737288 | tf_op jit(solution)/shard_map/ppermute | solution.py:469
